TPU v7x, 128 devices: a whole 4x4x4 slice. The times are simulated.
128 devices in a mesh: surf: 32 (over z_lo, x, y), wall: 4 (over z_hi, core).
Axes of the slice: x: 4, y: 4, z: 4 (z_hi: 2, z_lo: 2; z = z_hi * 2 + z_lo), core: 2. Of those that a mesh axis runs over, the one named last changes fastest.
Arguments:
- flow_state: float32 [5, 128, 256, 512], P(None, 'wall', 'surf'), may hold values from -1 to 6, as said below
- spacing: float32 [128, 256, 512], P('wall', 'surf'), may hold values from 0.6 to 1.8
- bc_kind: int32 [256, 512], P('surf'), may hold values from 0 to 2
- cell_of: int32 [131072], P(('surf', 'wall')), may hold values from 0 to 131071, as said below
- zone_id: int32 [131072], P(('surf', 'wall')), may hold values from 0 to 7
- abl_temp: float32 [64, 131072], P(None, ('surf', 'wall')), may hold values from 0.5 to 2
- conduct: float32 [8], replicated, may hold values from 0.3 to 3
- diffuse: float32 [8], replicated, may hold values from 0.1 to 0.45
- rate: float32 [8], replicated, may hold values from 0.3 to 3
Outputs:
- state_next: float32 [5, 128, 256, 512], P(None, 'wall', 'surf')
- node_shift: float32 [128, 256, 512], P('wall', 'surf')
- ablator_next: float32 [64, 131072], P(None, ('surf', 'wall'))
Inputs may be any that keep to these rules, and one draw needn't show every extreme that they name: `cell_of`: each surface cell is named by exactly one column; the columns of one device name exactly 32 cells of every surface tile (tile = cell // 4096). `flow_state`: the density U0 is at least 0.45 and the pressure derived from U is at least 0.37 in every cell.
All inputs are finite; a program needn't handle non-finite values.
Results may differ from a plain program's by a relative error of at most 0.0003.
Values sent between devices are 32-bit elements; how exact they have to be, the bound alone decides.
No kernel may reach another device: no remote copies, remote signals or barrier semaphores. Data moves between devices by JAX's collectives and lax.ppermute only.
A program may use at most 128 MiB of HBM per device.

v0:
```python
import jax
import jax.numpy as jnp
from jax import lax
from jax.sharding import PartitionSpec as P

heat_ratio = 1.4
time_step = 0.15
viscosity = 0.05
conduction = 0.07
sponge_rate = 0.5
activation = 2.0
blow_ratio = 1.0
radiation = 0.8
film_conduct = 1.0
recovery = 0.2
far_values = (1.0, 0.5, 0.0, 0.0, 2.625)


def from_root(value, axis, source):
    kept = jnp.where(lax.axis_index(axis) == source, value, 0).astype(value.dtype)
    return lax.psum(kept, axis)


def prefix(value, axis, join, neutral):
    count, mine = (lax.axis_size(axis), lax.axis_index(axis))
    pieces = lax.all_gather(value, axis)
    running = jnp.full_like(value, 0) + jnp.asarray(neutral, value.dtype)

    def hop(position, running):
        longer = join(running, pieces[position])
        return jnp.where(position < mine, longer, running)

    return lax.fori_loop(0, count - 1, hop, running)


def padded_2(value, sides, width, wrap):
    for axis, dim in sides:
        size, length = (lax.axis_size(axis), value.shape[dim])
        up = [(i, (i + 1) % size) for i in range(size if wrap else size - 1)]
        down = [(j, i) for i, j in up]
        last = lax.slice_in_dim(value, length - width, length, axis=dim)
        initial = lax.slice_in_dim(value, 0, width, axis=dim)
        before = lax.ppermute(last, axis, up)
        after = lax.ppermute(initial, axis, down)
        value = jnp.concatenate([before, value, after], axis=dim)
    return value


def primitives(values):
    density = values[0]
    velo_x = values[1] / density
    velo_y = values[2] / density
    velo_z = values[3] / density
    kinetic = 0.5 * density * (velo_x * velo_x + velo_y * velo_y + velo_z * velo_z)
    pressure = (heat_ratio - 1.0) * (values[4] - kinetic)
    return (density, velo_x, velo_y, velo_z, pressure)


def conserved(density, velo_x, velo_y, velo_z, pressure):
    energy = pressure / (heat_ratio - 1.0) + 0.5 * density * (
        velo_x * velo_x + velo_y * velo_y + velo_z * velo_z
    )
    return jnp.stack([density, density * velo_x, density * velo_y, density * velo_z, energy])


def wall_ghost(cell_row, surf_temp, surf_blow, kind_rows):
    density, velo_x, velo_y, velo_z, pressure = primitives(cell_row)
    wall_density = pressure / surf_temp
    noslip = conserved(wall_density, -velo_x, -velo_y, -velo_z, pressure)
    slip_state = conserved(density, velo_x, velo_y, -velo_z, pressure)
    blow_state = conserved(wall_density, -velo_x, -velo_y, 2.0 * surf_blow - velo_z, pressure)
    return jnp.where(kind_rows == 0, noslip, jnp.where(kind_rows == 1, slip_state, blow_state))


def shifted_slice(padded, along_axis, offset, length):
    return lax.slice_in_dim(padded, 2 + offset, 2 + offset + length, axis=along_axis)


def first_diff(padded, along_axis, length):
    near_diff = shifted_slice(padded, along_axis, 1, length) - shifted_slice(
        padded, along_axis, -1, length
    )
    outer_diff = shifted_slice(padded, along_axis, 2, length) - shifted_slice(
        padded, along_axis, -2, length
    )
    return (8.0 * near_diff - outer_diff) / 12.0


def second_diff(padded, along_axis, length):
    near_sum = shifted_slice(padded, along_axis, 1, length) + shifted_slice(
        padded, along_axis, -1, length
    )
    outer_sum = shifted_slice(padded, along_axis, 2, length) + shifted_slice(
        padded, along_axis, -2, length
    )
    return (
        16.0 * near_sum - outer_sum - 30.0 * shifted_slice(padded, along_axis, 0, length)
    ) / 12.0


def wrap_last(values):
    return jnp.concatenate([values[..., -2:], values, values[..., :2]], axis=-1)


def fluxes(values, normal):
    density, velo_x, velo_y, velo_z, pressure = primitives(values)
    speeds = (velo_x, velo_y, velo_z)
    normal_speed = speeds[normal]
    momentum_flux = [values[1] * normal_speed, values[2] * normal_speed, values[3] * normal_speed]
    momentum_flux[normal] = momentum_flux[normal] + pressure
    face_flux = jnp.stack(
        [
            values[normal + 1],
            momentum_flux[0],
            momentum_flux[1],
            momentum_flux[2],
            (values[4] + pressure) * normal_speed,
        ]
    )
    lap_fields = jnp.stack([velo_x, velo_y, velo_z, pressure / density])
    return (face_flux, lap_fields)


def advance(padded_state, padded_heights, normalized):
    depth_k = padded_heights.shape[0] - 4
    rows_i = padded_state.shape[2] - 4
    cols_j = padded_state.shape[3]
    center_state = padded_state[:, 2:-2, 2:-2, :]
    side_state = padded_state[:, 2:-2, :, :]
    stack_state = padded_state[:, :, 2:-2, :]
    flux_i, lap_i = fluxes(side_state, 0)
    flux_j, lap_j = fluxes(wrap_last(center_state), 1)
    flux_k, lap_k = fluxes(stack_state, 2)
    metric = first_diff(padded_heights, 0, depth_k)
    convect = (
        first_diff(flux_i, 2, rows_i)
        + first_diff(flux_j, 3, cols_j)
        + first_diff(flux_k, 1, depth_k) / metric
    )
    laplace = (
        second_diff(lap_i, 2, rows_i)
        + second_diff(lap_j, 3, cols_j)
        + second_diff(lap_k, 1, depth_k) / (metric * metric)
    )
    viscous = jnp.stack(
        [
            jnp.zeros_like(laplace[0]),
            viscosity * laplace[0],
            viscosity * laplace[1],
            viscosity * laplace[2],
            conduction * laplace[3],
        ]
    )
    far_field = jnp.array(far_values, jnp.float32)[:, None, None, None]
    sponge = sponge_rate * normalized * normalized * (center_state - far_field)
    return center_state + time_step * (viscous - convect - sponge)


def ablate(abl_temp, col_film, col_recovery, col_conduct, col_diffuse, col_rate):
    inner_temp = abl_temp[1]
    surface = abl_temp[0]
    for newton_pass in range(2):
        surface_cube = surface * surface * surface
        surface = (
            col_film * col_recovery
            + col_conduct * inner_temp
            + 3.0 * radiation * surface_cube * surface
        ) / (col_film + col_conduct + 4.0 * radiation * surface_cube)
    recession = col_rate * jnp.exp(-activation / surface)
    blowing = blow_ratio * recession
    profile = jnp.concatenate([surface[None], abl_temp[1:]], axis=0)
    for heat_pass in range(2):
        middle = profile[1:-1] + col_diffuse * (profile[2:] - 2.0 * profile[1:-1] + profile[:-2])
        bottom = profile[-1] + 2.0 * col_diffuse * (profile[-2] - profile[-1])
        profile = jnp.concatenate([profile[:1], middle, bottom[None]], axis=0)
    return (surface, blowing, recession, profile)


def add_terms(earlier, later):
    return earlier + later


def shards(flow_state, spacing, bc_kind, cell_of, zone_id, abl_temp, conduct, diffuse, rate):
    tile_count = lax.axis_size("surf")
    wall_count = lax.axis_size("wall")
    wall_pos = lax.axis_index("wall")
    rows_i = flow_state.shape[2]
    cols_j = flow_state.shape[3]
    tile_cells = rows_i * cols_j
    density, velo_x, velo_y, velo_z, pressure = primitives(flow_state[:, 0])
    recovery_temp = pressure / density + recovery * (
        velo_x * velo_x + velo_y * velo_y + velo_z * velo_z
    )
    film = film_conduct / (0.5 * spacing[0])
    wall_fields = from_root(jnp.stack([film, recovery_temp]).reshape(2, tile_cells), "wall", 0)
    per_tile = cell_of.shape[0] // tile_count
    owner_tile = cell_of // tile_cells
    within_tile = cell_of % tile_cells
    sort_order = jnp.argsort(owner_tile, stable=True)
    inverse_order = jnp.argsort(sort_order)
    sorted_cells = within_tile[sort_order].reshape(tile_count, per_tile)
    asked_cells = lax.all_to_all(sorted_cells, "surf", split_axis=0, concat_axis=0, tiled=True)
    film_ask = jnp.take(wall_fields[0], asked_cells)
    recovery_ask = jnp.take(wall_fields[1], asked_cells)
    film_back = lax.all_to_all(film_ask, "surf", split_axis=0, concat_axis=0, tiled=True)
    recovery_back = lax.all_to_all(recovery_ask, "surf", split_axis=0, concat_axis=0, tiled=True)
    film_rows, recovery_rows, asked_cells = (film_back, recovery_back, asked_cells)
    col_film = film_rows.reshape(-1)[inverse_order]
    col_recovery = recovery_rows.reshape(-1)[inverse_order]
    zone_mask = (zone_id[None, :] == jnp.arange(conduct.shape[0], dtype=jnp.int32)[:, None]).astype(
        jnp.float32
    )
    col_conduct = jnp.sum(zone_mask * conduct[:, None], axis=0)
    col_diffuse = jnp.sum(zone_mask * diffuse[:, None], axis=0)
    col_rate = jnp.sum(zone_mask * rate[:, None], axis=0)
    surface, blowing, recession, ablator_next = ablate(
        abl_temp, col_film, col_recovery, col_conduct, col_diffuse, col_rate
    )
    outgoing = jnp.stack([surface, blowing, recession])[:, sort_order].reshape(
        3, tile_count, per_tile
    )
    arrived = lax.all_to_all(outgoing, "surf", split_axis=1, concat_axis=1, tiled=True)
    dense_rows = jnp.zeros((3, tile_cells), jnp.float32).at[:, asked_cells].set(arrived)
    slab_total = jnp.sum(spacing, axis=0)
    wall_sums, column_total = lax.psum((dense_rows, slab_total), "wall")
    slab_offset = prefix(slab_total, "wall", add_terms, jnp.zeros_like(slab_total))
    wall_grid = wall_sums.reshape(3, rows_i, cols_j)
    surf_temp = wall_grid[0]
    surf_blow = wall_grid[1]
    surf_recess = wall_grid[2]
    center = slab_offset + jnp.cumsum(spacing, axis=0) - 0.5 * spacing
    node_shift = surf_recess * (center / column_total - 1.0)
    shifted = center + node_shift
    is_bottom = wall_pos == 0
    is_top = wall_pos == wall_count - 1
    padded_state = padded_2(flow_state, (("surf", 2), ("wall", 1)), 2, True)
    padded_heights = padded_2(shifted, (("wall", 0),), 2, False)
    wall_low = jnp.stack([3.0 * shifted[0] - 2.0 * shifted[1], 2.0 * shifted[0] - shifted[1]])
    wall_high = jnp.stack([2.0 * shifted[-1] - shifted[-2], 3.0 * shifted[-1] - 2.0 * shifted[-2]])
    padded_heights = jnp.concatenate(
        [
            jnp.where(is_bottom, wall_low, padded_heights[:2]),
            padded_heights[2:-2],
            jnp.where(is_top, wall_high, padded_heights[-2:]),
        ],
        axis=0,
    )
    ghost_one = wall_ghost(flow_state[:, 0], surf_temp, surf_blow, bc_kind)
    ghost_two = wall_ghost(flow_state[:, 1], surf_temp, surf_blow, bc_kind)
    bottom_rows = jnp.stack([ghost_two, ghost_one], axis=1)
    top_rows = jnp.broadcast_to(
        jnp.array(far_values, jnp.float32)[:, None, None, None], (5, 2, rows_i, cols_j)
    )
    inner_cols = padded_state[:, :, 2:-2, :]
    low_rows = jnp.where(is_bottom, bottom_rows, inner_cols[:, :2])
    high_rows = jnp.where(is_top, top_rows, inner_cols[:, -2:])
    inner_cols = jnp.concatenate([low_rows, inner_cols[:, 2:-2], high_rows], axis=1)
    padded_state = padded_state.at[:, :, 2:-2, :].set(inner_cols)
    state_next = advance(padded_state, padded_heights, center / column_total)
    return (state_next, node_shift, ablator_next)


def solution(mesh):
    in_specs = (
        P(None, "wall", "surf", None),
        P("wall", "surf", None),
        P("surf", None),
        P(("surf", "wall")),
        P(("surf", "wall")),
        P(None, ("surf", "wall")),
        P(),
        P(),
        P(),
    )
    out_specs = (P(None, "wall", "surf", None), P("wall", "surf", None), P(None, ("surf", "wall")))
    return jax.shard_map(shards, mesh=mesh, in_specs=in_specs, out_specs=out_specs, check_vma=False)
```

profile of v0, /device:TPU:1, one launch (start us, length us, event | category | flops | bytes accessed | tf_op | source)
XLA Modules:
  0.0 335.7 jit_solution(16355267957275769388)
XLA Ops:
  12.4 4.5 %gather_fusion = s32[1024]{0:T(1024)S(1)} fusion(s32[1024]{0:T(1024)S(1)} %get-tuple-element.224, s32[1024]{0:T(1024)S(1)} %fusion.49), kind=kCustom, calls=%fused_computation.2 | custom fusion | bytes 12288 | tf_op jit(solution)/shard_map/gather | solution.py:201
  17.6 9.2 %all-to-all-start = ((s32[32,1,32]{2,1,0:T(1,128)}), s32[32,1,32]{2,1,0:T(1,128)S(1)}, u32[]{:S(2)}, u32[]{:S(2)}) async-start(s32[32,1,32]{2,1,0:T(1,128)} %all_to_all.25), calls=%async_computation | async-start | bytes 32768 | tf_op jit(solution)/shard_map/all_to_all | solution.py:202
  29.6 4.5 %collective-permute-start.1 = (f32[5,32,2,512]{3,2,1,0:T(2,128)}, f32[5,32,2,512]{3,2,1,0:T(2,128)}, u32[]{:S(2)}, u32[]{:S(2)}) collective-permute-start(f32[5,32,2,512]{3,2,1,0:T(2,128)} %get-tuple-element.207), channel_id=1, source_target_pairs={{4,0},{8,4},{12,8},{16,12},{20,16},{24,20},{28,24},{32,28},{36,32}... | collective-permute-start | bytes 1966088 | tf_op jit(solution)/shard_map/ppermute | solution.py:44
  36.3 23.7 %psum.21 = f32[2,4096]{1,0:T(2,128)S(1)} all-reduce(f32[2,4096]{1,0:T(2,128)S(1)} %maximum_select_fusion), channel_id=1, replica_groups=mesh['surf'=32,'wall'=4] {'wall'}, use_global_device_ids=true, to_apply=%region_1.2 | all-reduce | flops 8192 | bytes 65536 | tf_op jit(solution)/shard_map/psum | solution.py:21
  65.1 6.7 %all-gather = f32[32,512]{1,0:T(8,128)S(1)} all-gather(f32[8,512]{1,0:T(8,128)S(1)} %reduce_sum.44), channel_id=2, replica_groups=mesh['surf'=32,'wall'=4] {'wall'}, dimensions={0}, use_global_device_ids=true | all-gather | bytes 81920 | tf_op jit(solution)/shard_map/all_gather | solution.py:26
  84.3 6.1 %gather_fusion.5 = f32[1024]{0:T(1024)S(1)} fusion(f32[4096]{0:T(1024)S(1)} %bitcast.52, s32[1024]{0:T(1024)S(1)} %broadcast_clamp_fusion), kind=kCustom, calls=%fused_computation.1.clone | custom fusion | bytes 12288 | tf_op jit(solution)/shard_map/jit(_take)/gather | solution.py:204
  91.2 6.1 %gather_fusion.4 = f32[1024]{0:T(1024)S(1)} fusion(f32[4096]{0:T(1024)S(1)} %bitcast.51, s32[1024]{0:T(1024)S(1)} %broadcast_clamp_fusion), kind=kCustom, calls=%fused_computation.clone | custom fusion | bytes 12288 | tf_op jit(solution)/shard_map/jit(_take)/gather | solution.py:203
  98.7 6.7 %all-to-all-start.1 = ((f32[32,1,32]{2,1,0:T(1,128)}), f32[32,1,32]{2,1,0:T(1,128)S(1)}, u32[]{:S(2)}, u32[]{:S(2)}) async-start(f32[32,1,32]{2,1,0:T(1,128)} %bitcast.62), calls=%async_computation.1 | async-start | bytes 32768 | tf_op jit(solution)/shard_map/all_to_all | solution.py:205
  107.0 5.5 %all-to-all-done.1 = f32[32,1,32]{2,1,0:T(1,128)S(1)} async-done(((f32[32,1,32]{2,1,0:T(1,128)}), f32[32,1,32]{2,1,0:T(1,128)S(1)}, u32[]{:S(2)}, u32[]{:S(2)}) %all-to-all-start.1) | async-done | bytes 4128 | tf_op jit(solution)/shard_map/all_to_all | solution.py:205
  112.5 4.5 %all-to-all-start.2 = ((f32[32,1,32]{2,1,0:T(1,128)}), f32[32,1,32]{2,1,0:T(1,128)}, u32[]{:S(2)}, u32[]{:S(2)}) async-start(f32[32,1,32]{2,1,0:T(1,128)} %bitcast.61), calls=%async_computation.2 | async-start | bytes 32768 | tf_op jit(solution)/shard_map/all_to_all | solution.py:206
  119.1 4.8 %all-to-all-done.2 = f32[32,1,32]{2,1,0:T(1,128)} async-done(((f32[32,1,32]{2,1,0:T(1,128)}), f32[32,1,32]{2,1,0:T(1,128)}, u32[]{:S(2)}, u32[]{:S(2)}) %all-to-all-start.2) | async-done | bytes 4128 | tf_op jit(solution)/shard_map/all_to_all | solution.py:206
  125.5 5.0 %gather_fusion.1 = f32[1024]{0:T(1024)S(1)} fusion(f32[1024]{0:T(1024)S(1)} %reshape.984, s32[1024]{0:T(1024)} %fusion.50), kind=kCustom, calls=%fused_computation.3 | custom fusion | bytes 12288 | tf_op jit(solution)/shard_map/gather | solution.py:208
  130.5 4.5 %gather_fusion.2 = f32[1024]{0:T(1024)S(1)} fusion(f32[1024]{0:T(1024)S(1)} %reshape.985, s32[1024]{0:T(1024)S(1)} %copy-done.22), kind=kCustom, calls=%fused_computation.4 | custom fusion | bytes 12288 | tf_op jit(solution)/shard_map/gather | solution.py:209
  136.2 5.1 %gather_fusion.3 = f32[1024,3]{1,0:T(8,128)} fusion(f32[3,1024]{0,1:T(8,128)} %copy.46, s32[1024]{0:T(1024)S(1)} %fusion.49), kind=kCustom, calls=%fused_computation.5 | custom fusion | bytes 28672 | tf_op jit(solution)/shard_map/gather | solution.py:219
  143.2 4.6 %all-to-all-start.3 = ((f32[3,32,32]{2,0,1:T(4,128)}), f32[3,32,32]{2,0,1:T(4,128)}, u32[]{:S(2)}, u32[]{:S(2)}) async-start(f32[3,32,32]{2,0,1:T(4,128)} %copy.47), calls=%async_computation.3 | async-start | bytes 131072 | tf_op jit(solution)/shard_map/all_to_all | solution.py:222
  149.0 5.9 %all-to-all-done.3 = f32[3,32,32]{2,0,1:T(4,128)} async-done(((f32[3,32,32]{2,0,1:T(4,128)}), f32[3,32,32]{2,0,1:T(4,128)}, u32[]{:S(2)}, u32[]{:S(2)}) %all-to-all-start.3) | async-done | bytes 12320 | tf_op jit(solution)/shard_map/all_to_all | solution.py:222
  156.8 4.9 %scatter_custom_fusion = f32[3,4096]{0,1:T(8,128)} fusion(s32[1024]{0:T(1024)S(1)} %reshape.1037, f32[1024,3]{1,0:T(8,128)} %bitcast.56, f32[]{:T(128)} %constant.146.clone.1), kind=kCustom, calls=%fused_computation.67 | custom fusion | bytes 49664 | tf_op jit(solution)/shard_map/scatter | solution.py:223
  162.5 61.3 %all-reduce.3.cloned.1.call-done = (f32[3,4096]{0,1:T(8,128)}, f32[8,512]{1,0:T(8,128)}) async-done(((f32[3,4096]{0,1:T(8,128)}, f32[8,512]{1,0:T(8,128)}), (f32[3,4096]{0,1:T(8,128)}, f32[8,512]{1,0:T(8,128)})) %all-reduce.3.cloned.1.call-update) | async-done | bytes 65552 | tf_op jit(solution)/shard_map/psum | solution.py:225
  223.8 5.8 %slice_reduce_fusion = (f32[4096]{0:T(1024)S(1)}, f32[4096]{0:T(1024)S(1)}, f32[4096]{0:T(1024)S(1)}) fusion(f32[3,4096]{0,1:T(8,128)} %get-tuple-element.129), kind=kLoop, calls=%fused_computation.35 | loop fusion | flops 4096 | bytes 98304 | tf_op jit(solution)/shard_map/slice | solution.py:230
  233.9 4.8 %collective-permute-start.5 = (f32[2,8,512]{2,1,0:T(8,128)S(1)}, f32[2,8,512]{2,1,0:T(8,128)S(1)}, u32[]{:S(2)}, u32[]{:S(2)}) collective-permute-start(f32[2,8,512]{2,1,0:T(8,128)S(1)} %get-tuple-element.214), channel_id=1, source_target_pairs={{0,1},{1,2},{2,3},{4,5},{5,6},{6,7},{8,9},{9,10},{10,11},{12,13},{... | collective-permute-start | bytes 98312 | tf_op jit(solution)/shard_map/ppermute | solution.py:43
  245.7 7.3 %collective-permute-done.3 = f32[5,2,12,512]{3,2,1,0:T(8,128)S(1)} collective-permute-done((f32[5,2,12,512]{3,2,1,0:T(8,128)S(1)}, f32[5,2,12,512]{3,2,1,0:T(8,128)S(1)}, u32[]{:S(2)}, u32[]{:S(2)}) %collective-permute-start.3) | collective-permute-done | bytes 245792 | tf_op jit(solution)/shard_map/ppermute | solution.py:44
  260.3 20.5 %scatter.13 = f32[5,36,12,512]{3,2,1,0:T(8,128)} dynamic-update-slice(f32[5,36,12,512]{3,2,1,0:T(8,128)} %pad_maximum_fusion, f32[5,36,8,512]{3,2,1,0:T(8,128)} %copy-done.2, s32[]{:T(128)} %constant.148.clone.1, s32[]{:T(128)} %constant.148.clone.1, s32[]{:T(128)} %constant.164.clone.1, s32[]{:T(128)} %constant.148.clone.1) | dynamic-update-slice | bytes 5898244 | tf_op jit(solution)/shard_map/scatter | solution.py:258
  295.2 10.6 %fusion.16 = f32[4,32,8,512]{3,2,1,0:T(8,128)} fusion(f32[4,36,8,512]{3,2,1,0:T(8,128)S(1)} %pad_maximum_fusion.5, f32[4,32,8,516]{3,2,1,0:T(8,128)S(1)} %copy-done.1, f32[4,32,12,512]{3,2,1,0:T(8,128)} %pad_maximum_fusion.1, f32[32,8,512]{2,1,0:T(8,128)} %get-tuple-element.150), kind=kLoop, calls=%fused_computation.40 | loop fusion | flops 12058624 | bytes 34078720 | tf_op jit(solution)/shard_map/add | solution.py:141
  313.4 15.5 %multiply_add_fusion = f32[5,32,8,512]{3,2,1,0:T(8,128)} fusion(f32[5,32,8,512]{3,2,1,0:T(8,128)S(1)} %copy-done, f32[5,32,8,512]{3,2,1,0:T(8,128)} %fusion.37, f32[5,36,8,512]{3,2,1,0:T(8,128)S(1)} %get-tuple-element.186, f32[5,32,8,516]{3,2,1,0:T(8,128)} %get-tuple-element.182, f32[5,32,12,512]{3,2,1,0:T(8,128)} %copy-done.5, f32[5]{0:T(128)S(1)} %copy-done.34, ...), kind=kLoop, calls=%fused_computation.33 | loop fusion | flops 15073280 | bytes 40370196 | tf_op jit(solution)/shard_map/add | solution.py:156
  (198 shorter events, 82.5 us)
Async XLA Ops:
  7.2 19.7 %copy-start = (f32[5,32,8,512]{3,2,1,0:T(8,128)S(1)}, f32[5,32,8,512]{3,2,1,0:T(8,128)}, u32[]{:S(2)}) copy-start(f32[5,32,8,512]{3,2,1,0:T(8,128)} %param.17) | copy-start | bytes 7864324
  17.6 66.6 %all-to-all-start = ((s32[32,1,32]{2,1,0:T(1,128)}), s32[32,1,32]{2,1,0:T(1,128)S(1)}, u32[]{:S(2)}, u32[]{:S(2)}) async-start(s32[32,1,32]{2,1,0:T(1,128)} %all_to_all.25), calls=%async_computation | async-start | bytes 32768 | tf_op jit(solution)/shard_map/all_to_all | solution.py:202
  26.9 9.3 %copy-start.6 = (f32[32,8,512]{2,1,0:T(8,128)S(1)}, f32[32,8,512]{2,1,0:T(8,128)}, u32[]{:S(2)}) copy-start(f32[32,8,512]{2,1,0:T(8,128)} %param.18) | copy-start | bytes 1572868
  28.4 211.6 %collective-permute-start = (f32[5,32,2,512]{3,2,1,0:T(2,128)}, f32[5,32,2,512]{3,2,1,0:T(2,128)}, u32[]{:S(2)}, u32[]{:S(2)}) collective-permute-start(f32[5,32,2,512]{3,2,1,0:T(2,128)} %get-tuple-element.206), channel_id=1, source_target_pairs={{0,4},{4,8},{8,12},{12,16},{16,20},{20,24},{24,28},{28,32},{32,36}... | collective-permute-start | bytes 1966088 | tf_op jit(solution)/shard_map/ppermute | solution.py:43
  29.6 210.4 %collective-permute-start.1 = (f32[5,32,2,512]{3,2,1,0:T(2,128)}, f32[5,32,2,512]{3,2,1,0:T(2,128)}, u32[]{:S(2)}, u32[]{:S(2)}) collective-permute-start(f32[5,32,2,512]{3,2,1,0:T(2,128)} %get-tuple-element.207), channel_id=1, source_target_pairs={{4,0},{8,4},{12,8},{16,12},{20,16},{24,20},{28,24},{32,28},{36,32}... | collective-permute-start | bytes 1966088 | tf_op jit(solution)/shard_map/ppermute | solution.py:44
  35.4 46.5 %copy-start.10 = (f32[1,1,8,512]{3,2,1,0:T(8,128)}, f32[1,1,8,512]{3,2,1,0:T(8,128)S(1)}, u32[]{:S(2)}) copy-start(f32[1,1,8,512]{3,2,1,0:T(8,128)S(1)} %get-tuple-element.171) | copy-start | bytes 49156
  36.0 39.6 %copy-start.17 = (f32[5,1,8,512]{3,2,1,0:T(8,128)}, f32[5,1,8,512]{3,2,1,0:T(8,128)S(1)}, u32[]{:S(2)}) copy-start(f32[5,1,8,512]{3,2,1,0:T(8,128)S(1)} %get-tuple-element.154) | copy-start | bytes 245764
  91.1 15.1 %copy-start.9 = (f32[64,1024]{1,0:T(8,128)S(1)}, f32[64,1024]{1,0:T(8,128)}, u32[]{:S(2)}) copy-start(f32[64,1024]{1,0:T(8,128)} %param.22) | copy-start | bytes 786436
  91.1 25.9 %copy-start.13 = (s32[32,1,32]{2,1,0:T(1,128)S(1)}, s32[32,1,32]{2,1,0:T(1,128)}, u32[]{:S(2)}) copy-start(s32[32,1,32]{2,1,0:T(1,128)} %copy-done.12) | copy-start | bytes 12292
  98.7 13.9 %all-to-all-start.1 = ((f32[32,1,32]{2,1,0:T(1,128)}), f32[32,1,32]{2,1,0:T(1,128)S(1)}, u32[]{:S(2)}, u32[]{:S(2)}) async-start(f32[32,1,32]{2,1,0:T(1,128)} %bitcast.62), calls=%async_computation.1 | async-start | bytes 32768 | tf_op jit(solution)/shard_map/all_to_all | solution.py:205
  105.4 25.1 %copy-start.22 = (s32[1024]{0:T(1024)S(1)}, s32[1024]{0:T(1024)}, u32[]{:S(2)}) copy-start(s32[1024]{0:T(1024)} %fusion.50) | copy-start | bytes 12292
  112.5 11.4 %all-to-all-start.2 = ((f32[32,1,32]{2,1,0:T(1,128)}), f32[32,1,32]{2,1,0:T(1,128)}, u32[]{:S(2)}, u32[]{:S(2)}) async-start(f32[32,1,32]{2,1,0:T(1,128)} %bitcast.61), calls=%async_computation.2 | async-start | bytes 32768 | tf_op jit(solution)/shard_map/all_to_all | solution.py:206
  130.5 18.4 %copy-start.26 = (f32[1024]{0:T(1024)S(1)}, f32[1024]{0:T(1024)}, u32[]{:S(2)}) copy-start(f32[1024]{0:T(1024)} %broadcast_multiply_fusion) | copy-start | bytes 12292
  143.2 11.8 %all-to-all-start.3 = ((f32[3,32,32]{2,0,1:T(4,128)}), f32[3,32,32]{2,0,1:T(4,128)}, u32[]{:S(2)}, u32[]{:S(2)}) async-start(f32[3,32,32]{2,0,1:T(4,128)} %copy.47), calls=%async_computation.3 | async-start | bytes 131072 | tf_op jit(solution)/shard_map/all_to_all | solution.py:222
  147.7 76.0 %all-reduce.3.cloned.1.call-start = ((), (), s32[]{:S(2)}) async-start(), calls=%async_computation.4 | async-start | bytes 4227072 | tf_op jit(solution)/shard_map/psum | solution.py:225
  229.6 9.4 %copy-start.18 = (f32[5,1,8,512]{3,2,1,0:T(8,128)S(1)}, f32[5,1,8,512]{3,2,1,0:T(8,128)}, u32[]{:S(2)}) copy-start(f32[5,1,8,512]{3,2,1,0:T(8,128)} %copy-done.17) | copy-start | bytes 245764
  229.6 9.4 %copy-start.20 = (f32[5,1,8,512]{3,2,1,0:T(8,128)S(1)}, f32[5,1,8,512]{3,2,1,0:T(8,128)}, u32[]{:S(2)}) copy-start(f32[5,1,8,512]{3,2,1,0:T(8,128)} %copy-done.19) | copy-start | bytes 245764
  229.7 9.4 %copy-start.27 = (pred[8,512]{1,0:T(8,128)(4,1)S(1)}, pred[8,512]{1,0:T(8,128)(4,1)}, u32[]{:S(2)}) copy-start(pred[8,512]{1,0:T(8,128)(4,1)} %get-tuple-element.219) | copy-start | bytes 12292
  229.7 9.4 %copy-start.28 = (pred[8,512]{1,0:T(8,128)(4,1)S(1)}, pred[8,512]{1,0:T(8,128)(4,1)}, u32[]{:S(2)}) copy-start(pred[8,512]{1,0:T(8,128)(4,1)} %get-tuple-element.220) | copy-start | bytes 12292
  231.7 9.3 %collective-permute-start.4 = (f32[2,8,512]{2,1,0:T(8,128)S(1)}, f32[2,8,512]{2,1,0:T(8,128)S(1)}, u32[]{:S(2)}, u32[]{:S(2)}) collective-permute-start(f32[2,8,512]{2,1,0:T(8,128)S(1)} %get-tuple-element.213), channel_id=1, source_target_pairs={{1,0},{2,1},{3,2},{5,4},{6,5},{7,6},{9,8},{10,9},{11,10},{13,12},{... | collective-permute-start | bytes 98312 | tf_op jit(solution)/shard_map/ppermute | solution.py:44
  233.9 6.0 %collective-permute-start.5 = (f32[2,8,512]{2,1,0:T(8,128)S(1)}, f32[2,8,512]{2,1,0:T(8,128)S(1)}, u32[]{:S(2)}, u32[]{:S(2)}) collective-permute-start(f32[2,8,512]{2,1,0:T(8,128)S(1)} %get-tuple-element.214), channel_id=1, source_target_pairs={{0,1},{1,2},{2,3},{4,5},{5,6},{6,7},{8,9},{9,10},{10,11},{12,13},{... | collective-permute-start | bytes 98312 | tf_op jit(solution)/shard_map/ppermute | solution.py:43
  240.0 13.1 %copy-start.30 = (f32[5]{0:T(128)S(1)}, f32[5]{0:T(128)}, u32[]{:S(2)}) copy-start(f32[5]{0:T(128)} %constant.174.clone) | copy-start | bytes 64
  241.0 12.1 %collective-permute-start.3 = (f32[5,2,12,512]{3,2,1,0:T(8,128)S(1)}, f32[5,2,12,512]{3,2,1,0:T(8,128)S(1)}, u32[]{:S(2)}, u32[]{:S(2)}) collective-permute-start(f32[5,2,12,512]{3,2,1,0:T(8,128)S(1)} %get-tuple-element.185), channel_id=1, source_target_pairs={{1,0},{2,1},{3,2},{0,3},{5,4},{6,5},{7,6},{4,7},{9,8},{10,9},{11,1... | collective-permute-start | bytes 737288 | tf_op jit(solution)/shard_map/ppermute | solution.py:44
  241.1 12.0 %collective-permute-start.2 = (f32[5,2,12,512]{3,2,1,0:T(8,128)S(1)}, f32[5,2,12,512]{3,2,1,0:T(8,128)S(1)}, u32[]{:S(2)}, u32[]{:S(2)}) collective-permute-start(f32[5,2,12,512]{3,2,1,0:T(8,128)S(1)} %get-tuple-element.184), channel_id=1, source_target_pairs={{0,1},{1,2},{2,3},{3,0},{4,5},{5,6},{6,7},{7,4},{8,9},{9,10},{10,1... | collective-permute-start | bytes 737288 | tf_op jit(solution)/shard_map/ppermute | solution.py:43
  (24 other events, 104.3 us)
Sparse Core Ops, SparseCore 0:
  161.9 61.8 all-reduce.2
where the time goes:
time: 338 us; the launch traced here: 336 us
  other arithmetic  86.1 us (25%)
  waiting for transfers between devices  84.9 us (25%)
  local copies, waits for them, and re-layouts  77.7 us (23%)
  starting transfers between devices  41.6 us (12%)
  blocking collectives  30.4 us (9%)
  between operations  14.9 us (4%)
    psum x1, waiting for transfers between devices, shards(): wall_sums, column_total = lax.psum((dense_rows, slab_total), 'wall')  61.3 us
    psum x1, blocking collectives, from_root(): return lax.psum(kept, axis)  23.7 us
    scatter x1, local copies, waits for them, and re-layouts, shards(): padded_state = padded_state.at[:, :, 2:-2, :].set(inner_cols)  20.5 us
    add x1, other arithmetic, advance(): return center_state + time_step * (viscous - convect - sponge)  15.5 us
    unnamed x27, other arithmetic  13.4 us
    unnamed x87, local copies, waits for them, and re-layouts  10.9 us
    add x1, other arithmetic, advance(): second_diff(lap_i, 2, rows_i) + second_diff(lap_j, 3, cols_j)  10.6 us
    ppermute x3, starting transfers between devices, padded_2(): before = lax.ppermute(last, axis, up)  9.75 us
  transfers between devices with their start and end apart: 11, of which 5 were waited for; matrix products, arithmetic and copies ran while one was open for 23% of the time, Pallas kernels for 0%

commit v1 on v0

v1 whole, which is shorter than its diff:
```python
import functools
import jax
import jax.numpy as jnp
from jax import lax
from jax.experimental import pallas as pl
from jax.experimental.pallas import tpu as pltpu
from jax.sharding import PartitionSpec as P

gas = 0.4
time_step = 0.15
viscosity = 0.05
conduction = 0.07
sponge_rate = 0.5
activation = 2.0
radiation = 0.8
recovery = 0.2
far_values = (1.0, 0.5, 0.0, 0.0, 2.625)
diffusivity = (viscosity, viscosity, viscosity, conduction)

F32 = jnp.float32
BF16 = jnp.bfloat16
CHUNK = 4


def iota(shape, axis):
    return lax.broadcasted_iota(jnp.int32, shape, axis)


def split3(x):
    high = x.astype(BF16)
    rest = x - high.astype(F32)
    middle = rest.astype(BF16)
    low = (rest - middle.astype(F32)).astype(BF16)
    return high, middle, low


def dot_nn(a, b):
    return lax.dot_general(a, b, (((1,), (0,)), ((), ())), preferred_element_type=F32)


def dot_nt(a, b):
    return lax.dot_general(a, b, (((1,), (1,)), ((), ())), preferred_element_type=F32)


def join3(x, rows):
    return x[:rows] + x[rows : 2 * rows] + x[2 * rows :]


def to_rows(x):
    return jnp.concatenate([x[:, 128 * c : 128 * c + 128] for c in range(4)], axis=0)


def to_grid(x):
    return jnp.concatenate([x[8 * c : 8 * c + 8] for c in range(4)], axis=1)


def onehot(mask):
    return jnp.where(mask, 1.0, 0.0).astype(BF16)


def primitives(u0, u1, u2, u3, u4):
    inverse = 1.0 / u0
    vx = u1 * inverse
    vy = u2 * inverse
    vz = u3 * inverse
    pressure = gas * (u4 - 0.5 * (u1 * vx + u2 * vy + u3 * vz))
    return inverse, vx, vy, vz, pressure


def pack_kernel(flow, spacing, next_side, prev_side, up_wall, down_wall, wall_fields):
    row = iota((8, 512), 0) // 2
    for m in range(5):

        def gather(block, carry, m=m):
            high = jnp.zeros((8, 512), F32)
            low = jnp.zeros((8, 512), F32)
            for b in range(4):
                plane = flow[m, block * 4 + b]
                rolled_high = pltpu.roll(plane, (2 * b + 2) % 8, 0)
                rolled_low = pltpu.roll(plane, 2 * b, 0) if b else plane
                high = jnp.where(row == b, rolled_high, high)
                low = jnp.where(row == b, rolled_low, low)
            next_side[m, block] = high
            prev_side[m, block] = low
            return carry

        lax.fori_loop(0, 8, gather, 0)
    for m in range(5):
        for layer in range(2):
            up_wall[2 * m + layer] = flow[m, 30 + layer]
            down_wall[2 * m + layer] = flow[m, layer]
    for layer in range(2):
        up_wall[10 + layer] = spacing[30 + layer]
        down_wall[10 + layer] = spacing[layer]
    inverse, vx, vy, vz, pressure = primitives(*[flow[m, 0] for m in range(5)])
    film = 2.0 / spacing[0]
    temp = pressure * inverse + recovery * (vx * vx + vy * vy + vz * vz)
    total = spacing[0]
    for k in range(1, 32):
        total = total + spacing[k]
    for index, value in enumerate((film, temp, total)):
        up_wall[12 + index] = value
        down_wall[12 + index] = value
        wall_fields[index] = value


def route_kernel(cell, zone, temps, outgoing, rank_out):
    cells = cell[...]
    tile = cells // 4096
    within = cells - tile * 4096
    hit = iota((32, 1024), 0) == tile
    ones = jnp.where(hit, 1.0, 0.0)
    stacked = jnp.concatenate([ones[:, 128 * k : 128 * k + 128] for k in range(8)], axis=0)
    inner = iota((128, 256), 0)
    outer = iota((128, 256), 1)
    ahead = onehot((inner < outer) | (outer >= 128))
    counts = dot_nn(stacked.astype(BF16), ahead)
    offset = jnp.zeros((32, 128), F32)
    ranks = []
    for k in range(8):
        part = slice(32 * k, 32 * k + 32)
        place = counts[part, :128] + offset
        ranks.append(jnp.sum(stacked[part] * place, axis=0, keepdims=True))
        offset = offset + counts[part, 128:]
    rank = jnp.concatenate(ranks, axis=1).astype(jnp.int32)
    rank_out[...] = rank
    slot = iota((32, 1024), 0) == rank
    first, second = temps[0:1], temps[1:2]
    fields = (within.astype(F32), (zone[...] + 1).astype(F32), first, second)
    pieces = [split3(value) for value in fields]
    rows = []
    for level in range(3):
        for piece in pieces:
            rows.append(jnp.where(slot, piece[level].astype(F32), 0.0).astype(BF16))
    sent = dot_nt(ones.astype(BF16), jnp.concatenate(rows, axis=0))
    outgoing[...] = sent[:, :128] + sent[:, 128:256] + sent[:, 256:]


def pick_wall(wall, own, low, opposite, high):
    return jnp.where(wall == 0, own, jnp.where(wall == 1, low, jnp.where(wall == 2, opposite, high)))


def surface_kernel(place, conduct, rate, arrived, own, low, opposite, high, dense, where_out):
    wall = place[0]
    received = arrived[...]
    pieces = jnp.concatenate(split3(received), axis=0)
    lane = iota((128, 1024), 1) % 32
    line = iota((128, 1024), 0)
    source = iota((32, 1024), 0) == iota((32, 1024), 1) // 32
    flat = []
    for f in range(4):
        spread = join3(dot_nn(pieces, onehot(line == lane + 32 * f)), 32)
        flat.append(jnp.sum(jnp.where(source, spread, 0.0), axis=0, keepdims=True))
    where_out[...] = flat[0]
    cells = flat[0].astype(jnp.int32)
    block = ((cells % 512) // 128) * 8 + cells // 512
    block_hit = iota((32, 1024), 0) == block
    lane_hit = onehot(line == cells % 128)
    rows = [jnp.where(block_hit, flat[1], 0.0).astype(BF16)]
    for value in flat[2:]:
        for piece in split3(value):
            rows.append(jnp.where(block_hit, piece.astype(F32), 0.0).astype(BF16))
    grid = dot_nt(jnp.concatenate(rows, axis=0), lane_hit)
    zones = to_grid(grid[:32])
    first = to_grid(join3(grid[32:128], 32))
    inner = to_grid(join3(grid[128:], 32))
    film = pick_wall(wall, own[0], low[12], opposite[0], high[12])
    recover = pick_wall(wall, own[1], low[13], opposite[1], high[13])
    cond = jnp.zeros((8, 512), F32)
    speed = jnp.zeros((8, 512), F32)
    for z in range(8):
        cond = jnp.where(zones == z + 1.0, conduct[z], cond)
        speed = jnp.where(zones == z + 1.0, rate[z], speed)
    surface = first
    base = film * recover + cond * inner
    for step in range(2):
        cube = surface * surface * surface
        surface = (base + 3.0 * radiation * cube * surface) / (film + cond + 4.0 * radiation * cube)
    recess = speed * jnp.exp(-activation / surface)
    taken = zones > 0.5
    dense[0] = jnp.where(taken, surface, 0.0)
    dense[1] = jnp.where(taken, recess, 0.0)


def return_kernel(where_in, dense, outgoing):
    cells = where_in[...].astype(jnp.int32)
    block = ((cells % 512) // 128) * 8 + cells // 512
    block_hit = iota((32, 1024), 0) == block
    line = iota((128, 1024), 0)
    lane_hit = onehot(line == cells % 128)
    pieces = jnp.concatenate(split3(to_rows(dense[0])), axis=0)
    spread = join3(dot_nn(pieces, lane_hit), 32)
    flat = jnp.sum(jnp.where(block_hit, spread, 0.0), axis=0, keepdims=True)
    source = iota((32, 1024), 0) == iota((32, 1024), 1) // 32
    rows = [jnp.where(source, piece.astype(F32), 0.0).astype(BF16) for piece in split3(flat)]
    slot = onehot(line == iota((128, 1024), 1) % 32)
    outgoing[...] = join3(dot_nt(jnp.concatenate(rows, axis=0), slot), 32)


def ablate_kernel(diffuse, cell, rank, zone, back, temps, out):
    pieces = jnp.concatenate(split3(back[...]), axis=0)
    slot = onehot(iota((128, 1024), 0) == rank[...])
    spread = join3(dot_nn(pieces, slot), 32)
    tile_hit = iota((32, 1024), 0) == cell[...] // 4096
    surface = jnp.sum(jnp.where(tile_hit, spread, 0.0), axis=0, keepdims=True)
    zones = zone[...]
    spread_rate = jnp.zeros((1, 1024), F32)
    for z in range(8):
        spread_rate = jnp.where(zones == z, diffuse[z], spread_rate)
    row = iota((64, 1024), 0)
    profile = jnp.where(row == 0, surface, temps[...])
    for step in range(2):
        before = pltpu.roll(profile, 1, 0)
        after = pltpu.roll(profile, 63, 0)
        after = jnp.where(row == 63, before, after)
        changed = profile + spread_rate * (after - 2.0 * profile + before)
        profile = jnp.where(row == 0, profile, changed)
    out[...] = profile


def stencil_kernel(
    place, flow, spacing, low, high, opposite, own, base, slope, curve, norm, total_out, fields, gaps, run
):
    wall = place[0]
    step = pl.program_id(0)
    twelfth = time_step / 12.0
    is_low = wall == 0
    is_high = wall == 3
    keep_low = jnp.where(is_low, 0.0, 1.0)

    def store_fields(position, values, keep):
        u0, u1, u2, u3, u4 = values
        inverse, vx, vy, vz, pressure = primitives(*values)
        results = (
            u3,
            u1 * vz,
            u2 * vz,
            u3 * vz + pressure,
            (u4 + pressure) * vz,
            vx,
            vy,
            vz,
            pressure * inverse,
            pressure,
        )
        for index, value in enumerate(results):
            fields[index, position] = value if keep is None else value * keep

    def own_plane(k, carry):
        store_fields(k + 2, [flow[m, k] for m in range(5)], None)
        return carry

    @pl.when(step == 0)
    def first():
        for layer in range(2):
            store_fields(layer, [low[2 * m + layer] for m in range(5)], keep_low)
            top = [jnp.where(is_high, far_values[m], high[2 * m + layer]) for m in range(5)]
            store_fields(34 + layer, top, None)
        lax.fori_loop(0, 2, own_plane, 0)
        before = jnp.where(wall >= 1, low[14], 0.0)
        before = before + jnp.where(wall >= 2, opposite[2], 0.0)
        before = before + jnp.where(wall >= 3, high[14], 0.0)
        run[0] = before
        total = own[2] + low[14] + opposite[2] + high[14]
        run[1] = 1.0 / total
        total_out[...] = total

        def gap(k, carry):
            gaps[k + 2] = 0.5 * (spacing[k] + spacing[k + 1])
            return carry

        lax.fori_loop(0, 31, gap, 0)
        gap_low = gaps[2]
        gap_high = gaps[32]
        gaps[0] = jnp.where(is_low, gap_low, 0.5 * (low[10] + low[11]))
        gaps[1] = jnp.where(is_low, gap_low, 0.5 * (low[11] + spacing[0]))
        gaps[33] = jnp.where(is_high, gap_high, 0.5 * (spacing[31] + high[10]))
        gaps[34] = jnp.where(is_high, gap_high, 0.5 * (high[10] + high[11]))

    ahead = jnp.minimum(step * CHUNK + 2 + CHUNK, 32)
    lax.fori_loop(step * CHUNK + 2, ahead, own_plane, 0)

    row = iota((8, 512), 0)
    inverse_total = run[1]

    def one_plane(b, below):
        k = step * CHUNK + b
        thick = spacing[k]
        center = below + 0.5 * thick
        normal = center * inverse_total
        norm[b] = normal - 1.0
        stretch = 7.0 * (gaps[k + 2] + gaps[k + 1]) - gaps[k + 3] - gaps[k]
        inverse_metric = 12.0 / stretch
        damp = time_step * sponge_rate * normal * normal
        slope_scale = -twelfth * inverse_metric
        curve_scale = twelfth * inverse_metric * inverse_metric
        u = [flow[m, k] for m in range(5)]
        vx, vy, vz, temp, pressure = [fields[m, k + 2] for m in range(5, 10)]
        heat = u[4] + pressure
        shear = u[1] * vy
        flux_i = (u[1], u[1] * vx + pressure, shear, u[1] * vz, heat * vx)
        flux_j = (u[2], shear, u[2] * vy + pressure, u[2] * vz, heat * vy)
        smooth = (None, vx, vy, vz, temp)
        for m in range(5):
            result = u[m] - damp * (u[m] - far_values[m])
            w = smooth[m]
            if w is not None:
                amount = twelfth * diffusivity[m - 1]
                w16 = (16.0 * amount) * w
                w1 = amount * w
                result = result - (60.0 * amount) * w
            for axis, flux in ((0, flux_i[m]), (1, flux_j[m])):
                near = (8.0 * twelfth) * flux
                far = twelfth * flux
                if w is None:
                    sources = (near, -near, -far, far)
                else:
                    sources = (w16 + near, w16 - near, -w1 - far, far - w1)
                if axis == 0:
                    limits = (row != 7, row != 0, row < 6, row >= 2)
                    sources = [jnp.where(limit, value, 0.0) for limit, value in zip(limits, sources)]
                size = (8, 512)[axis]
                for shift, value in zip((1, size - 1, 2, size - 2), sources):
                    result = result + pltpu.roll(value, shift, axis)
            base[m, b] = result
            f = [fields[m, k + o] for o in (0, 1, 3, 4)]
            slope[m, b] = slope_scale * (8.0 * (f[2] - f[1]) - (f[3] - f[0]))
            if w is not None:
                g = [fields[m + 4, k + o] for o in (0, 1, 3, 4)]
                bend = 16.0 * (g[1] + g[2]) - (g[0] + g[3]) - 30.0 * w
                curve[m - 1, b] = (curve_scale * diffusivity[m - 1]) * bend
        return below + thick

    run[0] = lax.fori_loop(0, CHUNK, one_plane, run[0])


def final_kernel(
    place,
    base,
    slope,
    curve,
    norm,
    before,
    after,
    total_ref,
    dense,
    dense_1,
    dense_2,
    dense_3,
    bottom,
    thin,
    kinds,
    out,
    shift_out,
    pull,
):
    wall = place[0]
    step = pl.program_id(0)
    twelfth = time_step / 12.0
    row = iota((8, 512), 0)
    odd = row % 2 == 1
    total = total_ref[...]

    @pl.when(step == 0)
    def first():
        recess = dense[1] + dense_1[1] + dense_2[1] + dense_3[1]
        pull[0] = recess
        pull[1] = total / (total + recess)

    recess = pull[0]
    alpha = pull[1]
    edges = []
    for side, near_sign in ((before, 1.0), (after, -1.0)):
        u = [side[m, 0] for m in range(5)]
        inverse, vx, vy, vz, pressure = primitives(*u)
        flux = (u[1], u[1] * vx + pressure, u[1] * vy, u[1] * vz, (u[4] + pressure) * vx)
        smooth = (None, vx, vy, vz, pressure * inverse)
        results = []
        for m in range(5):
            near = (8.0 * twelfth * near_sign) * flux[m]
            far = (-twelfth * near_sign) * flux[m]
            if smooth[m] is not None:
                amount = twelfth * diffusivity[m - 1]
                near = near + (16.0 * amount) * smooth[m]
                far = far - amount * smooth[m]
            if near_sign > 0:
                moved = jnp.where(odd, 0.0, pltpu.roll(near, 7, 0))
            else:
                moved = jnp.where(odd, pltpu.roll(near, 1, 0), 0.0)
            results.append(far + moved)
        edges.append(results)
    for b in range(CHUNK):
        for m in range(5):
            value = slope[m, b]
            if m:
                value = value + alpha * curve[m - 1, b]
            value = base[m, b] + alpha * value
            low_edge = pltpu.roll(edges[0][m], (8 - 2 * b) % 8, 0) if b else edges[0][m]
            high_edge = pltpu.roll(edges[1][m], (6 - 2 * b) % 8, 0) if b != 3 else edges[1][m]
            value = value + jnp.where(row < 2, low_edge, jnp.where(row >= 6, high_edge, 0.0))
            out[m, b] = value
        shift_out[b] = recess * norm[b]

    @pl.when((step == 0) & (wall == 0))
    def ghosts():
        hot = dense[0] + dense_1[0] + dense_2[0] + dense_3[0]
        kind = kinds[...]
        cooled = 1.0 / hot
        ghost_flux = []
        ghost_smooth = []
        for layer in range(2):
            u = [bottom[m, layer] for m in range(5)]
            inverse, vx, vy, vz, pressure = primitives(*u)
            slip = kind == 1
            density = jnp.where(slip, u[0], pressure * cooled)
            gx = jnp.where(slip, vx, -vx)
            gy = jnp.where(slip, vy, -vy)
            gz = jnp.where(kind == 2, 2.0 * recess - vz, -vz)
            gas_temp = pressure / density
            heat = pressure * (1.0 / gas + 1.0) + 0.5 * density * (gx * gx + gy * gy + gz * gz)
            flow_z = density * gz
            ghost_flux.append((flow_z, flow_z * gx, flow_z * gy, flow_z * gz + pressure, heat * gz))
            ghost_smooth.append((gx, gy, gz, gas_temp))
        gap = [0.5 * (thin[k] + thin[k + 1]) for k in range(3)]
        stretch = (13.0 * gap[0] - gap[1], 7.0 * gap[1] + 6.0 * gap[0] - gap[2])
        for k in range(2):
            scale = alpha * (12.0 / stretch[k])
            for m in range(5):
                near = ghost_flux[0][m]
                if k == 0:
                    value = (-twelfth * scale) * (ghost_flux[1][m] - 8.0 * near)
                else:
                    value = (-twelfth * scale) * near
                if m:
                    close = ghost_smooth[0][m - 1]
                    bend = 16.0 * close - ghost_smooth[1][m - 1] if k == 0 else -close
                    value = value + (twelfth * diffusivity[m - 1]) * scale * scale * bend
                out[m, k] = out[m, k] + value


def whole(shape):
    return pl.BlockSpec(shape, lambda *_: (0,) * len(shape))


SCALARS = pl.BlockSpec(memory_space=pltpu.SMEM)


def params(limit=None):
    return pltpu.CompilerParams(vmem_limit_bytes=limit or 48 * 1024 * 1024)


def cost(flops, moved):
    return pl.CostEstimate(flops=flops, transcendentals=0, bytes_accessed=moved)


def struct(*shape, dtype=F32):
    return jax.ShapeDtypeStruct(shape, dtype)


def shards(flow_state, spacing, bc_kind, cell_of, zone_id, abl_temp, conduct, diffuse, rate):
    surf_count = lax.axis_size("surf")
    wall_count = lax.axis_size("wall")
    place = lax.axis_index("wall").astype(jnp.int32).reshape(1)
    cells = cell_of.reshape(1, 1024)
    zones = zone_id.reshape(1, 1024)

    def turn(value, axis, count, by):
        return lax.ppermute(value, axis, [(i, (i + by) % count) for i in range(count)])

    outgoing, rank = pl.pallas_call(
        route_kernel,
        out_shape=(struct(32, 128), struct(1, 1024, dtype=jnp.int32)),
        in_specs=[
            pl.BlockSpec((1, 1024), lambda i: (0, 0)),
            pl.BlockSpec((1, 1024), lambda i: (0, 0)),
            pl.BlockSpec((8, 1024), lambda i: (0, 0)),
        ],
        out_specs=(whole((32, 128)), whole((1, 1024))),
        grid=(1,),
        compiler_params=params(),
        cost_estimate=cost(4000000, 60000),
        name="route",
    )(cells, zones, abl_temp)
    next_side, prev_side, up_wall, down_wall, wall_fields = pl.pallas_call(
        pack_kernel,
        out_shape=(
            struct(5, 8, 8, 512),
            struct(5, 8, 8, 512),
            struct(15, 8, 512),
            struct(15, 8, 512),
            struct(3, 8, 512),
        ),
        compiler_params=params(),
        cost_estimate=cost(4000000, 5000000),
        name="pack",
    )(flow_state, spacing)
    arrived = lax.all_to_all(outgoing, "surf", split_axis=0, concat_axis=0, tiled=True)
    low = turn(up_wall, "wall", wall_count, 1)
    high = turn(down_wall, "wall", wall_count, wall_count - 1)
    opposite = turn(wall_fields, "wall", wall_count, 2)
    before = turn(next_side, "surf", surf_count, 1)
    after = turn(prev_side, "surf", surf_count, surf_count - 1)

    planes = lambda count: pl.BlockSpec((count, CHUNK, 8, 512), lambda i: (0, i, 0, 0))
    plane = pl.BlockSpec((CHUNK, 8, 512), lambda i: (i, 0, 0))
    base, slope, curve, norm, total = pl.pallas_call(
        stencil_kernel,
        out_shape=(
            struct(5, 32, 8, 512),
            struct(5, 32, 8, 512),
            struct(4, 32, 8, 512),
            struct(32, 8, 512),
            struct(8, 512),
        ),
        grid=(32 // CHUNK,),
        in_specs=[
            SCALARS,
            whole((5, 32, 8, 512)),
            whole((32, 8, 512)),
            whole((15, 8, 512)),
            whole((15, 8, 512)),
            whole((3, 8, 512)),
            whole((3, 8, 512)),
        ],
        out_specs=(planes(5), planes(5), planes(4), plane, whole((8, 512))),
        scratch_shapes=[
            pltpu.VMEM((10, 36, 8, 512), F32),
            pltpu.VMEM((35, 8, 512), F32),
            pltpu.VMEM((2, 8, 512), F32),
        ],
        compiler_params=params(),
        cost_estimate=cost(50000000, 11000000),
        name="stencil",
    )(place, flow_state, spacing, low, high, opposite, wall_fields)

    dense, where_cells = pl.pallas_call(
        surface_kernel,
        out_shape=(struct(2, 8, 512), struct(1, 1024)),
        in_specs=[SCALARS, SCALARS, SCALARS] + [pl.BlockSpec(memory_space=pltpu.VMEM)] * 5,
        compiler_params=params(),
        cost_estimate=cost(4000000, 600000),
        name="surface",
    )(place, conduct, rate, arrived, wall_fields, low, opposite, high)
    dense_1 = turn(dense, "wall", wall_count, 1)
    dense_2 = turn(dense, "wall", wall_count, 2)
    dense_3 = turn(dense, "wall", wall_count, 3)
    returned = pl.pallas_call(
        return_kernel,
        out_shape=struct(32, 128),
        compiler_params=params(),
        cost_estimate=cost(4000000, 60000),
        name="answer",
    )(where_cells, dense)
    back = lax.all_to_all(returned, "surf", split_axis=0, concat_axis=0, tiled=True)

    state_next, node_shift = pl.pallas_call(
        final_kernel,
        out_shape=(struct(5, 32, 8, 512), struct(32, 8, 512)),
        grid=(32 // CHUNK,),
        in_specs=[
            SCALARS,
            planes(5),
            planes(5),
            planes(4),
            plane,
            pl.BlockSpec((5, 1, 8, 512), lambda i: (0, i, 0, 0)),
            pl.BlockSpec((5, 1, 8, 512), lambda i: (0, i, 0, 0)),
            whole((8, 512)),
            whole((2, 8, 512)),
            whole((2, 8, 512)),
            whole((2, 8, 512)),
            whole((2, 8, 512)),
            whole((5, 4, 8, 512)),
            whole((4, 8, 512)),
            whole((8, 512)),
        ],
        out_specs=(planes(5), plane),
        scratch_shapes=[pltpu.VMEM((2, 8, 512), F32)],
        compiler_params=params(),
        cost_estimate=cost(20000000, 14000000),
        name="final",
    )(
        place,
        base,
        slope,
        curve,
        norm,
        before,
        after,
        total,
        dense,
        dense_1,
        dense_2,
        dense_3,
        flow_state,
        spacing,
        bc_kind,
    )
    ablator_next = pl.pallas_call(
        ablate_kernel,
        out_shape=struct(64, 1024),
        in_specs=[SCALARS] + [pl.BlockSpec(memory_space=pltpu.VMEM)] * 5,
        compiler_params=params(),
        cost_estimate=cost(4000000, 600000),
        name="ablate",
    )(diffuse, cells, rank, zones, back, abl_temp)
    return (state_next, node_shift, ablator_next)


def solution(mesh):
    in_specs = (
        P(None, "wall", "surf", None),
        P("wall", "surf", None),
        P("surf", None),
        P(("surf", "wall")),
        P(("surf", "wall")),
        P(None, ("surf", "wall")),
        P(),
        P(),
        P(),
    )
    out_specs = (P(None, "wall", "surf", None), P("wall", "surf", None), P(None, ("surf", "wall")))
    return jax.shard_map(shards, mesh=mesh, in_specs=in_specs, out_specs=out_specs, check_vma=False)
```

time: 338 us -> 75.1 us (0.22)
  the two profiles are of different devices: /device:TPU:1 before, /device:TPU:2 now
where the time goes in v1:
time: 75.1 us; the launch traced here: 74.4 us
  starting transfers between devices  32.8 us (44%)
  Pallas kernels  23.7 us (32%)
  local copies, waits for them, and re-layouts  9.96 us (13%)
  waiting for transfers between devices  7.12 us (9%)
  between operations  0.77 us (1%)
    ppermute x8, starting transfers between devices, turn(): lax.ppermute(value, axis, [(i, (i + by) % count) for i in range(count)])  15.2 us
    all_to_all x1, starting transfers between devices, shards(): lax.all_to_all(returned, 'surf', split_axis=0, concat_axis=0, tiled=True)  11.4 us
    unnamed x36, local copies, waits for them, and re-layouts  9.96 us
    pallas_call x1, Pallas kernels, shards(): pl.pallas_call(stencil_kernel, out_shape=(struct(5, 32, 8, 512), struct(5...  9.94 us
    pallas_call x1, Pallas kernels, shards(): pl.pallas_call(final_kernel, out_shape=(struct(5, 32, 8, 512), struct(32,...  7.45 us
    all_to_all x1, waiting for transfers between devices, shards(): lax.all_to_all(outgoing, 'surf', split_axis=0, concat_axis=0, tiled=True)  7.09 us
    all_to_all x1, starting transfers between devices, shards(): lax.all_to_all(outgoing, 'surf', split_axis=0, concat_axis=0, tiled=True)  6.17 us
    pallas_call x1, Pallas kernels, shards(): pl.pallas_call(pack_kernel, out_shape=(struct(5, 8, 8, 512), struct(5, 8,...  1.55 us
  transfers between devices with their start and end apart: 10, of which 1 were waited for; matrix products, arithmetic and copies ran while one was open for 0% of the time, Pallas kernels for 20%

profile of v1, /device:TPU:2, one launch (start us, length us, event | category | flops | bytes accessed | tf_op | source)
XLA Modules:
  0.0 74.4 jit_solution(7298056821552486389)
XLA Ops:
  0.6 1.7 %copy-done = f32[5,32,8,512]{3,2,1,0:T(8,128)S(1)} copy-done((f32[5,32,8,512]{3,2,1,0:T(8,128)S(1)}, f32[5,32,8,512]{3,2,1,0:T(8,128)}, u32[]{:S(2)}) %copy-start) | copy-done | bytes 2621464
  2.4 1.0 %copy-done.1 = f32[32,8,512]{2,1,0:T(8,128)S(1)} copy-done((f32[32,8,512]{2,1,0:T(8,128)S(1)}, f32[32,8,512]{2,1,0:T(8,128)}, u32[]{:S(2)}) %copy-start.1) | copy-done | bytes 524312
  3.4 1.5 %pack.1 = (f32[5,8,8,512]{3,2,1,0:T(8,128)}, f32[5,8,8,512]{3,2,1,0:T(8,128)}, f32[15,8,512]{2,1,0:T(8,128)S(1)}, f32[15,8,512]{2,1,0:T(8,128)S(1)}, f32[3,8,512]{2,1,0:T(8,128)S(1)}) custom-call(f32[5,32,8,512]{3,2,1,0:T(8,128)S(1)} %copy-done, f32[32,8,512]{2,1,0:T(8,128)S(1)} %copy-done.1), custom_call_target="tpu_custom_call" | custom-call | flops 4000000 | bytes 5000000 | tf_op jit(solution)/shard_map/pack/pallas_call | solution.py:484
  5.0 1.6 %collective-permute-start.3 = (f32[5,8,8,512]{3,2,1,0:T(8,128)}, f32[5,8,8,512]{3,2,1,0:T(8,128)}, u32[]{:S(2)}, u32[]{:S(2)}) collective-permute-start(f32[5,8,8,512]{3,2,1,0:T(8,128)} %get-tuple-element.26), channel_id=1, source_target_pairs={{0,4},{4,8},{8,12},{12,16},{16,20},{20,24},{24,28},{28,32},{32,36}... | collective-permute-start | bytes 1966088 | tf_op jit(solution)/shard_map/ppermute | solution.py:468
  6.6 2.6 %collective-permute-start.4 = (f32[5,8,8,512]{3,2,1,0:T(8,128)}, f32[5,8,8,512]{3,2,1,0:T(8,128)}, u32[]{:S(2)}, u32[]{:S(2)}) collective-permute-start(f32[5,8,8,512]{3,2,1,0:T(8,128)} %get-tuple-element.27), channel_id=1, source_target_pairs={{0,124},{4,0},{8,4},{12,8},{16,12},{20,16},{24,20},{28,24},{32,28}... | collective-permute-start | bytes 1966088 | tf_op jit(solution)/shard_map/ppermute | solution.py:468
  9.1 3.2 %collective-permute-start.1 = (f32[15,8,512]{2,1,0:T(8,128)S(1)}, f32[15,8,512]{2,1,0:T(8,128)S(1)}, u32[]{:S(2)}, u32[]{:S(2)}) collective-permute-start(f32[15,8,512]{2,1,0:T(8,128)S(1)} %get-tuple-element.20), channel_id=1, source_target_pairs={{0,3},{1,0},{2,1},{3,2},{4,7},{5,4},{6,5},{7,6},{8,11},{9,8},{10,9... | collective-permute-start | bytes 737288 | tf_op jit(solution)/shard_map/ppermute | solution.py:468
  12.4 3.9 %collective-permute-start.2 = (f32[3,8,512]{2,1,0:T(8,128)S(1)}, f32[3,8,512]{2,1,0:T(8,128)S(1)}, u32[]{:S(2)}, u32[]{:S(2)}) collective-permute-start(f32[3,8,512]{2,1,0:T(8,128)S(1)} %get-tuple-element.21.own), channel_id=1, source_target_pairs={{0,2},{1,3},{2,0},{3,1},{4,6},{5,7},{6,4},{7,5},{8,10},{9,11},{10,... | collective-permute-start | bytes 147464 | tf_op jit(solution)/shard_map/ppermute | solution.py:468
  16.3 1.1 %route.1 = (f32[32,128]{1,0:T(8,128)}, s32[1,1024]{1,0:T(1,128)S(1)}) custom-call(s32[1,1024]{1,0:T(1,128)S(1)} %bitcast.13, s32[1,1024]{1,0:T(1,128)S(1)} %bitcast.15, f32[64,1024]{1,0:T(8,128)S(1)} %copy-done.3), custom_call_target="tpu_custom_call" | custom-call | flops 4000000 | bytes 60000 | tf_op jit(solution)/shard_map/route/pallas_call | solution.py:470
  18.0 6.2 %all-to-all-start = ((f32[32,1,128]{2,1,0:T(1,128)}), f32[32,1,128]{2,1,0:T(1,128)S(1)}, u32[]{:S(2)}, u32[]{:S(2)}) async-start(f32[32,1,128]{2,1,0:T(1,128)} %bitcast.4), calls=%async_computation | async-start | bytes 32768 | tf_op jit(solution)/shard_map/all_to_all | solution.py:497
  24.2 7.1 %all-to-all-done = f32[32,1,128]{2,1,0:T(1,128)S(1)} async-done(((f32[32,1,128]{2,1,0:T(1,128)}), f32[32,1,128]{2,1,0:T(1,128)S(1)}, u32[]{:S(2)}, u32[]{:S(2)}) %all-to-all-start) | async-done | bytes 16416 | tf_op jit(solution)/shard_map/all_to_all | solution.py:497
  31.3 1.1 %surface.1 = (f32[2,8,512]{2,1,0:T(8,128)S(1)}, f32[1,1024]{1,0:T(1,128)S(1)}) custom-call(s32[1]{0:T(128)} %bitcast.place, f32[8]{0:T(128)S(1)} %copy-done.16, f32[8]{0:T(128)S(1)} %copy-done.17, f32[32,128]{1,0:T(8,128)S(1)} %bitcast.11, f32[3,8,512]{2,1,0:T(8,128)S(1)} %get-tuple-element.21.own, f32[15,8,512]{2,1,0:T(8,128)S(1)} %collective-permute-done.low, ...), custom_call_target="tpu_custom_call" | custom-call | flops 4000000 | bytes 600000 | tf_op jit(solution)/shard_map/surface/pallas_call | solution.py:536
  32.5 0.9 %collective-permute-start.6 = (f32[2,8,512]{2,1,0:T(8,128)S(1)}, f32[2,8,512]{2,1,0:T(8,128)}, u32[]{:S(2)}, u32[]{:S(2)}) collective-permute-start(f32[2,8,512]{2,1,0:T(8,128)S(1)} %get-tuple-element.30.dense), channel_id=1, source_target_pairs={{0,2},{1,3},{2,0},{3,1},{4,6},{5,7},{6,4},{7,5},{8,10},{9,11},{10,... | collective-permute-start | bytes 98312 | tf_op jit(solution)/shard_map/ppermute | solution.py:468
  33.5 2.9 %collective-permute-start.7 = (f32[2,8,512]{2,1,0:T(8,128)S(1)}, f32[2,8,512]{2,1,0:T(8,128)}, u32[]{:S(2)}, u32[]{:S(2)}) collective-permute-start(f32[2,8,512]{2,1,0:T(8,128)S(1)} %get-tuple-element.30.dense), channel_id=1, source_target_pairs={{0,3},{1,0},{2,1},{3,2},{4,7},{5,4},{6,5},{7,6},{8,11},{9,8},{10,9... | collective-permute-start | bytes 98312 | tf_op jit(solution)/shard_map/ppermute | solution.py:468
  36.3 1.0 %answer.1 = f32[32,128]{1,0:T(8,128)} custom-call(f32[1,1024]{1,0:T(1,128)S(1)} %get-tuple-element.34.where_in, f32[2,8,512]{2,1,0:T(8,128)S(1)} %get-tuple-element.30.dense), custom_call_target="tpu_custom_call" | custom-call | flops 4000000 | bytes 60000 | tf_op jit(solution)/shard_map/answer/pallas_call | solution.py:547
  37.4 11.4 %all-to-all-start.1 = ((f32[32,1,128]{2,1,0:T(1,128)}), f32[32,1,128]{2,1,0:T(1,128)S(1)}, u32[]{:S(2)}, u32[]{:S(2)}) async-start(f32[32,1,128]{2,1,0:T(1,128)} %bitcast.7), calls=%async_computation.1 | async-start | bytes 32768 | tf_op jit(solution)/shard_map/all_to_all | solution.py:554
  48.8 9.9 %stencil.1 = (f32[5,32,8,512]{3,2,1,0:T(8,128)}, f32[5,32,8,512]{3,2,1,0:T(8,128)}, f32[4,32,8,512]{3,2,1,0:T(8,128)S(1)}, f32[32,8,512]{2,1,0:T(8,128)S(1)}, f32[8,512]{1,0:T(8,128)S(1)}) custom-call(s32[1]{0:T(128)} %bitcast.place, f32[5,32,8,512]{3,2,1,0:T(8,128)} %bottom.1, f32[32,8,512]{2,1,0:T(8,128)S(1)} %copy-done.2, ...), custom_call_target="tpu_custom_call" | custom-call | flops 50000000 | bytes 11000000 | tf_op jit(solution)/shard_map/stencil/pallas_call | solution.py:506
  58.7 0.8 %copy-done.4 = f32[32,8,512]{2,1,0:T(8,128)} copy-done((f32[32,8,512]{2,1,0:T(8,128)}, f32[32,8,512]{2,1,0:T(8,128)S(1)}, u32[]{:S(2)}) %copy-start.4) | copy-done | bytes 524312
  60.1 0.7 copy-done.10
  60.8 0.7 copy-done.12
  62.8 1.5 %ablate.1 = f32[64,1024]{1,0:T(8,128)} custom-call(f32[8]{0:T(128)S(1)} %copy-done.15, s32[1,1024]{1,0:T(1,128)S(1)} %bitcast.14, s32[1,1024]{1,0:T(1,128)S(1)} %copy-done.14, s32[1,1024]{1,0:T(1,128)S(1)} %bitcast.16, f32[32,128]{1,0:T(8,128)S(1)} %bitcast.12, f32[64,1024]{1,0:T(8,128)S(1)} %copy-done.3), custom_call_target="tpu_custom_call" | custom-call | flops 4000000 | bytes 600000 | tf_op jit(solution)/shard_map/ablate/pallas_call | solution.py:599
  64.4 1.0 %copy-done.5 = f32[32,8,512]{2,1,0:T(8,128)S(1)} copy-done((f32[32,8,512]{2,1,0:T(8,128)S(1)}, f32[32,8,512]{2,1,0:T(8,128)}, u32[]{:S(2)}) %copy-start.5) | copy-done | bytes 524312
  65.5 0.7 copy-done.6
  66.2 0.7 copy-done.8
  66.9 7.4 %final.1 = (f32[5,32,8,512]{3,2,1,0:T(8,128)}, f32[32,8,512]{2,1,0:T(8,128)}) custom-call(s32[1]{0:T(128)} %bitcast.place, f32[5,32,8,512]{3,2,1,0:T(8,128)} %get-tuple-element.22.base, f32[5,32,8,512]{3,2,1,0:T(8,128)} %get-tuple-element.23.slope, f32[4,32,8,512]{3,2,1,0:T(8,128)S(1)} %get-tuple-element.24.curve, f32[32,8,512]{2,1,0:T(8,128)S(1)} %copy-done.5, ...), custom_call_target="tpu_custom_call" | custom-call | flops 20000000 | bytes 14000000 | tf_op jit(solution)/shard_map/final/pallas_call | solution.py:556
  (39 shorter events, 2.7 us)
Async XLA Ops:
  0.6 1.7 %copy-start = (f32[5,32,8,512]{3,2,1,0:T(8,128)S(1)}, f32[5,32,8,512]{3,2,1,0:T(8,128)}, u32[]{:S(2)}) copy-start(f32[5,32,8,512]{3,2,1,0:T(8,128)} %bottom.1) | copy-start | bytes 7864324
  2.4 1.0 %copy-start.1 = (f32[32,8,512]{2,1,0:T(8,128)S(1)}, f32[32,8,512]{2,1,0:T(8,128)}, u32[]{:S(2)}) copy-start(f32[32,8,512]{2,1,0:T(8,128)} %thin.1) | copy-start | bytes 1572868
  3.4 12.8 %copy-start.3 = (f32[64,1024]{1,0:T(8,128)S(1)}, f32[64,1024]{1,0:T(8,128)}, u32[]{:S(2)}) copy-start(f32[64,1024]{1,0:T(8,128)} %temps.3) | copy-start | bytes 786436
  3.4 12.8 %copy-start.9 = (s32[1024]{0:T(1024)S(1)}, s32[1024]{0:T(1024)}, u32[]{:S(2)}) copy-start(s32[1024]{0:T(1024)} %param.12) | copy-start | bytes 12292
  3.4 12.8 %copy-start.11 = (s32[1024]{0:T(1024)S(1)}, s32[1024]{0:T(1024)}, u32[]{:S(2)}) copy-start(s32[1024]{0:T(1024)} %param.13) | copy-start | bytes 12292
  3.4 27.8 %copy-start.16 = (f32[8]{0:T(128)S(1)}, f32[8]{0:T(128)}, u32[]{:S(2)}) copy-start(f32[8]{0:T(128)} %conduct.1) | copy-start | bytes 100
  3.4 27.9 %copy-start.17 = (f32[8]{0:T(128)S(1)}, f32[8]{0:T(128)}, u32[]{:S(2)}) copy-start(f32[8]{0:T(128)} %rate.1) | copy-start | bytes 100
  3.4 45.4 %copy-start.2 = (f32[32,8,512]{2,1,0:T(8,128)S(1)}, f32[32,8,512]{2,1,0:T(8,128)}, u32[]{:S(2)}) copy-start(f32[32,8,512]{2,1,0:T(8,128)} %thin.1) | copy-start | bytes 1572868
  5.0 59.4 %collective-permute-start.3 = (f32[5,8,8,512]{3,2,1,0:T(8,128)}, f32[5,8,8,512]{3,2,1,0:T(8,128)}, u32[]{:S(2)}, u32[]{:S(2)}) collective-permute-start(f32[5,8,8,512]{3,2,1,0:T(8,128)} %get-tuple-element.26), channel_id=1, source_target_pairs={{0,4},{4,8},{8,12},{12,16},{16,20},{20,24},{24,28},{28,32},{32,36}... | collective-permute-start | bytes 1966088 | tf_op jit(solution)/shard_map/ppermute | solution.py:468
  6.6 57.8 %collective-permute-start.4 = (f32[5,8,8,512]{3,2,1,0:T(8,128)}, f32[5,8,8,512]{3,2,1,0:T(8,128)}, u32[]{:S(2)}, u32[]{:S(2)}) collective-permute-start(f32[5,8,8,512]{3,2,1,0:T(8,128)} %get-tuple-element.27), channel_id=1, source_target_pairs={{0,124},{4,0},{8,4},{12,8},{16,12},{20,16},{24,20},{28,24},{32,28}... | collective-permute-start | bytes 1966088 | tf_op jit(solution)/shard_map/ppermute | solution.py:468
  9.1 22.1 %collective-permute-start = (f32[15,8,512]{2,1,0:T(8,128)S(1)}, f32[15,8,512]{2,1,0:T(8,128)S(1)}, u32[]{:S(2)}, u32[]{:S(2)}) collective-permute-start(f32[15,8,512]{2,1,0:T(8,128)S(1)} %get-tuple-element.19), channel_id=1, source_target_pairs={{0,1},{1,2},{2,3},{3,0},{4,5},{5,6},{6,7},{7,4},{8,9},{9,10},{10,1... | collective-permute-start | bytes 737288 | tf_op jit(solution)/shard_map/ppermute | solution.py:468
  9.1 22.1 %collective-permute-start.1 = (f32[15,8,512]{2,1,0:T(8,128)S(1)}, f32[15,8,512]{2,1,0:T(8,128)S(1)}, u32[]{:S(2)}, u32[]{:S(2)}) collective-permute-start(f32[15,8,512]{2,1,0:T(8,128)S(1)} %get-tuple-element.20), channel_id=1, source_target_pairs={{0,3},{1,0},{2,1},{3,2},{4,7},{5,4},{6,5},{7,6},{8,11},{9,8},{10,9... | collective-permute-start | bytes 737288 | tf_op jit(solution)/shard_map/ppermute | solution.py:468
  12.4 18.9 %collective-permute-start.2 = (f32[3,8,512]{2,1,0:T(8,128)S(1)}, f32[3,8,512]{2,1,0:T(8,128)S(1)}, u32[]{:S(2)}, u32[]{:S(2)}) collective-permute-start(f32[3,8,512]{2,1,0:T(8,128)S(1)} %get-tuple-element.21.own), channel_id=1, source_target_pairs={{0,2},{1,3},{2,0},{3,1},{4,6},{5,7},{6,4},{7,5},{8,10},{9,11},{10,... | collective-permute-start | bytes 147464 | tf_op jit(solution)/shard_map/ppermute | solution.py:468
  18.0 13.3 %all-to-all-start = ((f32[32,1,128]{2,1,0:T(1,128)}), f32[32,1,128]{2,1,0:T(1,128)S(1)}, u32[]{:S(2)}, u32[]{:S(2)}) async-start(f32[32,1,128]{2,1,0:T(1,128)} %bitcast.4), calls=%async_computation | async-start | bytes 32768 | tf_op jit(solution)/shard_map/all_to_all | solution.py:497
  32.4 32.0 %collective-permute-start.5 = (f32[2,8,512]{2,1,0:T(8,128)S(1)}, f32[2,8,512]{2,1,0:T(8,128)S(1)}, u32[]{:S(2)}, u32[]{:S(2)}) collective-permute-start(f32[2,8,512]{2,1,0:T(8,128)S(1)} %get-tuple-element.30.dense), channel_id=1, source_target_pairs={{0,1},{1,2},{2,3},{3,0},{4,5},{5,6},{6,7},{7,4},{8,9},{9,10},{10,1... | collective-permute-start | bytes 98312 | tf_op jit(solution)/shard_map/ppermute | solution.py:468
  32.5 31.9 %collective-permute-start.6 = (f32[2,8,512]{2,1,0:T(8,128)S(1)}, f32[2,8,512]{2,1,0:T(8,128)}, u32[]{:S(2)}, u32[]{:S(2)}) collective-permute-start(f32[2,8,512]{2,1,0:T(8,128)S(1)} %get-tuple-element.30.dense), channel_id=1, source_target_pairs={{0,2},{1,3},{2,0},{3,1},{4,6},{5,7},{6,4},{7,5},{8,10},{9,11},{10,... | collective-permute-start | bytes 98312 | tf_op jit(solution)/shard_map/ppermute | solution.py:468
  33.5 30.9 %collective-permute-start.7 = (f32[2,8,512]{2,1,0:T(8,128)S(1)}, f32[2,8,512]{2,1,0:T(8,128)}, u32[]{:S(2)}, u32[]{:S(2)}) collective-permute-start(f32[2,8,512]{2,1,0:T(8,128)S(1)} %get-tuple-element.30.dense), channel_id=1, source_target_pairs={{0,3},{1,0},{2,1},{3,2},{4,7},{5,4},{6,5},{7,6},{8,11},{9,8},{10,9... | collective-permute-start | bytes 98312 | tf_op jit(solution)/shard_map/ppermute | solution.py:468
  37.4 22.8 %all-to-all-start.1 = ((f32[32,1,128]{2,1,0:T(1,128)}), f32[32,1,128]{2,1,0:T(1,128)S(1)}, u32[]{:S(2)}, u32[]{:S(2)}) async-start(f32[32,1,128]{2,1,0:T(1,128)} %bitcast.7), calls=%async_computation.1 | async-start | bytes 32768 | tf_op jit(solution)/shard_map/all_to_all | solution.py:554
  58.7 0.8 %copy-start.4 = (f32[32,8,512]{2,1,0:T(8,128)}, f32[32,8,512]{2,1,0:T(8,128)S(1)}, u32[]{:S(2)}) copy-start(f32[32,8,512]{2,1,0:T(8,128)S(1)} %get-tuple-element.25.norm) | copy-start | bytes 1572868
  60.1 0.7 copy-start.10
  60.8 0.7 copy-start.12
  64.4 1.0 %copy-start.5 = (f32[32,8,512]{2,1,0:T(8,128)S(1)}, f32[32,8,512]{2,1,0:T(8,128)}, u32[]{:S(2)}) copy-start(f32[32,8,512]{2,1,0:T(8,128)} %copy-done.4) | copy-start | bytes 1572868
  65.5 0.7 copy-start.6
  66.2 0.7 copy-start.8
  (4 other events, 2.5 us)

commit v2 on v1

v2 whole, which is shorter than its diff:
```python
import functools
import jax
import jax.numpy as jnp
from jax import lax
from jax.experimental import pallas as pl
from jax.experimental.pallas import tpu as pltpu
from jax.sharding import PartitionSpec as P

gas = 0.4
time_step = 0.15
viscosity = 0.05
conduction = 0.07
sponge_rate = 0.5
activation = 2.0
radiation = 0.8
recovery = 0.2
far_values = (1.0, 0.5, 0.0, 0.0, 2.625)
diffusivity = (viscosity, viscosity, viscosity, conduction)

F32 = jnp.float32
BF16 = jnp.bfloat16


def iota(shape, axis):
    return lax.broadcasted_iota(jnp.int32, shape, axis)


def split3(x):
    high = x.astype(BF16)
    rest = x - high.astype(F32)
    middle = rest.astype(BF16)
    low = (rest - middle.astype(F32)).astype(BF16)
    return high, middle, low


def dot_nn(a, b):
    return lax.dot_general(a, b, (((1,), (0,)), ((), ())), preferred_element_type=F32)


def dot_nt(a, b):
    return lax.dot_general(a, b, (((1,), (1,)), ((), ())), preferred_element_type=F32)


def join3(x, rows):
    return x[:rows] + x[rows : 2 * rows] + x[2 * rows :]


def to_rows(x):
    return jnp.concatenate([x[:, 128 * c : 128 * c + 128] for c in range(4)], axis=0)


def to_grid(x):
    return jnp.concatenate([x[8 * c : 8 * c + 8] for c in range(4)], axis=1)


def onehot(mask):
    return jnp.where(mask, 1.0, 0.0).astype(BF16)


def primitives(u0, u1, u2, u3, u4):
    inverse = 1.0 / u0
    vx = u1 * inverse
    vy = u2 * inverse
    vz = u3 * inverse
    pressure = gas * (u4 - 0.5 * (u1 * vx + u2 * vy + u3 * vz))
    return inverse, vx, vy, vz, pressure


def start_all(copies):
    for copy in copies:
        copy.start()


def wait_all(copies):
    for copy in copies:
        copy.wait()


def pack_kernel(token, flow_hbm, next_hbm, prev_hbm, flow, next_side, prev_side, in_sem, out_sem):
    loads = [
        pltpu.make_async_copy(flow_hbm.at[:, pl.ds(8 * c, 8)], flow.at[:, pl.ds(8 * c, 8)], in_sem.at[c])
        for c in range(4)
    ]
    start_all(loads)
    row = iota((8, 512), 0) // 2
    stores = []
    for c in range(4):
        loads[c].wait()

        def field(m, carry, c=c):
            for block in (2 * c, 2 * c + 1):
                high = jnp.zeros((8, 512), F32)
                low = jnp.zeros((8, 512), F32)
                for b in range(4):
                    plane = flow[m, block * 4 + b]
                    rolled_high = pltpu.roll(plane, (2 * b + 2) % 8, 0) if b != 3 else plane
                    rolled_low = pltpu.roll(plane, 2 * b, 0) if b else plane
                    high = jnp.where(row == b, rolled_high, high)
                    low = jnp.where(row == b, rolled_low, low)
                next_side[m, block] = high
                prev_side[m, block] = low
            return carry

        lax.fori_loop(0, 5, field, 0)
        part = pl.ds(2 * c, 2)
        for side, (here, there) in enumerate(((next_side, next_hbm), (prev_side, prev_hbm))):
            copy = pltpu.make_async_copy(here.at[:, part], there.at[:, part], out_sem.at[side, c])
            copy.start()
            stores.append(copy)
    wait_all(stores)


def route_kernel(cell, zone, temps, outgoing, rank_out):
    cells = cell[...]
    tile = cells // 4096
    within = cells - tile * 4096
    hit = iota((32, 1024), 0) == tile
    ones = jnp.where(hit, 1.0, 0.0)
    stacked = jnp.concatenate([ones[:, 128 * k : 128 * k + 128] for k in range(8)], axis=0)
    inner = iota((128, 256), 0)
    outer = iota((128, 256), 1)
    ahead = onehot((inner < outer) | (outer >= 128))
    counts = dot_nn(stacked.astype(BF16), ahead)
    offset = jnp.zeros((32, 128), F32)
    ranks = []
    for k in range(8):
        part = slice(32 * k, 32 * k + 32)
        place = counts[part, :128] + offset
        ranks.append(jnp.sum(stacked[part] * place, axis=0, keepdims=True))
        offset = offset + counts[part, 128:]
    rank = jnp.concatenate(ranks, axis=1).astype(jnp.int32)
    rank_out[...] = rank
    slot = iota((32, 1024), 0) == rank
    first, second = temps[0:1], temps[1:2]
    fields = (within.astype(F32), (zone[...] + 1).astype(F32), first, second)
    pieces = [split3(value) for value in fields]
    rows = []
    for level in range(3):
        for piece in pieces:
            rows.append(jnp.where(slot, piece[level].astype(F32), 0.0).astype(BF16))
    sent = dot_nt(ones.astype(BF16), jnp.concatenate(rows, axis=0))
    outgoing[...] = sent[:, :128] + sent[:, 128:256] + sent[:, 256:]


def scatter_kernel(
    token, arrived, flow_low, flow_high, spacing, up_wall, down_wall, wall_fields, where_out
):
    for m in range(5):
        for layer in range(2):
            up_wall[2 * m + layer] = flow_high[m, layer]
            down_wall[2 * m + layer] = flow_low[m, layer]
    for layer in range(2):
        up_wall[10 + layer] = spacing[30 + layer]
        down_wall[10 + layer] = spacing[layer]
    inverse, vx, vy, vz, pressure = primitives(*[flow_low[m, 0] for m in range(5)])
    film = 2.0 / spacing[0]
    temp = pressure * inverse + recovery * (vx * vx + vy * vy + vz * vz)
    total = spacing[0]
    for k in range(1, 32):
        total = total + spacing[k]
    received = arrived[...]
    pieces = jnp.concatenate(split3(received), axis=0)
    lane = iota((128, 1024), 1) % 32
    line = iota((128, 1024), 0)
    source = iota((32, 1024), 0) == iota((32, 1024), 1) // 32
    flat = []
    for f in range(4):
        spread = join3(dot_nn(pieces, onehot(line == lane + 32 * f)), 32)
        flat.append(jnp.sum(jnp.where(source, spread, 0.0), axis=0, keepdims=True))
    where_out[...] = flat[0]
    cells = flat[0].astype(jnp.int32)
    block = ((cells % 512) // 128) * 8 + cells // 512
    block_hit = iota((32, 1024), 0) == block
    lane_hit = onehot(line == cells % 128)
    rows = [jnp.where(block_hit, flat[1], 0.0).astype(BF16)]
    for value in flat[2:]:
        for piece in split3(value):
            rows.append(jnp.where(block_hit, piece.astype(F32), 0.0).astype(BF16))
    grid = dot_nt(jnp.concatenate(rows, axis=0), lane_hit)
    zones = to_grid(grid[:32])
    first = to_grid(join3(grid[32:128], 32))
    inner = to_grid(join3(grid[128:], 32))
    for index, value in enumerate((film, temp, total, zones, first, inner)):
        up_wall[12 + index] = value
        down_wall[12 + index] = value
        wall_fields[index] = value


def surface_kernel(
    place, conduct, rate, token, where_in, own, low, opposite, high, surface_out, outgoing
):
    wall = place[0]

    def from_bottom(f):
        return jnp.where(
            wall == 0,
            own[f],
            jnp.where(wall == 1, low[12 + f], jnp.where(wall == 2, opposite[f], high[12 + f])),
        )

    def everywhere(f):
        return (own[f] + low[12 + f]) + (opposite[f] + high[12 + f])

    film = from_bottom(0)
    recover = from_bottom(1)
    below = jnp.where(wall >= 1, low[14], 0.0)
    below = below + jnp.where(wall >= 2, opposite[2], 0.0)
    below = below + jnp.where(wall >= 3, high[14], 0.0)
    zones = everywhere(3)
    surface = everywhere(4)
    inner = everywhere(5)
    cond = jnp.zeros((8, 512), F32)
    speed = jnp.zeros((8, 512), F32)
    for z in range(8):
        cond = jnp.where(zones == z + 1.0, conduct[z], cond)
        speed = jnp.where(zones == z + 1.0, rate[z], speed)
    base = film * recover + cond * inner
    for step in range(2):
        cube = surface * surface * surface
        surface = (base + 3.0 * radiation * cube * surface) / (film + cond + 4.0 * radiation * cube)
    surface_out[0] = surface
    surface_out[1] = speed * jnp.exp(-activation / surface)
    surface_out[2] = everywhere(2)
    surface_out[3] = below
    cells = where_in[...].astype(jnp.int32)
    block = ((cells % 512) // 128) * 8 + cells // 512
    block_hit = iota((32, 1024), 0) == block
    line = iota((128, 1024), 0)
    lane_hit = onehot(line == cells % 128)
    pieces = jnp.concatenate(split3(to_rows(surface)), axis=0)
    spread = join3(dot_nn(pieces, lane_hit), 32)
    flat = jnp.sum(jnp.where(block_hit, spread, 0.0), axis=0, keepdims=True)
    source = iota((32, 1024), 0) == iota((32, 1024), 1) // 32
    rows = [jnp.where(source, piece.astype(F32), 0.0).astype(BF16) for piece in split3(flat)]
    slot = onehot(line == iota((128, 1024), 1) % 32)
    outgoing[...] = join3(dot_nt(jnp.concatenate(rows, axis=0), slot), 32)


def ablate_kernel(diffuse, token, cell, rank, zone, back, temps, out):
    pieces = jnp.concatenate(split3(back[...]), axis=0)
    slot = onehot(iota((128, 1024), 0) == rank[...])
    spread = join3(dot_nn(pieces, slot), 32)
    tile_hit = iota((32, 1024), 0) == cell[...] // 4096
    surface = jnp.sum(jnp.where(tile_hit, spread, 0.0), axis=0, keepdims=True)
    zones = zone[...]
    spread_rate = jnp.zeros((1, 1024), F32)
    for z in range(8):
        spread_rate = jnp.where(zones == z, diffuse[z], spread_rate)
    row = iota((64, 1024), 0)
    profile = jnp.where(row == 0, surface, temps[...])
    for step in range(2):
        before = pltpu.roll(profile, 1, 0)
        after = pltpu.roll(profile, 63, 0)
        after = jnp.where(row == 63, before, after)
        changed = profile + spread_rate * (after - 2.0 * profile + before)
        profile = jnp.where(row == 0, profile, changed)
    out[...] = profile


def chunk_of(ref, c):
    return ref.at[:, pl.ds(8 * c, 8)]


TWELFTH = time_step / 12.0


def side_kernel(flow_hbm, base_hbm, flow, base, in_sem, out_sem):
    loads = [
        pltpu.make_async_copy(chunk_of(flow_hbm, c), chunk_of(flow, c), in_sem.at[c]) for c in range(4)
    ]
    start_all(loads)
    row = iota((8, 512), 0)
    limits = (row != 7, row != 0, row < 6, row >= 2)

    def one_plane(k, carry):
        u = [flow[m, k] for m in range(5)]
        inverse, vx, vy, vz, pressure = primitives(*u)
        temp = pressure * inverse
        heat = u[4] + pressure
        shear = u[1] * vy
        flux_i = (u[1], u[1] * vx + pressure, shear, u[1] * vz, heat * vx)
        flux_j = (u[2], shear, u[2] * vy + pressure, u[2] * vz, heat * vy)
        smooth = (None, vx, vy, vz, temp)
        for m in range(5):
            result = u[m]
            w = smooth[m]
            if w is not None:
                amount = TWELFTH * diffusivity[m - 1]
                w16 = (16.0 * amount) * w
                w1 = amount * w
                result = result - (60.0 * amount) * w
            for axis, flux in ((0, flux_i[m]), (1, flux_j[m])):
                near = (8.0 * TWELFTH) * flux
                far = TWELFTH * flux
                if w is None:
                    sources = (near, -near, -far, far)
                else:
                    sources = (w16 + near, w16 - near, -w1 - far, far - w1)
                if axis == 0:
                    sources = [jnp.where(limit, value, 0.0) for limit, value in zip(limits, sources)]
                size = (8, 512)[axis]
                for shift, value in zip((1, size - 1, 2, size - 2), sources):
                    result = result + pltpu.roll(value, shift, axis)
            base[m, k] = result
        return carry

    stores = []
    for c in range(4):
        loads[c].wait()
        lax.fori_loop(8 * c, 8 * c + 8, one_plane, 0)
        copy = pltpu.make_async_copy(chunk_of(base, c), chunk_of(base_hbm, c), out_sem.at[c])
        copy.start()
        stores.append(copy)
    wait_all(stores)


def normal_flux(u3, density_x, density_y, vx, vy, vz, pressure, heat):
    return (u3, density_x * vz, density_y * vz, u3 * vz + pressure, heat * vz)


def normal_kernel(
    token, flow_hbm, slope_hbm, curve_hbm, flow, fields, slope, curve, in_sem, out_sem
):
    loads = [
        pltpu.make_async_copy(chunk_of(flow_hbm, c), chunk_of(flow, c), in_sem.at[c]) for c in range(4)
    ]
    start_all(loads)
    for f in range(9):
        for edge in (0, 1, 34, 35):
            fields[f, edge] = jnp.zeros((8, 512), F32)

    def one_field(k, carry):
        u = [flow[m, k] for m in range(5)]
        inverse, vx, vy, vz, pressure = primitives(*u)
        values = normal_flux(u[3], u[1], u[2], vx, vy, vz, pressure, u[4] + pressure)
        for index, value in enumerate(values + (vx, vy, vz, pressure * inverse)):
            fields[index, k + 2] = value
        return carry

    def one_plane(k, carry):
        for m in range(5):
            f = [fields[m, k + o] for o in (0, 1, 3, 4)]
            slope[m, k] = 8.0 * (f[2] - f[1]) - (f[3] - f[0])
        for m in range(4):
            g = [fields[m + 5, k + o] for o in range(5)]
            curve[m, k] = 16.0 * (g[1] + g[3]) - (g[0] + g[4]) - 30.0 * g[2]
        return carry

    stores = []
    for c in range(4):
        loads[c].wait()
        lax.fori_loop(8 * c, 8 * c + 8, one_field, 0)
        first = 8 * c - 2 if c else 0
        last = 8 * c + 6 if c < 3 else 32
        lax.fori_loop(first, last, one_plane, 0)
        if c:
            for index, (here, there) in enumerate(((slope, slope_hbm), (curve, curve_hbm))):
                copy = pltpu.make_async_copy(
                    chunk_of(here, c - 1), chunk_of(there, c - 1), out_sem.at[index, c - 1]
                )
                copy.start()
                stores.append(copy)
    for index, (here, there) in enumerate(((slope, slope_hbm), (curve, curve_hbm))):
        copy = pltpu.make_async_copy(chunk_of(here, 3), chunk_of(there, 3), out_sem.at[index, 3])
        copy.start()
        stores.append(copy)
    wait_all(stores)


def final_kernel(
    place,
    surface_hbm,
    low_hbm,
    high_hbm,
    kinds_hbm,
    spacing_hbm,
    flow_hbm,
    base_hbm,
    slope_hbm,
    curve_hbm,
    before_hbm,
    after_hbm,
    out_hbm,
    shift_hbm,
    surface,
    low,
    high,
    kinds,
    thick,
    flow,
    base,
    slope,
    curve,
    before,
    after,
    edges,
    run,
    shift,
    small_sem,
    in_sem,
    side_sem,
    out_sem,
    shift_sem,
):
    wall = place[0]
    small = [
        pltpu.make_async_copy(source, target, small_sem.at[index])
        for index, (source, target) in enumerate(
            (
                (surface_hbm, surface),
                (low_hbm.at[pl.ds(0, 12)], low),
                (high_hbm.at[pl.ds(0, 12)], high),
                (kinds_hbm, kinds),
                (spacing_hbm, thick.at[pl.ds(2, 32)]),
            )
        )
    ]
    start_all(small)
    loads = []
    for c in range(4):
        part = [
            pltpu.make_async_copy(chunk_of(source, c), chunk_of(target, c), in_sem.at[index, c])
            for index, (source, target) in enumerate(
                ((flow_hbm, flow), (slope_hbm, slope), (curve_hbm, curve), (base_hbm, base))
            )
        ]
        for index, (source, target) in enumerate(((before_hbm, before), (after_hbm, after))):
            part.append(
                pltpu.make_async_copy(
                    source.at[:, pl.ds(2 * c, 2)], target.at[:, pl.ds(2 * c, 2)], side_sem.at[index, c]
                )
            )
        start_all(part)
        loads.append(part)
    row = iota((8, 512), 0)
    odd = row % 2 == 1
    wait_all(small)
    is_low = wall == 0
    is_high = wall == 3
    hot = surface[0]
    recess = surface[1]
    total = surface[2]
    alpha = total / (total + recess)
    inverse_total = 1.0 / total
    run[0] = surface[3]
    run[1] = alpha
    run[2] = inverse_total
    thick[0] = jnp.where(is_low, thick[2], low[10])
    thick[1] = jnp.where(is_low, thick[3], low[11])
    thick[34] = jnp.where(is_high, thick[32], high[10])
    thick[35] = jnp.where(is_high, thick[33], high[11])

    def add_edges(near, far, direction, planes):
        near_flux, near_smooth = near
        far_flux, far_smooth = far
        for m in range(5):
            slope[m, planes[0]] += direction * (8.0 * near_flux[m] - far_flux[m])
            slope[m, planes[1]] += direction * (-near_flux[m])
        for m in range(4):
            curve[m, planes[0]] += 16.0 * near_smooth[m] - far_smooth[m]
            curve[m, planes[1]] += -near_smooth[m]

    def low_side():
        kind = kinds[...]
        cooled = 1.0 / hot
        slip = is_low & (kind == 1)
        blow = is_low & (kind == 2)
        sign = jnp.where(is_low, -1.0, 1.0)
        sides = []
        for layer in range(2):
            u = [jnp.where(is_low, flow[m, layer], low[2 * m + 1 - layer]) for m in range(5)]
            inverse, vx, vy, vz, pressure = primitives(*u)
            density = jnp.where(slip | jnp.logical_not(is_low), u[0], pressure * cooled)
            gx = jnp.where(slip, vx, sign * vx)
            gy = jnp.where(slip, vy, sign * vy)
            gz = jnp.where(blow, 2.0 * recess, 0.0) + sign * vz
            heat = pressure * (1.0 / gas + 1.0) + 0.5 * density * (gx * gx + gy * gy + gz * gz)
            flux = normal_flux(density * gz, density * gx, density * gy, gx, gy, gz, pressure, heat)
            sides.append((flux, (gx, gy, gz, pressure / density)))
        add_edges(sides[0], sides[1], -1.0, (0, 1))

    def high_side():
        sides = []
        for layer in range(2):
            u = [jnp.where(is_high, far_values[m], high[2 * m + layer]) for m in range(5)]
            inverse, vx, vy, vz, pressure = primitives(*u)
            flux = normal_flux(u[3], u[1], u[2], vx, vy, vz, pressure, u[4] + pressure)
            sides.append((flux, (vx, vy, vz, pressure * inverse)))
        add_edges(sides[0], sides[1], 1.0, (31, 30))

    def one_block(block, carry):
        for side, (source, near_sign) in enumerate(((before, 1.0), (after, -1.0))):
            u = [source[m, block] for m in range(5)]
            inverse, vx, vy, vz, pressure = primitives(*u)
            flux = (u[1], u[1] * vx + pressure, u[1] * vy, u[1] * vz, (u[4] + pressure) * vx)
            smooth = (None, vx, vy, vz, pressure * inverse)
            for m in range(5):
                near = (8.0 * TWELFTH * near_sign) * flux[m]
                far = (-TWELFTH * near_sign) * flux[m]
                if smooth[m] is not None:
                    amount = TWELFTH * diffusivity[m - 1]
                    near = near + (16.0 * amount) * smooth[m]
                    far = far - amount * smooth[m]
                if near_sign > 0:
                    moved = jnp.where(odd, 0.0, pltpu.roll(near, 7, 0))
                else:
                    moved = jnp.where(odd, pltpu.roll(near, 1, 0), 0.0)
                edges[side, m] = far + moved
        for b in range(4):
            k = block * 4 + b
            width = thick[k + 2]
            center = run[0] + 0.5 * width
            run[0] = run[0] + width
            normal = center * run[2]
            shift[k] = surface[1] * (normal - 1.0)
            stretch = 7.0 * width + 3.0 * (thick[k + 1] + thick[k + 3]) - 0.5 * (thick[k] + thick[k + 4])
            factor = run[1] * (12.0 / stretch)
            damp = (time_step * sponge_rate) * (normal * normal)
            slope_scale = -TWELFTH * factor
            curve_scale = TWELFTH * (factor * factor)
            for m in range(5):
                value = base[m, k] + slope_scale * slope[m, k] - damp * (flow[m, k] - far_values[m])
                if m:
                    value = value + (curve_scale * diffusivity[m - 1]) * curve[m - 1, k]
                low_edge = pltpu.roll(edges[0, m], 8 - 2 * b, 0) if b else edges[0, m]
                high_edge = pltpu.roll(edges[1, m], (6 - 2 * b) % 8, 0) if b != 3 else edges[1, m]
                base[m, k] = value + jnp.where(row < 2, low_edge, jnp.where(row >= 6, high_edge, 0.0))
        return carry

    stores = []
    for c in range(4):
        wait_all(loads[c])
        if c == 0:
            low_side()
        if c == 3:
            high_side()
        lax.fori_loop(2 * c, 2 * c + 2, one_block, 0)
        for copy in (
            pltpu.make_async_copy(chunk_of(base, c), chunk_of(out_hbm, c), out_sem.at[c]),
            pltpu.make_async_copy(
                shift.at[pl.ds(8 * c, 8)], shift_hbm.at[pl.ds(8 * c, 8)], shift_sem.at[c]
            ),
        ):
            copy.start()
            stores.append(copy)
    wait_all(stores)


def whole(shape):
    return pl.BlockSpec(shape, lambda *_: (0,) * len(shape))


SCALARS = pl.BlockSpec(memory_space=pltpu.SMEM)
ANY = pl.BlockSpec(memory_space=pl.ANY)
VMEM = pl.BlockSpec(memory_space=pltpu.VMEM)


def params():
    return pltpu.CompilerParams(vmem_limit_bytes=63 * 1024 * 1024)


def cost():
    return pl.CostEstimate(flops=1000, transcendentals=0, bytes_accessed=1000)


def struct(*shape, dtype=F32):
    return jax.ShapeDtypeStruct(shape, dtype)


def call(kernel, name, out_shape, **options):
    return pl.pallas_call(
        kernel, out_shape=out_shape, name=name, compiler_params=params(), cost_estimate=cost(), **options
    )


def scratch(*shape):
    return pltpu.VMEM(shape, F32)


def copies(*shape):
    return pltpu.SemaphoreType.DMA(shape)


def shards(flow_state, spacing, bc_kind, cell_of, zone_id, abl_temp, conduct, diffuse, rate):
    surf_count = lax.axis_size("surf")
    wall_count = lax.axis_size("wall")
    place = lax.axis_index("wall").astype(jnp.int32).reshape(1)
    cells = cell_of.reshape(1, 1024)
    zones = zone_id.reshape(1, 1024)

    def turn(value, axis, count, by):
        return lax.ppermute(value, axis, [(i, (i + by) % count) for i in range(count)])

    outgoing, rank = call(
        route_kernel,
        "route",
        (struct(32, 128), struct(1, 1024, dtype=jnp.int32)),
        in_specs=[
            pl.BlockSpec((1, 1024), lambda i: (0, 0)),
            pl.BlockSpec((1, 1024), lambda i: (0, 0)),
            pl.BlockSpec((8, 1024), lambda i: (0, 0)),
        ],
        out_specs=(whole((32, 128)), whole((1, 1024))),
        grid=(1,),
    )(cells, zones, abl_temp)
    arrived = lax.all_to_all(outgoing, "surf", split_axis=0, concat_axis=0, tiled=True)
    next_side, prev_side = call(
        pack_kernel,
        "pack",
        (struct(5, 8, 8, 512), struct(5, 8, 8, 512)),
        in_specs=[ANY, ANY],
        out_specs=(ANY, ANY),
        scratch_shapes=[
            scratch(5, 32, 8, 512),
            scratch(5, 8, 8, 512),
            scratch(5, 8, 8, 512),
            copies(4),
            copies(2, 4),
        ],
    )(rank, flow_state)
    before = turn(next_side, "surf", surf_count, 1)
    after = turn(prev_side, "surf", surf_count, surf_count - 1)
    base = call(
        side_kernel,
        "side",
        struct(5, 32, 8, 512),
        in_specs=[ANY],
        out_specs=ANY,
        scratch_shapes=[scratch(5, 32, 8, 512), scratch(5, 32, 8, 512), copies(4), copies(4)],
    )(flow_state)
    up_wall, down_wall, wall_fields, where_cells = call(
        scatter_kernel,
        "scatter",
        (struct(18, 8, 512), struct(18, 8, 512), struct(6, 8, 512), struct(1, 1024)),
        in_specs=[
            ANY,
            whole((32, 128)),
            pl.BlockSpec((5, 2, 8, 512), lambda i: (0, 0, 0, 0)),
            pl.BlockSpec((5, 2, 8, 512), lambda i: (0, 15, 0, 0)),
            whole((32, 8, 512)),
        ],
        out_specs=(whole((18, 8, 512)), whole((18, 8, 512)), whole((6, 8, 512)), whole((1, 1024))),
        grid=(1,),
    )(base, arrived, flow_state, flow_state, spacing)
    low = turn(up_wall, "wall", wall_count, 1)
    high = turn(down_wall, "wall", wall_count, wall_count - 1)
    opposite = turn(wall_fields, "wall", wall_count, 2)
    slope, curve = call(
        normal_kernel,
        "normal",
        (struct(5, 32, 8, 512), struct(4, 32, 8, 512)),
        in_specs=[ANY, ANY],
        out_specs=(ANY, ANY),
        scratch_shapes=[
            scratch(5, 32, 8, 512),
            scratch(9, 36, 8, 512),
            scratch(5, 32, 8, 512),
            scratch(4, 32, 8, 512),
            copies(4),
            copies(2, 4),
        ],
    )(where_cells, flow_state)
    surface, returned = call(
        surface_kernel,
        "surface",
        (struct(4, 8, 512), struct(32, 128)),
        in_specs=[SCALARS] * 3 + [ANY] + [VMEM] * 5,
    )(place, conduct, rate, slope, where_cells, wall_fields, low, opposite, high)
    back = lax.all_to_all(returned, "surf", split_axis=0, concat_axis=0, tiled=True)
    state_next, node_shift = call(
        final_kernel,
        "final",
        (struct(5, 32, 8, 512), struct(32, 8, 512)),
        in_specs=[SCALARS] + [ANY] * 11,
        out_specs=(ANY, ANY),
        scratch_shapes=[
            scratch(4, 8, 512),
            scratch(12, 8, 512),
            scratch(12, 8, 512),
            pltpu.VMEM((8, 512), jnp.int32),
            scratch(36, 8, 512),
            scratch(5, 32, 8, 512),
            scratch(5, 32, 8, 512),
            scratch(5, 32, 8, 512),
            scratch(4, 32, 8, 512),
            scratch(5, 8, 8, 512),
            scratch(5, 8, 8, 512),
            scratch(2, 5, 8, 512),
            scratch(3, 8, 512),
            scratch(32, 8, 512),
            copies(5),
            copies(4, 4),
            copies(2, 4),
            copies(4),
            copies(4),
        ],
    )(place, surface, low, high, bc_kind, spacing, flow_state, base, slope, curve, before, after)
    ablator_next = call(
        ablate_kernel,
        "ablate",
        struct(64, 1024),
        in_specs=[SCALARS, ANY] + [VMEM] * 5,
    )(diffuse, node_shift, cells, rank, zones, back, abl_temp)
    return (state_next, node_shift, ablator_next)


def solution(mesh):
    in_specs = (
        P(None, "wall", "surf", None),
        P("wall", "surf", None),
        P("surf", None),
        P(("surf", "wall")),
        P(("surf", "wall")),
        P(None, ("surf", "wall")),
        P(),
        P(),
        P(),
    )
    out_specs = (P(None, "wall", "surf", None), P("wall", "surf", None), P(None, ("surf", "wall")))
    return jax.shard_map(shards, mesh=mesh, in_specs=in_specs, out_specs=out_specs, check_vma=False)
```

time: 75.1 us -> 65.7 us (0.87)
  the two profiles are of different devices: /device:TPU:2 before, /device:TPU:1 now
where the time goes in v2:
time: 65.7 us; the launch traced here: 64.6 us
  Pallas kernels  30.6 us (47%)
  starting transfers between devices  22.9 us (35%)
  waiting for transfers between devices  8.31 us (13%)
  local copies, waits for them, and re-layouts  2.02 us (3%)
  between operations  0.73 us (1%)
    ppermute x5, starting transfers between devices, turn(): lax.ppermute(value, axis, [(i, (i + by) % count) for i in range(count)])  12.4 us
    pallas_call x1, Pallas kernels, shards(): call(final_kernel, 'final', (struct(5, 32, 8, 512), struct(32, 8, 512)),...  7.59 us
    pallas_call x1, Pallas kernels, shards(): call(side_kernel, 'side', struct(5, 32, 8, 512), in_specs=[ANY], out_spec...  7.29 us
    all_to_all x1, starting transfers between devices, shards(): lax.all_to_all(returned, 'surf', split_axis=0, concat_axis=0, tiled=True)  6.63 us
    pallas_call x1, Pallas kernels, shards(): call(normal_kernel, 'normal', (struct(5, 32, 8, 512), struct(4, 32, 8, 51...  4.43 us
    ppermute x5, waiting for transfers between devices, turn(): lax.ppermute(value, axis, [(i, (i + by) % count) for i in range(count)])  4.41 us
    all_to_all x1, waiting for transfers between devices, shards(): lax.all_to_all(outgoing, 'surf', split_axis=0, concat_axis=0, tiled=True)  3.9 us
    all_to_all x1, starting transfers between devices, shards(): lax.all_to_all(outgoing, 'surf', split_axis=0, concat_axis=0, tiled=True)  3.83 us
  transfers between devices with their start and end apart: 7, of which 2 were waited for; matrix products, arithmetic and copies ran while one was open for 0% of the time, Pallas kernels for 37%

profile of v2, /device:TPU:1, one launch (start us, length us, event | category | flops | bytes accessed | tf_op | source)
XLA Modules:
  0.0 64.6 jit_solution(16837787655108586851)
XLA Ops:
  0.6 1.9 %route.1 = (f32[32,128]{1,0:T(8,128)}, s32[1,1024]{1,0:T(1,128)}) custom-call(s32[1,1024]{1,0:T(1,128)} %bitcast.13, s32[1,1024]{1,0:T(1,128)} %bitcast.15, f32[64,1024]{1,0:T(8,128)} %temps.3), custom_call_target="tpu_custom_call" | custom-call | flops 1000 | bytes 1000 | tf_op jit(solution)/shard_map/route/pallas_call | solution.py:594
  2.5 2.6 %pack.1 = (f32[5,8,8,512]{3,2,1,0:T(8,128)}, f32[5,8,8,512]{3,2,1,0:T(8,128)}) custom-call(s32[1,1024]{1,0:T(1,128)} %get-tuple-element.25.token.rank, f32[5,32,8,512]{3,2,1,0:T(8,128)} %flow_hbm.7), custom_call_target="tpu_custom_call" | custom-call | flops 1000 | bytes 1000 | tf_op jit(solution)/shard_map/pack/pallas_call | solution.py:607
  5.1 2.2 %collective-permute-start.3 = (f32[5,8,8,512]{3,2,1,0:T(8,128)}, f32[5,8,8,512]{3,2,1,0:T(8,128)}, u32[]{:S(2)}, u32[]{:S(2)}) collective-permute-start(f32[5,8,8,512]{3,2,1,0:T(8,128)} %get-tuple-element.26), channel_id=1, source_target_pairs={{0,4},{4,8},{8,12},{12,16},{16,20},{20,24},{24,28},{28,32},{32,36}... | collective-permute-start | bytes 1966088 | tf_op jit(solution)/shard_map/ppermute | solution.py:592
  7.3 5.1 %collective-permute-start.4 = (f32[5,8,8,512]{3,2,1,0:T(8,128)}, f32[5,8,8,512]{3,2,1,0:T(8,128)}, u32[]{:S(2)}, u32[]{:S(2)}) collective-permute-start(f32[5,8,8,512]{3,2,1,0:T(8,128)} %get-tuple-element.27), channel_id=1, source_target_pairs={{0,124},{4,0},{8,4},{12,8},{16,12},{20,16},{24,20},{28,24},{32,28}... | collective-permute-start | bytes 1966088 | tf_op jit(solution)/shard_map/ppermute | solution.py:592
  12.4 3.8 %all-to-all-start = ((f32[32,1,128]{2,1,0:T(1,128)}), f32[32,1,128]{2,1,0:T(1,128)S(1)}, u32[]{:S(2)}, u32[]{:S(2)}) async-start(f32[32,1,128]{2,1,0:T(1,128)} %bitcast.4), calls=%async_computation | async-start | bytes 32768 | tf_op jit(solution)/shard_map/all_to_all | solution.py:606
  16.2 7.3 %side.1.token.base_hbm = f32[5,32,8,512]{3,2,1,0:T(8,128)} custom-call(f32[5,32,8,512]{3,2,1,0:T(8,128)} %flow_hbm.7), custom_call_target="tpu_custom_call" | custom-call | flops 1000 | bytes 1000 | tf_op jit(solution)/shard_map/side/pallas_call | solution.py:623
  23.5 3.9 %all-to-all-done = f32[32,1,128]{2,1,0:T(1,128)S(1)} async-done(((f32[32,1,128]{2,1,0:T(1,128)}), f32[32,1,128]{2,1,0:T(1,128)S(1)}, u32[]{:S(2)}, u32[]{:S(2)}) %all-to-all-start) | async-done | bytes 16416 | tf_op jit(solution)/shard_map/all_to_all | solution.py:606
  27.4 0.6 copy-done.4
  28.0 2.6 %scatter.1 = (f32[18,8,512]{2,1,0:T(8,128)}, f32[18,8,512]{2,1,0:T(8,128)}, f32[6,8,512]{2,1,0:T(8,128)}, f32[1,1024]{1,0:T(1,128)}) custom-call(f32[5,32,8,512]{3,2,1,0:T(8,128)} %side.1.token.base_hbm, f32[32,128]{1,0:T(8,128)} %bitcast.12, f32[5,32,8,512]{3,2,1,0:T(8,128)} %flow_hbm.7, f32[5,32,8,512]{3,2,1,0:T(8,128)} %flow_hbm.7, f32[32,8,512]{2,1,0:T(8,128)} %spacing_hbm.1), custom_call_target="tpu_custom_call" | custom-call | flops 1000 | bytes 1000 | tf_op jit(solution)/shard_map/scatter/pallas_call | solution.py:631
  30.7 5.0 %collective-permute-start = (f32[18,8,512]{2,1,0:T(8,128)}, f32[18,8,512]{2,1,0:T(8,128)S(1)}, u32[]{:S(2)}, u32[]{:S(2)}) collective-permute-start(f32[18,8,512]{2,1,0:T(8,128)} %get-tuple-element.21), channel_id=1, source_target_pairs={{0,1},{1,2},{2,3},{3,0},{4,5},{5,6},{6,7},{7,4},{8,9},{9,10},{10,1... | collective-permute-start | bytes 884744 | tf_op jit(solution)/shard_map/ppermute | solution.py:592
  35.7 0.0 collective-permute-start.2
  35.7 0.2 collective-permute-start.1
  35.8 4.4 %normal.1 = (f32[5,32,8,512]{3,2,1,0:T(8,128)}, f32[4,32,8,512]{3,2,1,0:T(8,128)}) custom-call(f32[1,1024]{1,0:T(1,128)} %get-tuple-element.18.token.where_in, f32[5,32,8,512]{3,2,1,0:T(8,128)} %flow_hbm.7), custom_call_target="tpu_custom_call" | custom-call | flops 1000 | bytes 1000 | tf_op jit(solution)/shard_map/normal/pallas_call | solution.py:648
  40.3 4.4 %collective-permute-done.1.opposite = f32[6,8,512]{2,1,0:T(8,128)S(1)} collective-permute-done((f32[6,8,512]{2,1,0:T(8,128)}, f32[6,8,512]{2,1,0:T(8,128)S(1)}, u32[]{:S(2)}, u32[]{:S(2)}) %collective-permute-start.1) | collective-permute-done | bytes 98336 | tf_op jit(solution)/shard_map/ppermute | solution.py:592
  44.7 0.0 collective-permute-done.low.low_hbm
  44.7 0.0 collective-permute-done.2.high.high_hbm
  44.7 0.6 copy-done.2
  45.3 0.1 copy-done
  45.4 0.1 copy-done.1
  45.5 2.2 %surface.1 = (f32[4,8,512]{2,1,0:T(8,128)}, f32[32,128]{1,0:T(8,128)}) custom-call(s32[1]{0:T(128)} %bitcast.place, f32[8]{0:T(128)} %conduct.1, f32[8]{0:T(128)} %rate.1, f32[5,32,8,512]{3,2,1,0:T(8,128)} %get-tuple-element.19.token.slope_hbm, f32[1,1024]{1,0:T(1,128)} %get-tuple-element.18.token.where_in, f32[6,8,512]{2,1,0:T(8,128)} %get-tuple-element.20.own, ...), custom_call_target="tpu_custom_call" | custom-call | flops 1000 | bytes 1000 | tf_op jit(solution)/shard_map/surface/pallas_call | solution.py:663
  47.7 6.6 %all-to-all-start.1 = ((f32[32,1,128]{2,1,0:T(1,128)}), f32[32,1,128]{2,1,0:T(1,128)S(1)}, u32[]{:S(2)}, u32[]{:S(2)}) async-start(f32[32,1,128]{2,1,0:T(1,128)} %bitcast.17), calls=%async_computation.1 | async-start | bytes 32768 | tf_op jit(solution)/shard_map/all_to_all | solution.py:669
  54.4 7.6 %final.1 = (f32[5,32,8,512]{3,2,1,0:T(8,128)}, f32[32,8,512]{2,1,0:T(8,128)}) custom-call(s32[1]{0:T(128)} %bitcast.place, f32[4,8,512]{2,1,0:T(8,128)} %get-tuple-element.23.surface_hbm, f32[18,8,512]{2,1,0:T(8,128)} %copy-done, f32[18,8,512]{2,1,0:T(8,128)} %copy-done.1, s32[8,512]{1,0:T(8,128)} %kinds_hbm.1, f32[32,8,512]{2,1,0:T(8,128)} %spacing_hbm.1, ...), custom_call_target="tpu_custom_call" | custom-call | flops 1000 | bytes 1000 | tf_op jit(solution)/shard_map/final/pallas_call | solution.py:670
  62.0 0.6 copy-done.3
  62.6 2.0 %ablate.1 = f32[64,1024]{1,0:T(8,128)} custom-call(f32[8]{0:T(128)} %diffuse.1, f32[32,8,512]{2,1,0:T(8,128)} %get-tuple-element.15.token, s32[1,1024]{1,0:T(1,128)} %bitcast.14, s32[1,1024]{1,0:T(1,128)} %get-tuple-element.25.token.rank, s32[1,1024]{1,0:T(1,128)} %bitcast.16, f32[32,128]{1,0:T(8,128)} %bitcast.11, f32[64,1024]{1,0:T(8,128)} %temps.3), custom_call_target="tpu_custom_call" | custom-call | flops 1000 | bytes 1000 | tf_op jit(solution)/shard_map/ablate/pallas_call | solution.py:698
  (8 shorter events, 0.0 us)
Async XLA Ops:
  5.1 49.2 %collective-permute-start.3 = (f32[5,8,8,512]{3,2,1,0:T(8,128)}, f32[5,8,8,512]{3,2,1,0:T(8,128)}, u32[]{:S(2)}, u32[]{:S(2)}) collective-permute-start(f32[5,8,8,512]{3,2,1,0:T(8,128)} %get-tuple-element.26), channel_id=1, source_target_pairs={{0,4},{4,8},{8,12},{12,16},{16,20},{20,24},{24,28},{28,32},{32,36}... | collective-permute-start | bytes 1966088 | tf_op jit(solution)/shard_map/ppermute | solution.py:592
  7.3 47.0 %collective-permute-start.4 = (f32[5,8,8,512]{3,2,1,0:T(8,128)}, f32[5,8,8,512]{3,2,1,0:T(8,128)}, u32[]{:S(2)}, u32[]{:S(2)}) collective-permute-start(f32[5,8,8,512]{3,2,1,0:T(8,128)} %get-tuple-element.27), channel_id=1, source_target_pairs={{0,124},{4,0},{8,4},{12,8},{16,12},{20,16},{24,20},{28,24},{32,28}... | collective-permute-start | bytes 1966088 | tf_op jit(solution)/shard_map/ppermute | solution.py:592
  12.4 15.0 %all-to-all-start = ((f32[32,1,128]{2,1,0:T(1,128)}), f32[32,1,128]{2,1,0:T(1,128)S(1)}, u32[]{:S(2)}, u32[]{:S(2)}) async-start(f32[32,1,128]{2,1,0:T(1,128)} %bitcast.4), calls=%async_computation | async-start | bytes 32768 | tf_op jit(solution)/shard_map/all_to_all | solution.py:606
  27.4 0.6 copy-start.4
  30.7 14.0 %collective-permute-start = (f32[18,8,512]{2,1,0:T(8,128)}, f32[18,8,512]{2,1,0:T(8,128)S(1)}, u32[]{:S(2)}, u32[]{:S(2)}) collective-permute-start(f32[18,8,512]{2,1,0:T(8,128)} %get-tuple-element.21), channel_id=1, source_target_pairs={{0,1},{1,2},{2,3},{3,0},{4,5},{5,6},{6,7},{7,4},{8,9},{9,10},{10,1... | collective-permute-start | bytes 884744 | tf_op jit(solution)/shard_map/ppermute | solution.py:592
  35.7 9.0 %collective-permute-start.2 = (f32[18,8,512]{2,1,0:T(8,128)}, f32[18,8,512]{2,1,0:T(8,128)S(1)}, u32[]{:S(2)}, u32[]{:S(2)}) collective-permute-start(f32[18,8,512]{2,1,0:T(8,128)} %get-tuple-element.22), channel_id=1, source_target_pairs={{0,3},{1,0},{2,1},{3,2},{4,7},{5,4},{6,5},{7,6},{8,11},{9,8},{10,9... | collective-permute-start | bytes 884744 | tf_op jit(solution)/shard_map/ppermute | solution.py:592
  35.7 9.0 %collective-permute-start.1 = (f32[6,8,512]{2,1,0:T(8,128)}, f32[6,8,512]{2,1,0:T(8,128)S(1)}, u32[]{:S(2)}, u32[]{:S(2)}) collective-permute-start(f32[6,8,512]{2,1,0:T(8,128)} %get-tuple-element.20.own), channel_id=1, source_target_pairs={{0,2},{1,3},{2,0},{3,1},{4,6},{5,7},{6,4},{7,5},{8,10},{9,11},{10,... | collective-permute-start | bytes 294920 | tf_op jit(solution)/shard_map/ppermute | solution.py:592
  44.7 0.6 copy-start.2
  44.7 0.7 %copy-start = (f32[18,8,512]{2,1,0:T(8,128)}, f32[18,8,512]{2,1,0:T(8,128)S(1)}, u32[]{:S(2)}) copy-start(f32[18,8,512]{2,1,0:T(8,128)S(1)} %collective-permute-done.low.low_hbm) | copy-start | bytes 884740
  44.7 0.8 %copy-start.1 = (f32[18,8,512]{2,1,0:T(8,128)}, f32[18,8,512]{2,1,0:T(8,128)S(1)}, u32[]{:S(2)}) copy-start(f32[18,8,512]{2,1,0:T(8,128)S(1)} %collective-permute-done.2.high.high_hbm) | copy-start | bytes 884740
  47.7 14.3 %all-to-all-start.1 = ((f32[32,1,128]{2,1,0:T(1,128)}), f32[32,1,128]{2,1,0:T(1,128)S(1)}, u32[]{:S(2)}, u32[]{:S(2)}) async-start(f32[32,1,128]{2,1,0:T(1,128)} %bitcast.17), calls=%async_computation.1 | async-start | bytes 32768 | tf_op jit(solution)/shard_map/all_to_all | solution.py:669
  62.0 0.6 copy-start.3

commit v3 on v2

v3 whole, which is shorter than its diff:
```python
import functools
import jax
import jax.numpy as jnp
from jax import lax
from jax.experimental import pallas as pl
from jax.experimental.pallas import tpu as pltpu
from jax.sharding import PartitionSpec as P

gas = 0.4
time_step = 0.15
viscosity = 0.05
conduction = 0.07
sponge_rate = 0.5
activation = 2.0
radiation = 0.8
recovery = 0.2
far_values = (1.0, 0.5, 0.0, 0.0, 2.625)
diffusivity = (viscosity, viscosity, viscosity, conduction)

F32 = jnp.float32
BF16 = jnp.bfloat16


def iota(shape, axis):
    return lax.broadcasted_iota(jnp.int32, shape, axis)


def split3(x):
    high = x.astype(BF16)
    rest = x - high.astype(F32)
    middle = rest.astype(BF16)
    low = (rest - middle.astype(F32)).astype(BF16)
    return high, middle, low


def dot_nn(a, b):
    return lax.dot_general(a, b, (((1,), (0,)), ((), ())), preferred_element_type=F32)


def dot_nt(a, b):
    return lax.dot_general(a, b, (((1,), (1,)), ((), ())), preferred_element_type=F32)


def join3(x, rows):
    return x[:rows] + x[rows : 2 * rows] + x[2 * rows :]


def to_rows(x):
    return jnp.concatenate([x[:, 128 * c : 128 * c + 128] for c in range(4)], axis=0)


def to_grid(x):
    return jnp.concatenate([x[8 * c : 8 * c + 8] for c in range(4)], axis=1)


def onehot(mask):
    return jnp.where(mask, 1.0, 0.0).astype(BF16)


def primitives(u0, u1, u2, u3, u4):
    inverse = 1.0 / u0
    vx = u1 * inverse
    vy = u2 * inverse
    vz = u3 * inverse
    pressure = gas * (u4 - 0.5 * (u1 * vx + u2 * vy + u3 * vz))
    return inverse, vx, vy, vz, pressure


def start_all(copies):
    for copy in copies:
        copy.start()


def wait_all(copies):
    for copy in copies:
        copy.wait()


def begin_kernel(
    place,
    cell_hbm,
    zone_hbm,
    temps_hbm,
    spacing_hbm,
    flow_hbm,
    outgoing,
    rank_out,
    core_wall,
    cross_wall,
    wall_fields,
    pair_hbm,
    cross_hbm,
    cell,
    zone,
    temps,
    spacing,
    flow,
    sides,
    small_sem,
    in_sem,
    out_sem,
):
    even = place[0] % 2 == 0
    parity = place[1]
    small = [
        pltpu.make_async_copy(source, target, small_sem.at[index])
        for index, (source, target) in enumerate(
            (
                (cell_hbm, cell),
                (zone_hbm, zone),
                (temps_hbm.at[pl.ds(0, 8)], temps),
                (spacing_hbm, spacing),
            )
        )
    ]
    loads = [
        pltpu.make_async_copy(chunk_of(flow_hbm, c), chunk_of(flow, c), in_sem.at[c]) for c in range(4)
    ]
    start_all(small)
    start_all(loads)
    wait_all(small)
    cells = cell[...]
    tile = cells // 4096
    within = cells - tile * 4096
    hit = iota((32, 1024), 0) == tile
    ones = jnp.where(hit, 1.0, 0.0)
    stacked = jnp.concatenate([ones[:, 128 * k : 128 * k + 128] for k in range(8)], axis=0)
    inner = iota((128, 256), 0)
    outer = iota((128, 256), 1)
    ahead = onehot((inner < outer) | (outer >= 128))
    counts = dot_nn(stacked.astype(BF16), ahead)
    offset = jnp.zeros((32, 128), F32)
    ranks = []
    for k in range(8):
        part = slice(32 * k, 32 * k + 32)
        place = counts[part, :128] + offset
        ranks.append(jnp.sum(stacked[part] * place, axis=0, keepdims=True))
        offset = offset + counts[part, 128:]
    rank = jnp.concatenate(ranks, axis=1).astype(jnp.int32)
    rank_out[...] = rank
    slot = iota((32, 1024), 0) == rank
    first, second = temps[0:1], temps[1:2]
    fields = (within.astype(F32), (zone[...] + 1).astype(F32), first, second)
    pieces = [split3(value) for value in fields]
    rows = []
    for level in range(3):
        for piece in pieces:
            rows.append(jnp.where(slot, piece[level].astype(F32), 0.0).astype(BF16))
    sent = dot_nt(ones.astype(BF16), jnp.concatenate(rows, axis=0))
    outgoing[...] = sent[:, :128] + sent[:, 128:256] + sent[:, 256:]
    row = iota((8, 512), 0) // 2
    stores = []
    for c in range(4):
        loads[c].wait()

        def field(m, carry, c=c):
            for block in (2 * c, 2 * c + 1):
                high = jnp.zeros((8, 512), F32)
                low = jnp.zeros((8, 512), F32)
                for b in range(4):
                    plane = flow[m, block * 4 + b]
                    rolled_high = pltpu.roll(plane, (2 * b + 2) % 8, 0) if b != 3 else plane
                    rolled_low = pltpu.roll(plane, 2 * b, 0) if b else plane
                    high = jnp.where(row == b, rolled_high, high)
                    low = jnp.where(row == b, rolled_low, low)
                sides[0, m, block] = high
                sides[1, m, block] = low
            return carry

        lax.fori_loop(0, 5, field, 0)
        part = pl.ds(2 * c, 2)
        for index, (side, there) in enumerate(((parity, pair_hbm), (1 - parity, cross_hbm))):
            copy = pltpu.make_async_copy(sides.at[side, :, part], there.at[:, part], out_sem.at[index, c])
            copy.start()
            stores.append(copy)
    layers = [(flow[m, 30 + n], flow[m, n]) for m in range(5) for n in range(2)]
    layers += [(spacing[30 + n], spacing[n]) for n in range(2)]
    for index, (top, bottom) in enumerate(layers):
        core_wall[index] = jnp.where(even, top, bottom)
        cross_wall[index] = jnp.where(even, bottom, top)
    inverse, vx, vy, vz, pressure = primitives(*[flow[m, 0] for m in range(5)])
    film = 2.0 / spacing[0]
    temp = pressure * inverse + recovery * (vx * vx + vy * vy + vz * vz)
    total = spacing[0]
    for k in range(1, 32):
        total = total + spacing[k]
    for index, value in enumerate((film, temp, total)):
        core_wall[12 + index] = value
        cross_wall[12 + index] = value
        wall_fields[index] = value
    wait_all(stores)


def surface_kernel(
    place, conduct, rate, token, arrived, own, core, twin, cross, dense, sums, where_out
):
    wall = place[0]
    received = arrived[...]
    pieces = jnp.concatenate(split3(received), axis=0)
    lane = iota((128, 1024), 1) % 32
    line = iota((128, 1024), 0)
    source = iota((32, 1024), 0) == iota((32, 1024), 1) // 32
    flat = []
    for f in range(4):
        spread = join3(dot_nn(pieces, onehot(line == lane + 32 * f)), 32)
        flat.append(jnp.sum(jnp.where(source, spread, 0.0), axis=0, keepdims=True))
    where_out[...] = flat[0]
    cells = flat[0].astype(jnp.int32)
    block = ((cells % 512) // 128) * 8 + cells // 512
    block_hit = iota((32, 1024), 0) == block
    lane_hit = onehot(line == cells % 128)
    rows = [jnp.where(block_hit, flat[1], 0.0).astype(BF16)]
    for value in flat[2:]:
        for piece in split3(value):
            rows.append(jnp.where(block_hit, piece.astype(F32), 0.0).astype(BF16))
    grid = dot_nt(jnp.concatenate(rows, axis=0), lane_hit)
    zones = to_grid(grid[:32])
    surface = to_grid(join3(grid[32:128], 32))
    inner = to_grid(join3(grid[128:], 32))

    def from_bottom(f):
        return jnp.where(
            wall == 0,
            own[f],
            jnp.where(wall == 1, core[12 + f], jnp.where(wall == 2, twin[f], cross[12 + f])),
        )

    sums[0] = (own[2] + core[14]) + (twin[2] + cross[14])
    below = jnp.where(wall % 2 == 1, core[14], 0.0)
    sums[1] = below + jnp.where(wall >= 2, twin[2] + cross[14], 0.0)
    film = from_bottom(0)
    recover = from_bottom(1)
    cond = jnp.zeros((8, 512), F32)
    speed = jnp.zeros((8, 512), F32)
    for z in range(8):
        cond = jnp.where(zones == z + 1.0, conduct[z], cond)
        speed = jnp.where(zones == z + 1.0, rate[z], speed)
    base = film * recover + cond * inner
    for step in range(2):
        cube = surface * surface * surface
        surface = (base + 3.0 * radiation * cube * surface) / (film + cond + 4.0 * radiation * cube)
    recess = speed * jnp.exp(-activation / surface)
    taken = zones > 0.5
    dense[0] = jnp.where(taken, surface, 0.0)
    dense[1] = jnp.where(taken, recess, 0.0)


def return_kernel(where_in, dense, outgoing):
    cells = where_in[...].astype(jnp.int32)
    block = ((cells % 512) // 128) * 8 + cells // 512
    block_hit = iota((32, 1024), 0) == block
    line = iota((128, 1024), 0)
    lane_hit = onehot(line == cells % 128)
    pieces = jnp.concatenate(split3(to_rows(dense[0])), axis=0)
    spread = join3(dot_nn(pieces, lane_hit), 32)
    flat = jnp.sum(jnp.where(block_hit, spread, 0.0), axis=0, keepdims=True)
    source = iota((32, 1024), 0) == iota((32, 1024), 1) // 32
    rows = [jnp.where(source, piece.astype(F32), 0.0).astype(BF16) for piece in split3(flat)]
    slot = onehot(line == iota((128, 1024), 1) % 32)
    outgoing[...] = join3(dot_nt(jnp.concatenate(rows, axis=0), slot), 32)


def ablate_kernel(diffuse, token, cell, rank, zone, back, temps, out):
    pieces = jnp.concatenate(split3(back[...]), axis=0)
    slot = onehot(iota((128, 1024), 0) == rank[...])
    spread = join3(dot_nn(pieces, slot), 32)
    tile_hit = iota((32, 1024), 0) == cell[...] // 4096
    surface = jnp.sum(jnp.where(tile_hit, spread, 0.0), axis=0, keepdims=True)
    zones = zone[...]
    spread_rate = jnp.zeros((1, 1024), F32)
    for z in range(8):
        spread_rate = jnp.where(zones == z, diffuse[z], spread_rate)
    row = iota((64, 1024), 0)
    profile = jnp.where(row == 0, surface, temps[...])
    for step in range(2):
        before = pltpu.roll(profile, 1, 0)
        after = pltpu.roll(profile, 63, 0)
        after = jnp.where(row == 63, before, after)
        changed = profile + spread_rate * (after - 2.0 * profile + before)
        profile = jnp.where(row == 0, profile, changed)
    out[...] = profile


def chunk_of(ref, c):
    return ref.at[:, pl.ds(8 * c, 8)]


TWELFTH = time_step / 12.0


def side_kernel(token, flow_hbm, base_hbm, flow, base, in_sem, out_sem):
    loads = [
        pltpu.make_async_copy(chunk_of(flow_hbm, c), chunk_of(flow, c), in_sem.at[c]) for c in range(4)
    ]
    start_all(loads)
    row = iota((8, 512), 0)
    limits = (row != 7, row != 0, row < 6, row >= 2)

    def one_plane(k, carry):
        u = [flow[m, k] for m in range(5)]
        inverse, vx, vy, vz, pressure = primitives(*u)
        temp = pressure * inverse
        heat = u[4] + pressure
        shear = u[1] * vy
        flux_i = (u[1], u[1] * vx + pressure, shear, u[1] * vz, heat * vx)
        flux_j = (u[2], shear, u[2] * vy + pressure, u[2] * vz, heat * vy)
        smooth = (None, vx, vy, vz, temp)
        for m in range(5):
            result = u[m]
            w = smooth[m]
            if w is not None:
                amount = TWELFTH * diffusivity[m - 1]
                w16 = (16.0 * amount) * w
                w1 = amount * w
                result = result - (60.0 * amount) * w
            for axis, flux in ((0, flux_i[m]), (1, flux_j[m])):
                near = (8.0 * TWELFTH) * flux
                far = TWELFTH * flux
                if w is None:
                    sources = (near, -near, -far, far)
                else:
                    sources = (w16 + near, w16 - near, -w1 - far, far - w1)
                if axis == 0:
                    sources = [jnp.where(limit, value, 0.0) for limit, value in zip(limits, sources)]
                size = (8, 512)[axis]
                for shift, value in zip((1, size - 1, 2, size - 2), sources):
                    result = result + pltpu.roll(value, shift, axis)
            base[m, k] = result
        return carry

    stores = []
    for c in range(4):
        loads[c].wait()
        lax.fori_loop(8 * c, 8 * c + 8, one_plane, 0)
        copy = pltpu.make_async_copy(chunk_of(base, c), chunk_of(base_hbm, c), out_sem.at[c])
        copy.start()
        stores.append(copy)
    wait_all(stores)


def normal_flux(u3, density_x, density_y, vx, vy, vz, pressure, heat):
    return (u3, density_x * vz, density_y * vz, u3 * vz + pressure, heat * vz)


def normal_flux(u3, density_x, density_y, vx, vy, vz, pressure, heat):
    return (u3, density_x * vz, density_y * vz, u3 * vz + pressure, heat * vz)


def final_kernel(
    place,
    dense_hbm,
    dense_1_hbm,
    dense_2_hbm,
    dense_3_hbm,
    sums_hbm,
    core_hbm,
    cross_hbm,
    kinds_hbm,
    spacing_hbm,
    flow_hbm,
    base_hbm,
    far_hbm,
    pair_hbm,
    out_hbm,
    shift_hbm,
    dense,
    sums,
    walls,
    kinds,
    thick,
    flow,
    base,
    sides,
    fields,
    edges,
    run,
    shift,
    small_sem,
    flow_sem,
    base_sem,
    side_sem,
    out_sem,
    shift_sem,
):
    wall = place[0]
    parity = place[1]
    odd_wall = wall % 2
    small = [
        pltpu.make_async_copy(source, target, small_sem.at[index])
        for index, (source, target) in enumerate(
            (
                (dense_hbm, dense.at[0]),
                (dense_1_hbm, dense.at[1]),
                (dense_2_hbm, dense.at[2]),
                (dense_3_hbm, dense.at[3]),
                (sums_hbm, sums),
                (core_hbm.at[pl.ds(0, 12)], walls.at[1 - odd_wall]),
                (cross_hbm.at[pl.ds(0, 12)], walls.at[odd_wall]),
                (kinds_hbm, kinds),
                (spacing_hbm, thick.at[pl.ds(2, 32)]),
            )
        )
    ]
    start_all(small)

    def flow_load(c):
        return pltpu.make_async_copy(chunk_of(flow_hbm, c), chunk_of(flow, c), flow_sem.at[c])

    def other_loads(c):
        loads = [pltpu.make_async_copy(chunk_of(base_hbm, c), chunk_of(base, c), base_sem.at[c])]
        part = pl.ds(2 * c, 2)
        for index, (source, side) in enumerate(((pair_hbm, 1 - parity), (far_hbm, parity))):
            loads.append(
                pltpu.make_async_copy(source.at[:, part], sides.at[side, :, part], side_sem.at[index, c])
            )
        return loads

    flow_load(0).start()
    for c in range(4):
        if c < 3:
            flow_load(c + 1).start()
        start_all(other_loads(c))
    row = iota((8, 512), 0)
    odd = row % 2 == 1
    is_low = wall == 0
    is_high = wall == 3

    def store_fields(position, flux, smooth):
        for index, value in enumerate(flux + smooth):
            fields[index, position] = value

    def one_field(k, carry):
        u = [flow[m, k] for m in range(5)]
        inverse, vx, vy, vz, pressure = primitives(*u)
        flux = normal_flux(u[3], u[1], u[2], vx, vy, vz, pressure, u[4] + pressure)
        store_fields(k + 2, flux, (vx, vy, vz, pressure * inverse))
        return carry

    def prepare():
        wait_all(small)
        recess = (dense[0, 1] + dense[1, 1]) + (dense[2, 1] + dense[3, 1])
        total = sums[0]
        run[0] = sums[1]
        run[1] = total / (total + recess)
        run[2] = 1.0 / total
        run[3] = recess
        thick[0] = jnp.where(is_low, thick[2], walls[0, 10])
        thick[1] = jnp.where(is_low, thick[3], walls[0, 11])
        thick[34] = jnp.where(is_high, thick[32], walls[1, 10])
        thick[35] = jnp.where(is_high, thick[33], walls[1, 11])
        for layer in range(2):
            u = [jnp.where(is_high, far_values[m], walls[1, 2 * m + layer]) for m in range(5)]
            inverse, vx, vy, vz, pressure = primitives(*u)
            flux = normal_flux(u[3], u[1], u[2], vx, vy, vz, pressure, u[4] + pressure)
            store_fields(34 + layer, flux, (vx, vy, vz, pressure * inverse))
        kind = kinds[...]
        hot = (dense[0, 0] + dense[1, 0]) + (dense[2, 0] + dense[3, 0])
        cooled = 1.0 / hot
        slip = is_low & (kind == 1)
        blow = is_low & (kind == 2)
        sign = jnp.where(is_low, -1.0, 1.0)
        for layer in range(2):
            u = [jnp.where(is_low, flow[m, layer], walls[0, 2 * m + 1 - layer]) for m in range(5)]
            inverse, vx, vy, vz, pressure = primitives(*u)
            density = jnp.where(slip | jnp.logical_not(is_low), u[0], pressure * cooled)
            gx = jnp.where(slip, vx, sign * vx)
            gy = jnp.where(slip, vy, sign * vy)
            gz = jnp.where(blow, 2.0 * recess, 0.0) + sign * vz
            heat = pressure * (1.0 / gas + 1.0) + 0.5 * density * (gx * gx + gy * gy + gz * gz)
            flux = normal_flux(density * gz, density * gx, density * gy, gx, gy, gz, pressure, heat)
            store_fields(1 - layer, flux, (gx, gy, gz, pressure / density))

    def one_block(block, carry):
        for side, near_sign in ((0, 1.0), (1, -1.0)):
            u = [sides[side, m, block] for m in range(5)]
            inverse, vx, vy, vz, pressure = primitives(*u)
            flux = (u[1], u[1] * vx + pressure, u[1] * vy, u[1] * vz, (u[4] + pressure) * vx)
            smooth = (None, vx, vy, vz, pressure * inverse)
            for m in range(5):
                near = (8.0 * TWELFTH * near_sign) * flux[m]
                far = (-TWELFTH * near_sign) * flux[m]
                if smooth[m] is not None:
                    amount = TWELFTH * diffusivity[m - 1]
                    near = near + (16.0 * amount) * smooth[m]
                    far = far - amount * smooth[m]
                if near_sign > 0:
                    moved = jnp.where(odd, 0.0, pltpu.roll(near, 7, 0))
                else:
                    moved = jnp.where(odd, pltpu.roll(near, 1, 0), 0.0)
                edges[side, m] = far + moved
        for b in range(4):
            k = block * 4 + b
            width = thick[k + 2]
            center = run[0] + 0.5 * width
            run[0] = run[0] + width
            normal = center * run[2]
            shift[k] = run[3] * (normal - 1.0)
            stretch = 7.0 * width + 3.0 * (thick[k + 1] + thick[k + 3]) - 0.5 * (thick[k] + thick[k + 4])
            factor = run[1] * (12.0 / stretch)
            damp = (time_step * sponge_rate) * (normal * normal)
            slope_scale = -TWELFTH * factor
            curve_scale = TWELFTH * (factor * factor)
            for m in range(5):
                f = [fields[m, k + o] for o in (0, 1, 3, 4)]
                slope = 8.0 * (f[2] - f[1]) - (f[3] - f[0])
                value = base[m, k] + slope_scale * slope - damp * (flow[m, k] - far_values[m])
                if m:
                    g = [fields[m + 4, k + o] for o in range(5)]
                    curve = 16.0 * (g[1] + g[3]) - (g[0] + g[4]) - 30.0 * g[2]
                    value = value + (curve_scale * diffusivity[m - 1]) * curve
                low_edge = pltpu.roll(edges[0, m], 8 - 2 * b, 0) if b else edges[0, m]
                high_edge = pltpu.roll(edges[1, m], (6 - 2 * b) % 8, 0) if b != 3 else edges[1, m]
                base[m, k] = value + jnp.where(row < 2, low_edge, jnp.where(row >= 6, high_edge, 0.0))
        return carry

    def stores(c):
        rows = pl.ds(8 * c, 8)
        return [
            pltpu.make_async_copy(chunk_of(base, c), chunk_of(out_hbm, c), out_sem.at[c]),
            pltpu.make_async_copy(shift.at[rows], shift_hbm.at[rows], shift_sem.at[c]),
        ]

    def one_chunk(c, carry):
        @pl.when(c < 4)
        def fill():
            flow_load(c).wait()
            lax.fori_loop(8 * c, 8 * c + 8, one_field, 0)

        @pl.when(c == 0)
        def begin():
            prepare()

        @pl.when(c > 0)
        def finish():
            wait_all(other_loads(c - 1))
            lax.fori_loop(2 * c - 2, 2 * c, one_block, 0)
            start_all(stores(c - 1))

        return carry

    lax.fori_loop(0, 5, one_chunk, 0)
    for c in range(4):
        wait_all(stores(c))


def whole(shape):
    return pl.BlockSpec(shape, lambda *_: (0,) * len(shape))


SCALARS = pl.BlockSpec(memory_space=pltpu.SMEM)
ANY = pl.BlockSpec(memory_space=pl.ANY)
VMEM = pl.BlockSpec(memory_space=pltpu.VMEM)


def params():
    return pltpu.CompilerParams(vmem_limit_bytes=62 * 1024 * 1024)


def cost():
    return pl.CostEstimate(flops=1000, transcendentals=0, bytes_accessed=1000)


def struct(*shape, dtype=F32):
    return jax.ShapeDtypeStruct(shape, dtype)


def call(kernel, name, out_shape, **options):
    return pl.pallas_call(
        kernel, out_shape=out_shape, name=name, compiler_params=params(), cost_estimate=cost(), **options
    )


def scratch(*shape):
    return pltpu.VMEM(shape, F32)


def copies(*shape):
    return pltpu.SemaphoreType.DMA(shape)


def shards(flow_state, spacing, bc_kind, cell_of, zone_id, abl_temp, conduct, diffuse, rate):
    surf_count = lax.axis_size("surf")
    place = jnp.stack([lax.axis_index("wall"), lax.axis_index("surf") % 2]).astype(jnp.int32)
    cells = cell_of.reshape(1, 1024)
    zones = zone_id.reshape(1, 1024)

    def swap(value, axis, partner):
        return lax.ppermute(value, axis, [(i, partner(i)) for i in range(lax.axis_size(axis))])

    outgoing, rank, core_wall, cross_wall, wall_fields, pair_side, cross_side = call(
        begin_kernel,
        "begin",
        (
            struct(32, 128),
            struct(1, 1024, dtype=jnp.int32),
            struct(15, 8, 512),
            struct(15, 8, 512),
            struct(3, 8, 512),
            struct(5, 8, 8, 512),
            struct(5, 8, 8, 512),
        ),
        in_specs=[SCALARS] + [ANY] * 5,
        out_specs=(VMEM,) * 5 + (ANY,) * 2,
        scratch_shapes=[
            pltpu.VMEM((1, 1024), jnp.int32),
            pltpu.VMEM((1, 1024), jnp.int32),
            scratch(8, 1024),
            scratch(32, 8, 512),
            scratch(5, 32, 8, 512),
            scratch(2, 5, 8, 8, 512),
            copies(4),
            copies(4),
            copies(2, 4),
        ],
    )(place, cells, zones, abl_temp, spacing, flow_state)
    arrived = lax.all_to_all(outgoing, "surf", split_axis=0, concat_axis=0, tiled=True)
    cross = swap(cross_wall, "wall", lambda i: i ^ 3)
    twin = swap(wall_fields, "wall", lambda i: i ^ 2)
    core = swap(core_wall, "wall", lambda i: i ^ 1)
    far = swap(cross_side, "surf", lambda i: (i - 1 + 2 * (i % 2)) % surf_count)
    pair = swap(pair_side, "surf", lambda i: i ^ 1)
    base = call(
        side_kernel,
        "side",
        struct(5, 32, 8, 512),
        in_specs=[ANY, ANY],
        out_specs=ANY,
        scratch_shapes=[scratch(5, 32, 8, 512), scratch(5, 32, 8, 512), copies(4), copies(4)],
    )(rank, flow_state)
    dense, sums, where_cells = call(
        surface_kernel,
        "surface",
        (struct(2, 8, 512), struct(2, 8, 512), struct(1, 1024)),
        in_specs=[SCALARS] * 3 + [ANY] + [VMEM] * 5,
    )(place, conduct, rate, base, arrived, wall_fields, core, twin, cross)
    dense_1, dense_2, dense_3 = (swap(dense, "wall", lambda i, by=by: i ^ by) for by in (1, 2, 3))
    returned = call(return_kernel, "answer", struct(32, 128))(where_cells, dense)
    back = lax.all_to_all(returned, "surf", split_axis=0, concat_axis=0, tiled=True)
    state_next, node_shift = call(
        final_kernel,
        "final",
        (struct(5, 32, 8, 512), struct(32, 8, 512)),
        in_specs=[SCALARS] + [ANY] * 13,
        out_specs=(ANY, ANY),
        scratch_shapes=[
            scratch(4, 2, 8, 512),
            scratch(2, 8, 512),
            scratch(2, 12, 8, 512),
            pltpu.VMEM((8, 512), jnp.int32),
            scratch(36, 8, 512),
            scratch(5, 32, 8, 512),
            scratch(5, 32, 8, 512),
            scratch(2, 5, 8, 8, 512),
            scratch(9, 36, 8, 512),
            scratch(2, 5, 8, 512),
            scratch(4, 8, 512),
            scratch(32, 8, 512),
            copies(9),
            copies(4),
            copies(4),
            copies(2, 4),
            copies(4),
            copies(4),
        ],
    )(
        place,
        dense,
        dense_1,
        dense_2,
        dense_3,
        sums,
        core,
        cross,
        bc_kind,
        spacing,
        flow_state,
        base,
        far,
        pair,
    )
    ablator_next = call(
        ablate_kernel,
        "ablate",
        struct(64, 1024),
        in_specs=[SCALARS, ANY] + [VMEM] * 5,
    )(diffuse, node_shift, cells, rank, zones, back, abl_temp)
    return (state_next, node_shift, ablator_next)


def solution(mesh):
    in_specs = (
        P(None, "wall", "surf", None),
        P("wall", "surf", None),
        P("surf", None),
        P(("surf", "wall")),
        P(("surf", "wall")),
        P(None, ("surf", "wall")),
        P(),
        P(),
        P(),
    )
    out_specs = (P(None, "wall", "surf", None), P("wall", "surf", None), P(None, ("surf", "wall")))
    return jax.shard_map(shards, mesh=mesh, in_specs=in_specs, out_specs=out_specs, check_vma=False)
```

time: 65.7 us -> 63 us (0.959); the launches traced: 64.6 us -> 62.6 us
  Pallas kernels: 30.6 us -> 26.5 us
  waiting for transfers between devices: 8.31 us -> 9.43 us
    pallas_call x6 -> x4, Pallas kernels: 21 us -> 16.3 us  [the longest x1 7.27 us: shards(): call(side_kernel, 'side', struct(5, 32, 8, 512), in_specs=[ANY, ANY], out...]
    all_to_all x1, starting transfers between devices: 6.63 us -> 3.88 us  [shards(): lax.all_to_all(returned, 'surf', split_axis=0, concat_axis=0, tiled=True)]
    ppermute x5 -> x8, starting transfers between devices: 12.4 us -> 15.1 us  [swap(): lax.ppermute(value, axis, [(i, partner(i)) for i in range(lax.axis_size(a...]
    all_to_all x1, waiting for transfers between devices: 3.9 us -> 6.48 us  [shards(): lax.all_to_all(outgoing, 'surf', split_axis=0, concat_axis=0, tiled=True)]
    ppermute x5 -> x8, waiting for transfers between devices: 4.41 us -> 2.95 us  [swap(): lax.ppermute(value, axis, [(i, partner(i)) for i in range(lax.axis_size(a...]
    unnamed x10 -> x20, local copies, waits for them, and re-layouts: 2.02 us -> 2.4 us
  transfers between devices with their start and end apart: 7 -> 10, of which waited for: 2 -> 2; matrix products, arithmetic and copies ran while one was open for 0% -> 0% of each run, Pallas kernels for 37% -> 31%
where the time goes in v3:
time: 63 us; the launch traced here: 62.6 us
  Pallas kernels  26.5 us (42%)
  starting transfers between devices  22.8 us (36%)
  waiting for transfers between devices  9.43 us (15%)
  local copies, waits for them, and re-layouts  2.4 us (4%)
  between operations  0.81 us (1%)
  other arithmetic  0.64 us (1%)
    ppermute x8, starting transfers between devices, swap(): lax.ppermute(value, axis, [(i, partner(i)) for i in range(lax.axis_size(a...  15.1 us
    pallas_call x1, Pallas kernels, shards(): call(final_kernel, 'final', (struct(5, 32, 8, 512), struct(32, 8, 512)),...  8.16 us
    pallas_call x1, Pallas kernels, shards(): call(side_kernel, 'side', struct(5, 32, 8, 512), in_specs=[ANY, ANY], out...  7.27 us
    all_to_all x1, waiting for transfers between devices, shards(): lax.all_to_all(outgoing, 'surf', split_axis=0, concat_axis=0, tiled=True)  6.48 us
    pallas_call x1, Pallas kernels, shards(): call(begin_kernel, 'begin', (struct(32, 128), struct(1, 1024, dtype=jnp.i...  4.91 us
    all_to_all x1, starting transfers between devices, shards(): lax.all_to_all(returned, 'surf', split_axis=0, concat_axis=0, tiled=True)  3.88 us
    all_to_all x1, starting transfers between devices, shards(): lax.all_to_all(outgoing, 'surf', split_axis=0, concat_axis=0, tiled=True)  3.84 us
    ppermute x8, waiting for transfers between devices, swap(): lax.ppermute(value, axis, [(i, partner(i)) for i in range(lax.axis_size(a...  2.95 us
  transfers between devices with their start and end apart: 10, of which 2 were waited for; matrix products, arithmetic and copies ran while one was open for 0% of the time, Pallas kernels for 31%

profile of v3, /device:TPU:1, one launch (start us, length us, event | category | flops | bytes accessed | tf_op | source)
XLA Modules:
  0.0 62.6 jit_solution(3332145194635389311)
XLA Ops:
  0.6 0.6 %pad_add_fusion.place = s32[2]{0:T(128)} fusion(s32[1]{0:T(128)} %bitcast.1, s32[1]{0:T(128)} %bitcast), kind=kLoop, calls=%fused_computation | loop fusion | flops 2 | bytes 16 | tf_op jit(solution)/shard_map/stack | solution.py:583
  1.3 4.9 %begin.1 = (f32[32,128]{1,0:T(8,128)}, s32[1,1024]{1,0:T(1,128)}, f32[15,8,512]{2,1,0:T(8,128)}, f32[15,8,512]{2,1,0:T(8,128)}, f32[3,8,512]{2,1,0:T(8,128)}, /*...) custom-call(s32[2]{0:T(128)} %pad_add_fusion.place, s32[1,1024]{1,0:T(1,128)} %bitcast.15, s32[1,1024]{1,0:T(1,128)} %bitcast.17, ...), custom_call_target="tpu_custom_call" | custom-call | flops 1000 | bytes 1000 | tf_op jit(solution)/shard_map/begin/pallas_call | solution.py:590
  6.2 7.2 %collective-permute-start.6 = (f32[5,8,8,512]{3,2,1,0:T(8,128)}, f32[5,8,8,512]{3,2,1,0:T(8,128)S(1)}, u32[]{:S(2)}, u32[]{:S(2)}) collective-permute-start(f32[5,8,8,512]{3,2,1,0:T(8,128)} %get-tuple-element.22), channel_id=1, source_target_pairs={{0,124},{4,8},{8,4},{12,16},{16,12},{20,24},{24,20},{28,32},{32,28... | collective-permute-start | bytes 1966088 | tf_op jit(solution)/shard_map/ppermute | solution.py:588
  13.4 1.0 %collective-permute-start = (f32[15,8,512]{2,1,0:T(8,128)}, f32[15,8,512]{2,1,0:T(8,128)S(1)}, u32[]{:S(2)}, u32[]{:S(2)}) collective-permute-start(f32[15,8,512]{2,1,0:T(8,128)} %get-tuple-element.18), channel_id=1, source_target_pairs={{0,1},{1,0},{2,3},{3,2},{4,5},{5,4},{6,7},{7,6},{8,9},{9,8},{10,11... | collective-permute-start | bytes 737288 | tf_op jit(solution)/shard_map/ppermute | solution.py:588
  14.4 3.2 %collective-permute-start.2 = (f32[15,8,512]{2,1,0:T(8,128)}, f32[15,8,512]{2,1,0:T(8,128)S(1)}, u32[]{:S(2)}, u32[]{:S(2)}) collective-permute-start(f32[15,8,512]{2,1,0:T(8,128)} %get-tuple-element.19), channel_id=1, source_target_pairs={{0,3},{1,2},{2,1},{3,0},{4,7},{5,6},{6,5},{7,4},{8,11},{9,10},{10,... | collective-permute-start | bytes 737288 | tf_op jit(solution)/shard_map/ppermute | solution.py:588
  17.5 0.1 collective-permute-start.1
  17.7 3.8 %all-to-all-start = ((f32[32,1,128]{2,1,0:T(1,128)}), f32[32,1,128]{2,1,0:T(1,128)S(1)}, u32[]{:S(2)}, u32[]{:S(2)}) async-start(f32[32,1,128]{2,1,0:T(1,128)} %bitcast.19), calls=%async_computation | async-start | bytes 32768 | tf_op jit(solution)/shard_map/all_to_all | solution.py:616
  21.5 7.3 %side.1.token.base_hbm = f32[5,32,8,512]{3,2,1,0:T(8,128)} custom-call(s32[1,1024]{1,0:T(1,128)} %get-tuple-element.15.token.rank, f32[5,32,8,512]{3,2,1,0:T(8,128)} %flow_hbm.5), custom_call_target="tpu_custom_call" | custom-call | flops 1000 | bytes 1000 | tf_op jit(solution)/shard_map/side/pallas_call | solution.py:622
  28.8 6.5 %all-to-all-done = f32[32,1,128]{2,1,0:T(1,128)S(1)} async-done(((f32[32,1,128]{2,1,0:T(1,128)}), f32[32,1,128]{2,1,0:T(1,128)S(1)}, u32[]{:S(2)}, u32[]{:S(2)}) %all-to-all-start) | async-done | bytes 16416 | tf_op jit(solution)/shard_map/all_to_all | solution.py:616
  35.3 2.9 %collective-permute-done.1.twin = f32[3,8,512]{2,1,0:T(8,128)S(1)} collective-permute-done((f32[3,8,512]{2,1,0:T(8,128)}, f32[3,8,512]{2,1,0:T(8,128)S(1)}, u32[]{:S(2)}, u32[]{:S(2)}) %collective-permute-start.1) | collective-permute-done | bytes 49184 | tf_op jit(solution)/shard_map/ppermute | solution.py:588
  38.3 0.6 copy-done.6
  38.8 0.1 copy-done
  39.0 2.3 %surface.1 = (f32[2,8,512]{2,1,0:T(8,128)}, f32[2,8,512]{2,1,0:T(8,128)}, f32[1,1024]{1,0:T(1,128)}) custom-call(s32[2]{0:T(128)} %pad_add_fusion.place, f32[8]{0:T(128)} %conduct.1, f32[8]{0:T(128)} %rate.1, f32[5,32,8,512]{3,2,1,0:T(8,128)} %side.1.token.base_hbm, f32[32,128]{1,0:T(8,128)} %bitcast.13, f32[3,8,512]{2,1,0:T(8,128)} %get-tuple-element.17.own, ...), custom_call_target="tpu_custom_call" | custom-call | flops 1000 | bytes 1000 | tf_op jit(solution)/shard_map/surface/pallas_call | solution.py:630
  41.4 0.4 collective-permute-start.3
  41.8 0.4 collective-permute-start.4
  42.2 2.8 %collective-permute-start.5 = (f32[2,8,512]{2,1,0:T(8,128)}, f32[2,8,512]{2,1,0:T(8,128)S(1)}, u32[]{:S(2)}, u32[]{:S(2)}) collective-permute-start(f32[2,8,512]{2,1,0:T(8,128)} %get-tuple-element.20.dense_hbm.dense), channel_id=1, source_target_pairs={{0,3},{1,2},{2,1},{3,0},{4,7},{5,6},{6,5},{7,4},{8,11},{9,10},{10,... | collective-permute-start | bytes 98312 | tf_op jit(solution)/shard_map/ppermute | solution.py:588
  45.0 1.8 %answer.1 = f32[32,128]{1,0:T(8,128)} custom-call(f32[1,1024]{1,0:T(1,128)} %get-tuple-element.26.where_in, f32[2,8,512]{2,1,0:T(8,128)} %get-tuple-element.20.dense_hbm.dense), custom_call_target="tpu_custom_call" | custom-call | flops 1000 | bytes 1000 | tf_op jit(solution)/shard_map/answer/pallas_call | solution.py:637
  46.8 3.9 %all-to-all-start.1 = ((f32[32,1,128]{2,1,0:T(1,128)}), f32[32,1,128]{2,1,0:T(1,128)S(1)}, u32[]{:S(2)}, u32[]{:S(2)}) async-start(f32[32,1,128]{2,1,0:T(1,128)} %bitcast.14), calls=%async_computation.1 | async-start | bytes 32768 | tf_op jit(solution)/shard_map/all_to_all | solution.py:638
  50.8 0.5 copy-done.7
  51.4 0.3 copy-done.2
  51.6 0.2 copy-done.3
  51.8 8.2 %final.1 = (f32[5,32,8,512]{3,2,1,0:T(8,128)}, f32[32,8,512]{2,1,0:T(8,128)}) custom-call(s32[2]{0:T(128)} %pad_add_fusion.place, f32[2,8,512]{2,1,0:T(8,128)} %get-tuple-element.20.dense_hbm.dense, f32[2,8,512]{2,1,0:T(8,128)} %copy-done.7, f32[2,8,512]{2,1,0:T(8,128)} %copy-done.8, f32[2,8,512]{2,1,0:T(8,128)} %copy-done.9, ...), custom_call_target="tpu_custom_call" | custom-call | flops 1000 | bytes 1000 | tf_op jit(solution)/shard_map/final/pallas_call | solution.py:639
  60.0 0.6 copy-done.4
  60.6 2.0 %ablate.1 = f32[64,1024]{1,0:T(8,128)} custom-call(f32[8]{0:T(128)} %diffuse.1, f32[32,8,512]{2,1,0:T(8,128)} %get-tuple-element.13.token, s32[1,1024]{1,0:T(1,128)} %bitcast.16, s32[1,1024]{1,0:T(1,128)} %get-tuple-element.15.token.rank, s32[1,1024]{1,0:T(1,128)} %bitcast.18, f32[32,128]{1,0:T(8,128)} %bitcast.12, f32[64,1024]{1,0:T(8,128)} %temps.1), custom_call_target="tpu_custom_call" | custom-call | flops 1000 | bytes 1000 | tf_op jit(solution)/shard_map/ablate/pallas_call | solution.py:681
  (23 shorter events, 0.2 us)
Async XLA Ops:
  6.2 44.6 %collective-permute-start.6 = (f32[5,8,8,512]{3,2,1,0:T(8,128)}, f32[5,8,8,512]{3,2,1,0:T(8,128)S(1)}, u32[]{:S(2)}, u32[]{:S(2)}) collective-permute-start(f32[5,8,8,512]{3,2,1,0:T(8,128)} %get-tuple-element.22), channel_id=1, source_target_pairs={{0,124},{4,8},{8,4},{12,16},{16,12},{20,24},{24,20},{28,32},{32,28... | collective-permute-start | bytes 1966088 | tf_op jit(solution)/shard_map/ppermute | solution.py:588
  13.4 37.4 %collective-permute-start.7 = (f32[5,8,8,512]{3,2,1,0:T(8,128)}, f32[5,8,8,512]{3,2,1,0:T(8,128)S(1)}, u32[]{:S(2)}, u32[]{:S(2)}) collective-permute-start(f32[5,8,8,512]{3,2,1,0:T(8,128)} %get-tuple-element.23), channel_id=1, source_target_pairs={{0,4},{4,0},{8,12},{12,8},{16,20},{20,16},{24,28},{28,24},{32,36},... | collective-permute-start | bytes 1966088 | tf_op jit(solution)/shard_map/ppermute | solution.py:588
  13.4 24.8 %collective-permute-start = (f32[15,8,512]{2,1,0:T(8,128)}, f32[15,8,512]{2,1,0:T(8,128)S(1)}, u32[]{:S(2)}, u32[]{:S(2)}) collective-permute-start(f32[15,8,512]{2,1,0:T(8,128)} %get-tuple-element.18), channel_id=1, source_target_pairs={{0,1},{1,0},{2,3},{3,2},{4,5},{5,4},{6,7},{7,6},{8,9},{9,8},{10,11... | collective-permute-start | bytes 737288 | tf_op jit(solution)/shard_map/ppermute | solution.py:588
  14.4 23.9 %collective-permute-start.2 = (f32[15,8,512]{2,1,0:T(8,128)}, f32[15,8,512]{2,1,0:T(8,128)S(1)}, u32[]{:S(2)}, u32[]{:S(2)}) collective-permute-start(f32[15,8,512]{2,1,0:T(8,128)} %get-tuple-element.19), channel_id=1, source_target_pairs={{0,3},{1,2},{2,1},{3,0},{4,7},{5,6},{6,5},{7,4},{8,11},{9,10},{10,... | collective-permute-start | bytes 737288 | tf_op jit(solution)/shard_map/ppermute | solution.py:588
  17.5 20.7 %collective-permute-start.1 = (f32[3,8,512]{2,1,0:T(8,128)}, f32[3,8,512]{2,1,0:T(8,128)S(1)}, u32[]{:S(2)}, u32[]{:S(2)}) collective-permute-start(f32[3,8,512]{2,1,0:T(8,128)} %get-tuple-element.17.own), channel_id=1, source_target_pairs={{0,2},{1,3},{2,0},{3,1},{4,6},{5,7},{6,4},{7,5},{8,10},{9,11},{10,... | collective-permute-start | bytes 147464 | tf_op jit(solution)/shard_map/ppermute | solution.py:588
  17.7 17.6 %all-to-all-start = ((f32[32,1,128]{2,1,0:T(1,128)}), f32[32,1,128]{2,1,0:T(1,128)S(1)}, u32[]{:S(2)}, u32[]{:S(2)}) async-start(f32[32,1,128]{2,1,0:T(1,128)} %bitcast.19), calls=%async_computation | async-start | bytes 32768 | tf_op jit(solution)/shard_map/all_to_all | solution.py:616
  35.3 3.0 %copy-start.5 = (f32[32,1,128]{2,1,0:T(1,128)}, f32[32,1,128]{2,1,0:T(1,128)S(1)}, u32[]{:S(2)}) copy-start(f32[32,1,128]{2,1,0:T(1,128)S(1)} %all-to-all-done) | copy-start | bytes 49156
  38.2 0.6 copy-start.6
  38.2 0.7 %copy-start = (f32[15,8,512]{2,1,0:T(8,128)}, f32[15,8,512]{2,1,0:T(8,128)S(1)}, u32[]{:S(2)}) copy-start(f32[15,8,512]{2,1,0:T(8,128)S(1)} %collective-permute-done.core.core_hbm) | copy-start | bytes 737284
  38.2 0.8 %copy-start.1 = (f32[15,8,512]{2,1,0:T(8,128)}, f32[15,8,512]{2,1,0:T(8,128)S(1)}, u32[]{:S(2)}) copy-start(f32[15,8,512]{2,1,0:T(8,128)S(1)} %collective-permute-done.2.cross.cross_hbm) | copy-start | bytes 737284
  41.4 9.3 %collective-permute-start.3 = (f32[2,8,512]{2,1,0:T(8,128)}, f32[2,8,512]{2,1,0:T(8,128)S(1)}, u32[]{:S(2)}, u32[]{:S(2)}) collective-permute-start(f32[2,8,512]{2,1,0:T(8,128)} %get-tuple-element.20.dense_hbm.dense), channel_id=1, source_target_pairs={{0,1},{1,0},{2,3},{3,2},{4,5},{5,4},{6,7},{7,6},{8,9},{9,8},{10,11... | collective-permute-start | bytes 98312 | tf_op jit(solution)/shard_map/ppermute | solution.py:588
  41.8 8.9 %collective-permute-start.4 = (f32[2,8,512]{2,1,0:T(8,128)}, f32[2,8,512]{2,1,0:T(8,128)S(1)}, u32[]{:S(2)}, u32[]{:S(2)}) collective-permute-start(f32[2,8,512]{2,1,0:T(8,128)} %get-tuple-element.20.dense_hbm.dense), channel_id=1, source_target_pairs={{0,2},{1,3},{2,0},{3,1},{4,6},{5,7},{6,4},{7,5},{8,10},{9,11},{10,... | collective-permute-start | bytes 98312 | tf_op jit(solution)/shard_map/ppermute | solution.py:588
  42.2 8.5 %collective-permute-start.5 = (f32[2,8,512]{2,1,0:T(8,128)}, f32[2,8,512]{2,1,0:T(8,128)S(1)}, u32[]{:S(2)}, u32[]{:S(2)}) collective-permute-start(f32[2,8,512]{2,1,0:T(8,128)} %get-tuple-element.20.dense_hbm.dense), channel_id=1, source_target_pairs={{0,3},{1,2},{2,1},{3,0},{4,7},{5,6},{6,5},{7,4},{8,11},{9,10},{10,... | collective-permute-start | bytes 98312 | tf_op jit(solution)/shard_map/ppermute | solution.py:588
  46.8 13.2 %all-to-all-start.1 = ((f32[32,1,128]{2,1,0:T(1,128)}), f32[32,1,128]{2,1,0:T(1,128)S(1)}, u32[]{:S(2)}, u32[]{:S(2)}) async-start(f32[32,1,128]{2,1,0:T(1,128)} %bitcast.14), calls=%async_computation.1 | async-start | bytes 32768 | tf_op jit(solution)/shard_map/all_to_all | solution.py:638
  50.7 0.6 copy-start.7
  50.7 0.6 copy-start.8
  50.8 0.6 copy-start.9
  50.8 0.8 %copy-start.2 = (f32[5,8,8,512]{3,2,1,0:T(8,128)}, f32[5,8,8,512]{3,2,1,0:T(8,128)S(1)}, u32[]{:S(2)}) copy-start(f32[5,8,8,512]{3,2,1,0:T(8,128)S(1)} %collective-permute-done.6.far_hbm) | copy-start | bytes 1966084
  50.8 1.0 %copy-start.3 = (f32[5,8,8,512]{3,2,1,0:T(8,128)}, f32[5,8,8,512]{3,2,1,0:T(8,128)S(1)}, u32[]{:S(2)}) copy-start(f32[5,8,8,512]{3,2,1,0:T(8,128)S(1)} %collective-permute-done.7.pair_hbm) | copy-start | bytes 1966084
  60.0 0.6 copy-start.4

commit v4 on v3

--- a/solution.py
+++ b/solution.py
@@ -77,7 +77,6 @@
 
 
 def begin_kernel(
-    place,
     cell_hbm,
     zone_hbm,
     temps_hbm,
@@ -86,7 +85,7 @@
     outgoing,
     rank_out,
     core_wall,
-    cross_wall,
+    cross_layers,
     wall_fields,
     pair_hbm,
     cross_hbm,
@@ -100,8 +99,8 @@
     in_sem,
     out_sem,
 ):
-    even = place[0] % 2 == 0
-    parity = place[1]
+    even = lax.axis_index("wall") % 2 == 0
+    parity = lax.axis_index("surf") % 2
     small = [
         pltpu.make_async_copy(source, target, small_sem.at[index])
         for index, (source, target) in enumerate(
@@ -177,7 +176,7 @@
     layers += [(spacing[30 + n], spacing[n]) for n in range(2)]
     for index, (top, bottom) in enumerate(layers):
         core_wall[index] = jnp.where(even, top, bottom)
-        cross_wall[index] = jnp.where(even, bottom, top)
+        cross_layers[index] = jnp.where(even, bottom, top)
     inverse, vx, vy, vz, pressure = primitives(*[flow[m, 0] for m in range(5)])
     film = 2.0 / spacing[0]
     temp = pressure * inverse + recovery * (vx * vx + vy * vy + vz * vz)
@@ -186,15 +185,14 @@
         total = total + spacing[k]
     for index, value in enumerate((film, temp, total)):
         core_wall[12 + index] = value
-        cross_wall[12 + index] = value
         wall_fields[index] = value
     wait_all(stores)
 
 
 def surface_kernel(
-    place, conduct, rate, token, arrived, own, core, twin, cross, dense, sums, where_out
+    conduct, rate, token, arrived, own, core, twin, cross, dense, sums, where_out
 ):
-    wall = place[0]
+    wall = lax.axis_index("wall")
     received = arrived[...]
     pieces = jnp.concatenate(split3(received), axis=0)
     lane = iota((128, 1024), 1) % 32
@@ -222,12 +220,12 @@
         return jnp.where(
             wall == 0,
             own[f],
-            jnp.where(wall == 1, core[12 + f], jnp.where(wall == 2, twin[f], cross[12 + f])),
+            jnp.where(wall == 1, core[12 + f], jnp.where(wall == 2, twin[f], cross[f])),
         )
 
-    sums[0] = (own[2] + core[14]) + (twin[2] + cross[14])
+    sums[0] = (own[2] + core[14]) + (twin[2] + cross[2])
     below = jnp.where(wall % 2 == 1, core[14], 0.0)
-    sums[1] = below + jnp.where(wall >= 2, twin[2] + cross[14], 0.0)
+    sums[1] = below + jnp.where(wall >= 2, twin[2] + cross[2], 0.0)
     film = from_bottom(0)
     recover = from_bottom(1)
     cond = jnp.zeros((8, 512), F32)
@@ -288,7 +286,8 @@
 TWELFTH = time_step / 12.0
 
 
-def side_kernel(token, flow_hbm, base_hbm, flow, base, in_sem, out_sem):
+def side_kernel(token, flow_hbm, base_hbm, done, flow, base, in_sem, out_sem):
+    done[...] = jnp.zeros_like(done)
     loads = [
         pltpu.make_async_copy(chunk_of(flow_hbm, c), chunk_of(flow, c), in_sem.at[c]) for c in range(4)
     ]
@@ -347,7 +346,6 @@
 
 
 def final_kernel(
-    place,
     dense_hbm,
     dense_1_hbm,
     dense_2_hbm,
@@ -363,6 +361,7 @@
     pair_hbm,
     out_hbm,
     shift_hbm,
+    done,
     dense,
     sums,
     walls,
@@ -382,8 +381,8 @@
     out_sem,
     shift_sem,
 ):
-    wall = place[0]
-    parity = place[1]
+    wall = lax.axis_index("wall")
+    parity = lax.axis_index("surf") % 2
     odd_wall = wall % 2
     small = [
         pltpu.make_async_copy(source, target, small_sem.at[index])
@@ -395,12 +394,13 @@
                 (dense_3_hbm, dense.at[3]),
                 (sums_hbm, sums),
                 (core_hbm.at[pl.ds(0, 12)], walls.at[1 - odd_wall]),
-                (cross_hbm.at[pl.ds(0, 12)], walls.at[odd_wall]),
+                (cross_hbm, walls.at[odd_wall]),
                 (kinds_hbm, kinds),
                 (spacing_hbm, thick.at[pl.ds(2, 32)]),
             )
         )
     ]
+    done[...] = jnp.zeros_like(done)
     start_all(small)
 
     def flow_load(c):
@@ -549,11 +549,12 @@
 
 SCALARS = pl.BlockSpec(memory_space=pltpu.SMEM)
 ANY = pl.BlockSpec(memory_space=pl.ANY)
+HBM = pl.BlockSpec(memory_space=pltpu.HBM)
 VMEM = pl.BlockSpec(memory_space=pltpu.VMEM)
 
 
-def params():
-    return pltpu.CompilerParams(vmem_limit_bytes=62 * 1024 * 1024)
+def params(grant):
+    return pltpu.CompilerParams(vmem_limit_bytes=grant * 1024 * 1024)
 
 
 def cost():
@@ -564,9 +565,14 @@
     return jax.ShapeDtypeStruct(shape, dtype)
 
 
-def call(kernel, name, out_shape, **options):
+def call(kernel, name, out_shape, grant=62, **options):
     return pl.pallas_call(
-        kernel, out_shape=out_shape, name=name, compiler_params=params(), cost_estimate=cost(), **options
+        kernel,
+        out_shape=out_shape,
+        name=name,
+        compiler_params=params(grant),
+        cost_estimate=cost(),
+        **options,
     )
 
 
@@ -580,26 +586,25 @@
 
 def shards(flow_state, spacing, bc_kind, cell_of, zone_id, abl_temp, conduct, diffuse, rate):
     surf_count = lax.axis_size("surf")
-    place = jnp.stack([lax.axis_index("wall"), lax.axis_index("surf") % 2]).astype(jnp.int32)
     cells = cell_of.reshape(1, 1024)
     zones = zone_id.reshape(1, 1024)
 
     def swap(value, axis, partner):
         return lax.ppermute(value, axis, [(i, partner(i)) for i in range(lax.axis_size(axis))])
 
-    outgoing, rank, core_wall, cross_wall, wall_fields, pair_side, cross_side = call(
+    outgoing, rank, core_wall, cross_layers, wall_fields, pair_side, cross_side = call(
         begin_kernel,
         "begin",
         (
             struct(32, 128),
             struct(1, 1024, dtype=jnp.int32),
             struct(15, 8, 512),
-            struct(15, 8, 512),
+            struct(12, 8, 512),
             struct(3, 8, 512),
             struct(5, 8, 8, 512),
             struct(5, 8, 8, 512),
         ),
-        in_specs=[SCALARS] + [ANY] * 5,
+        in_specs=[ANY] * 5,
         out_specs=(VMEM,) * 5 + (ANY,) * 2,
         scratch_shapes=[
             pltpu.VMEM((1, 1024), jnp.int32),
@@ -612,36 +617,40 @@
             copies(4),
             copies(2, 4),
         ],
-    )(place, cells, zones, abl_temp, spacing, flow_state)
+    )(cells, zones, abl_temp, spacing, flow_state)
     arrived = lax.all_to_all(outgoing, "surf", split_axis=0, concat_axis=0, tiled=True)
-    cross = swap(cross_wall, "wall", lambda i: i ^ 3)
+    cross = swap(wall_fields, "wall", lambda i: i ^ 3)
     twin = swap(wall_fields, "wall", lambda i: i ^ 2)
     core = swap(core_wall, "wall", lambda i: i ^ 1)
     far = swap(cross_side, "surf", lambda i: (i - 1 + 2 * (i % 2)) % surf_count)
     pair = swap(pair_side, "surf", lambda i: i ^ 1)
-    base = call(
+    base, side_done = call(
         side_kernel,
         "side",
-        struct(5, 32, 8, 512),
-        in_specs=[ANY, ANY],
-        out_specs=ANY,
+        (struct(5, 32, 8, 512), struct(8, 128)),
+        in_specs=[ANY, HBM],
+        out_specs=(HBM, VMEM),
         scratch_shapes=[scratch(5, 32, 8, 512), scratch(5, 32, 8, 512), copies(4), copies(4)],
     )(rank, flow_state)
     dense, sums, where_cells = call(
         surface_kernel,
         "surface",
         (struct(2, 8, 512), struct(2, 8, 512), struct(1, 1024)),
-        in_specs=[SCALARS] * 3 + [ANY] + [VMEM] * 5,
-    )(place, conduct, rate, base, arrived, wall_fields, core, twin, cross)
+        grant=32,
+        in_specs=[SCALARS] * 2 + [ANY] + [VMEM] * 5,
+    )(conduct, rate, side_done, arrived, wall_fields, core, twin, cross)
+    cross_layers, where_cells = lax.optimization_barrier((cross_layers, where_cells))
+    layers = lax.ppermute(cross_layers, "wall", [(1, 2), (2, 1)])
     dense_1, dense_2, dense_3 = (swap(dense, "wall", lambda i, by=by: i ^ by) for by in (1, 2, 3))
-    returned = call(return_kernel, "answer", struct(32, 128))(where_cells, dense)
+    returned = call(return_kernel, "answer", struct(32, 128), grant=32)(where_cells, dense)
     back = lax.all_to_all(returned, "surf", split_axis=0, concat_axis=0, tiled=True)
-    state_next, node_shift = call(
+    state_next, node_shift, final_done = call(
         final_kernel,
         "final",
-        (struct(5, 32, 8, 512), struct(32, 8, 512)),
-        in_specs=[SCALARS] + [ANY] * 13,
-        out_specs=(ANY, ANY),
+        (struct(5, 32, 8, 512), struct(32, 8, 512), struct(8, 128)),
+        grant=52,
+        in_specs=[ANY] * 8 + [HBM] * 5,
+        out_specs=(HBM, HBM, VMEM),
         scratch_shapes=[
             scratch(4, 2, 8, 512),
             scratch(2, 8, 512),
@@ -663,14 +672,13 @@
             copies(4),
         ],
     )(
-        place,
         dense,
         dense_1,
         dense_2,
         dense_3,
         sums,
         core,
-        cross,
+        layers,
         bc_kind,
         spacing,
         flow_state,
@@ -682,8 +690,9 @@
         ablate_kernel,
         "ablate",
         struct(64, 1024),
+        grant=32,
         in_specs=[SCALARS, ANY] + [VMEM] * 5,
-    )(diffuse, node_shift, cells, rank, zones, back, abl_temp)
+    )(diffuse, final_done, cells, rank, zones, back, abl_temp)
     return (state_next, node_shift, ablator_next)
 
 

time: 63 us -> 56.8 us (0.902)
  starting transfers between devices: 22.8 us -> 27.4 us
  waiting for transfers between devices: 9.43 us -> 4.92 us
  Pallas kernels: 26.5 us -> 22.6 us
  local copies, waits for them, and re-layouts: 2.4 us -> 0.73 us
  other arithmetic: 0.64 us -> 0 us
    all_to_all x1, waiting for transfers between devices: 6.48 us -> 1.76 us  [shards(): lax.all_to_all(outgoing, 'surf', split_axis=0, concat_axis=0, tiled=True)]
    ppermute x0 -> x1, starting transfers between devices: none -> 2.64 us  [shards(): layers = lax.ppermute(cross_layers, 'wall', [(1, 2), (2, 1)])]
    pallas_call x4, Pallas kernels: 19.2 us -> 17.1 us  [the longest x1 7.87 us: shards(): call(side_kernel, 'side', (struct(5, 32, 8, 512), struct(8, 128)), in_spe...]
    all_to_all x1, starting transfers between devices: 3.88 us -> 5.69 us  [shards(): lax.all_to_all(returned, 'surf', split_axis=0, concat_axis=0, tiled=True)]
    unnamed x20 -> x24, local copies, waits for them, and re-layouts: 2.4 us -> 0.73 us
    pallas_call x1, Pallas kernels: 2.35 us -> 1.14 us  [shards(): call(surface_kernel, 'surface', (struct(2, 8, 512), struct(2, 8, 512), st...]
    another operation x1 -> x0, other arithmetic: 0.64 us -> none  [shards(): jnp.stack([lax.axis_index('wall'), lax.axis_index('surf') % 2])]
  transfers between devices with their start and end apart: 10 -> 11, of which waited for: 2 -> 4; matrix products, arithmetic and copies ran while one was open for 0% -> 0% of each run, Pallas kernels for 31% -> 30%
where the time goes in v4:
time: 56.8 us; the launch traced here: 56.5 us
  starting transfers between devices  27.4 us (48%)
  Pallas kernels  22.6 us (40%)
  waiting for transfers between devices  4.92 us (9%)
  between operations  0.89 us (2%)
  local copies, waits for them, and re-layouts  0.73 us (1%)
    ppermute x8, starting transfers between devices, swap(): lax.ppermute(value, axis, [(i, partner(i)) for i in range(lax.axis_size(a...  15.3 us
    pallas_call x1, Pallas kernels, shards(): call(side_kernel, 'side', (struct(5, 32, 8, 512), struct(8, 128)), in_spe...  7.87 us
    pallas_call x1, Pallas kernels, shards(): call(final_kernel, 'final', (struct(5, 32, 8, 512), struct(32, 8, 512), s...  6.7 us
    all_to_all x1, starting transfers between devices, shards(): lax.all_to_all(returned, 'surf', split_axis=0, concat_axis=0, tiled=True)  5.69 us
    pallas_call x1, Pallas kernels, shards(): call(begin_kernel, 'begin', (struct(32, 128), struct(1, 1024, dtype=jnp.i...  4.31 us
    all_to_all x1, starting transfers between devices, shards(): lax.all_to_all(outgoing, 'surf', split_axis=0, concat_axis=0, tiled=True)  3.79 us
    ppermute x8, waiting for transfers between devices, swap(): lax.ppermute(value, axis, [(i, partner(i)) for i in range(lax.axis_size(a...  2.93 us
    ppermute x1, starting transfers between devices, shards(): layers = lax.ppermute(cross_layers, 'wall', [(1, 2), (2, 1)])  2.64 us
  transfers between devices with their start and end apart: 11, of which 4 were waited for; matrix products, arithmetic and copies ran while one was open for 0% of the time, Pallas kernels for 30%

profile of v4, /device:TPU:1, one launch (start us, length us, event | category | flops | bytes accessed | tf_op | source)
XLA Modules:
  0.0 56.5 jit_solution(8234964603406672736)
XLA Ops:
  0.7 4.3 %begin.1 = (f32[32,128]{1,0:T(8,128)}, s32[1,1024]{1,0:T(1,128)}, f32[15,8,512]{2,1,0:T(8,128)}, f32[12,8,512]{2,1,0:T(8,128)}, f32[3,8,512]{2,1,0:T(8,128)}, /*...) custom-call(s32[1,1024]{1,0:T(1,128)} %bitcast.12, s32[1,1024]{1,0:T(1,128)} %bitcast.14, f32[64,1024]{1,0:T(8,128)} %temps.1, ...), custom_call_target="tpu_custom_call" | custom-call | flops 1000 | bytes 1000 | tf_op jit(solution)/shard_map/begin/pallas_call | solution.py:595
  5.0 0.0 copy-start.11
  5.0 7.2 %collective-permute-start.7 = (f32[5,8,8,512]{3,2,1,0:T(8,128)}, f32[5,8,8,512]{3,2,1,0:T(8,128)S(1)}, u32[]{:S(2)}, u32[]{:S(2)}) collective-permute-start(f32[5,8,8,512]{3,2,1,0:T(8,128)} %get-tuple-element.31), channel_id=1, source_target_pairs={{0,124},{4,8},{8,4},{12,16},{16,12},{20,24},{24,20},{28,32},{32,28... | collective-permute-start | bytes 1966088 | tf_op jit(solution)/shard_map/ppermute | solution.py:593
  12.2 1.0 %collective-permute-start = (f32[15,8,512]{2,1,0:T(8,128)}, f32[15,8,512]{2,1,0:T(8,128)S(1)}, u32[]{:S(2)}, u32[]{:S(2)}) collective-permute-start(f32[15,8,512]{2,1,0:T(8,128)} %get-tuple-element.24), channel_id=1, source_target_pairs={{0,1},{1,0},{2,3},{3,2},{4,5},{5,4},{6,7},{7,6},{8,9},{9,8},{10,11... | collective-permute-start | bytes 737288 | tf_op jit(solution)/shard_map/ppermute | solution.py:593
  13.2 3.3 %collective-permute-start.1 = (f32[3,8,512]{2,1,0:T(8,128)}, f32[3,8,512]{2,1,0:T(8,128)S(1)}, u32[]{:S(2)}, u32[]{:S(2)}) collective-permute-start(f32[3,8,512]{2,1,0:T(8,128)} %get-tuple-element.23.own), channel_id=1, source_target_pairs={{0,2},{1,3},{2,0},{3,1},{4,6},{5,7},{6,4},{7,5},{8,10},{9,11},{10,... | collective-permute-start | bytes 147464 | tf_op jit(solution)/shard_map/ppermute | solution.py:593
  16.5 3.8 %all-to-all-start = ((f32[32,1,128]{2,1,0:T(1,128)}), f32[32,1,128]{2,1,0:T(1,128)S(1)}, u32[]{:S(2)}, u32[]{:S(2)}) async-start(f32[32,1,128]{2,1,0:T(1,128)} %bitcast.16), calls=%async_computation | async-start | bytes 32768 | tf_op jit(solution)/shard_map/all_to_all | solution.py:621
  20.3 7.9 %side.1 = (f32[5,32,8,512]{3,2,1,0:T(8,128)}, f32[8,128]{1,0:T(8,128)}) custom-call(s32[1,1024]{1,0:T(1,128)} %get-tuple-element.20.token.rank, f32[5,32,8,512]{3,2,1,0:T(8,128)} %flow_hbm.5), custom_call_target="tpu_custom_call" | custom-call | flops 1000 | bytes 1000 | tf_op jit(solution)/shard_map/side/pallas_call | solution.py:627
  28.2 1.8 %all-to-all-done = f32[32,1,128]{2,1,0:T(1,128)S(1)} async-done(((f32[32,1,128]{2,1,0:T(1,128)}), f32[32,1,128]{2,1,0:T(1,128)S(1)}, u32[]{:S(2)}, u32[]{:S(2)}) %all-to-all-start) | async-done | bytes 16416 | tf_op jit(solution)/shard_map/all_to_all | solution.py:621
  29.9 1.9 %collective-permute-done.1.twin = f32[3,8,512]{2,1,0:T(8,128)S(1)} collective-permute-done((f32[3,8,512]{2,1,0:T(8,128)}, f32[3,8,512]{2,1,0:T(8,128)S(1)}, u32[]{:S(2)}, u32[]{:S(2)}) %collective-permute-start.1) | collective-permute-done | bytes 49184 | tf_op jit(solution)/shard_map/ppermute | solution.py:593
  31.8 1.1 %collective-permute-done.2.cross = f32[3,8,512]{2,1,0:T(8,128)S(1)} collective-permute-done((f32[3,8,512]{2,1,0:T(8,128)}, f32[3,8,512]{2,1,0:T(8,128)S(1)}, u32[]{:S(2)}, u32[]{:S(2)}) %collective-permute-start.2) | collective-permute-done | bytes 49184 | tf_op jit(solution)/shard_map/ppermute | solution.py:593
  32.9 0.7 %copy-done.7 = f32[8,128]{1,0:T(8,128)S(1)} copy-done((f32[8,128]{1,0:T(8,128)S(1)}, f32[8,128]{1,0:T(8,128)}, u32[]{:S(2)}) %copy-start.7) | copy-done | bytes 4120
  33.5 1.1 %surface.1 = (f32[2,8,512]{2,1,0:T(8,128)S(1)}, f32[2,8,512]{2,1,0:T(8,128)S(1)}, f32[1,1024]{1,0:T(1,128)S(1)}) custom-call(f32[8]{0:T(128)S(1)} %copy-done.8, f32[8]{0:T(128)S(1)} %copy-done.9, f32[8,128]{1,0:T(8,128)S(1)} %copy-done.7, f32[32,128]{1,0:T(8,128)S(1)} %bitcast.11, f32[3,8,512]{2,1,0:T(8,128)S(1)} %copy-done.2, ...), custom_call_target="tpu_custom_call" | custom-call | flops 1000 | bytes 1000 | tf_op jit(solution)/shard_map/surface/pallas_call | solution.py:635
  34.7 2.6 %collective-permute-start.6 = (f32[12,8,512]{2,1,0:T(8,128)S(1)}, f32[12,8,512]{2,1,0:T(8,128)S(1)}, u32[]{:S(2)}, u32[]{:S(2)}) collective-permute-start(f32[12,8,512]{2,1,0:T(8,128)S(1)} %copy-done.11), channel_id=1, source_target_pairs={{1,2},{2,1},{5,6},{6,5},{9,10},{10,9},{13,14},{14,13},{17,18},{18,... | collective-permute-start | bytes 589832 | tf_op jit(solution)/shard_map/ppermute | solution.py:643
  37.3 0.1 collective-permute-start.3
  37.4 2.6 %collective-permute-start.4 = (f32[2,8,512]{2,1,0:T(8,128)S(1)}, f32[2,8,512]{2,1,0:T(8,128)S(1)}, u32[]{:S(2)}, u32[]{:S(2)}) collective-permute-start(f32[2,8,512]{2,1,0:T(8,128)S(1)} %get-tuple-element.25.dense_hbm.dense), channel_id=1, source_target_pairs={{0,2},{1,3},{2,0},{3,1},{4,6},{5,7},{6,4},{7,5},{8,10},{9,11},{10,... | collective-permute-start | bytes 98312 | tf_op jit(solution)/shard_map/ppermute | solution.py:593
  40.1 1.1 %collective-permute-start.5 = (f32[2,8,512]{2,1,0:T(8,128)S(1)}, f32[2,8,512]{2,1,0:T(8,128)S(1)}, u32[]{:S(2)}, u32[]{:S(2)}) collective-permute-start(f32[2,8,512]{2,1,0:T(8,128)S(1)} %get-tuple-element.25.dense_hbm.dense), channel_id=1, source_target_pairs={{0,3},{1,2},{2,1},{3,0},{4,7},{5,6},{6,5},{7,4},{8,11},{9,10},{10,... | collective-permute-start | bytes 98312 | tf_op jit(solution)/shard_map/ppermute | solution.py:593
  41.2 1.0 %answer.1 = f32[32,128]{1,0:T(8,128)} custom-call(f32[1,1024]{1,0:T(1,128)S(1)} %get-tuple-element.36.where_in, f32[2,8,512]{2,1,0:T(8,128)S(1)} %get-tuple-element.25.dense_hbm.dense), custom_call_target="tpu_custom_call" | custom-call | flops 1000 | bytes 1000 | tf_op jit(solution)/shard_map/answer/pallas_call | solution.py:645
  42.2 5.7 %all-to-all-start.1 = ((f32[32,1,128]{2,1,0:T(1,128)}), f32[32,1,128]{2,1,0:T(1,128)S(1)}, u32[]{:S(2)}, u32[]{:S(2)}) async-start(f32[32,1,128]{2,1,0:T(1,128)} %bitcast.6), calls=%async_computation.1 | async-start | bytes 32768 | tf_op jit(solution)/shard_map/all_to_all | solution.py:646
  47.9 0.0 copy-start.1
  48.0 0.0 copy-start.5
  48.0 0.0 copy-start.10
  48.0 6.7 %final.1 = (f32[5,32,8,512]{3,2,1,0:T(8,128)}, f32[32,8,512]{2,1,0:T(8,128)}, f32[8,128]{1,0:T(8,128)S(1)}) custom-call(f32[2,8,512]{2,1,0:T(8,128)S(1)} %get-tuple-element.25.dense_hbm.dense, f32[2,8,512]{2,1,0:T(8,128)S(1)} %collective-permute-done.3.dense_1_hbm, f32[2,8,512]{2,1,0:T(8,128)S(1)} %collective-permute-done.4.dense_2_hbm, ...), custom_call_target="tpu_custom_call" | custom-call | flops 1000 | bytes 1000 | tf_op jit(solution)/shard_map/final/pallas_call | solution.py:647
  54.7 0.2 all-to-all-done.1
  55.0 1.5 %ablate.1 = f32[64,1024]{1,0:T(8,128)} custom-call(f32[8]{0:T(128)S(1)} %copy-done.10, f32[8,128]{1,0:T(8,128)S(1)} %get-tuple-element.35.token, s32[1,1024]{1,0:T(1,128)S(1)} %bitcast.13, s32[1,1024]{1,0:T(1,128)S(1)} %copy-done.6, s32[1,1024]{1,0:T(1,128)S(1)} %bitcast.15, f32[32,128]{1,0:T(8,128)S(1)} %bitcast.10, f32[64,1024]{1,0:T(8,128)S(1)} %copy-done.1), custom_call_target="tpu_custom_call" | custom-call | flops 1000 | bytes 1000 | tf_op jit(solution)/shard_map/ablate/pallas_call | solution.py:689
  (28 shorter events, 0.1 us)
Async XLA Ops:
  0.6 32.2 %copy-start.8 = (f32[8]{0:T(128)S(1)}, f32[8]{0:T(128)}, u32[]{:S(2)}) copy-start(f32[8]{0:T(128)} %conduct.1) | copy-start | bytes 100
  0.6 32.2 %copy-start.9 = (f32[8]{0:T(128)S(1)}, f32[8]{0:T(128)}, u32[]{:S(2)}) copy-start(f32[8]{0:T(128)} %rate.1) | copy-start | bytes 100
  0.7 47.3 %copy-start = (f32[32,8,512]{2,1,0:T(8,128)S(1)}, f32[32,8,512]{2,1,0:T(8,128)}, u32[]{:S(2)}) copy-start(f32[32,8,512]{2,1,0:T(8,128)} %spacing_hbm.3) | copy-start | bytes 1572868
  0.7 47.3 %copy-start.3 = (s32[8,512]{1,0:T(8,128)S(1)}, s32[8,512]{1,0:T(8,128)}, u32[]{:S(2)}) copy-start(s32[8,512]{1,0:T(8,128)} %kinds_hbm.1) | copy-start | bytes 49156
  5.0 27.9 %copy-start.2 = (f32[3,8,512]{2,1,0:T(8,128)S(1)}, f32[3,8,512]{2,1,0:T(8,128)}, u32[]{:S(2)}) copy-start(f32[3,8,512]{2,1,0:T(8,128)} %get-tuple-element.23.own) | copy-start | bytes 147460
  5.0 29.7 %copy-start.11 = (f32[12,8,512]{2,1,0:T(8,128)S(1)}, f32[12,8,512]{2,1,0:T(8,128)}, u32[]{:S(2)}) copy-start(f32[12,8,512]{2,1,0:T(8,128)} %get-tuple-element.29) | copy-start | bytes 589828
  5.0 42.9 %collective-permute-start.7 = (f32[5,8,8,512]{3,2,1,0:T(8,128)}, f32[5,8,8,512]{3,2,1,0:T(8,128)S(1)}, u32[]{:S(2)}, u32[]{:S(2)}) collective-permute-start(f32[5,8,8,512]{3,2,1,0:T(8,128)} %get-tuple-element.31), channel_id=1, source_target_pairs={{0,124},{4,8},{8,4},{12,16},{16,12},{20,24},{24,20},{28,32},{32,28... | collective-permute-start | bytes 1966088 | tf_op jit(solution)/shard_map/ppermute | solution.py:593
  12.2 35.7 %collective-permute-start.8 = (f32[5,8,8,512]{3,2,1,0:T(8,128)}, f32[5,8,8,512]{3,2,1,0:T(8,128)}, u32[]{:S(2)}, u32[]{:S(2)}) collective-permute-start(f32[5,8,8,512]{3,2,1,0:T(8,128)} %get-tuple-element.32), channel_id=1, source_target_pairs={{0,4},{4,0},{8,12},{12,8},{16,20},{20,16},{24,28},{28,24},{32,36},... | collective-permute-start | bytes 1966088 | tf_op jit(solution)/shard_map/ppermute | solution.py:593
  12.2 20.6 %collective-permute-start = (f32[15,8,512]{2,1,0:T(8,128)}, f32[15,8,512]{2,1,0:T(8,128)S(1)}, u32[]{:S(2)}, u32[]{:S(2)}) collective-permute-start(f32[15,8,512]{2,1,0:T(8,128)} %get-tuple-element.24), channel_id=1, source_target_pairs={{0,1},{1,0},{2,3},{3,2},{4,5},{5,4},{6,7},{7,6},{8,9},{9,8},{10,11... | collective-permute-start | bytes 737288 | tf_op jit(solution)/shard_map/ppermute | solution.py:593
  13.2 18.6 %collective-permute-start.1 = (f32[3,8,512]{2,1,0:T(8,128)}, f32[3,8,512]{2,1,0:T(8,128)S(1)}, u32[]{:S(2)}, u32[]{:S(2)}) collective-permute-start(f32[3,8,512]{2,1,0:T(8,128)} %get-tuple-element.23.own), channel_id=1, source_target_pairs={{0,2},{1,3},{2,0},{3,1},{4,6},{5,7},{6,4},{7,5},{8,10},{9,11},{10,... | collective-permute-start | bytes 147464 | tf_op jit(solution)/shard_map/ppermute | solution.py:593
  16.5 16.4 %collective-permute-start.2 = (f32[3,8,512]{2,1,0:T(8,128)}, f32[3,8,512]{2,1,0:T(8,128)S(1)}, u32[]{:S(2)}, u32[]{:S(2)}) collective-permute-start(f32[3,8,512]{2,1,0:T(8,128)} %get-tuple-element.23.own), channel_id=1, source_target_pairs={{0,3},{1,2},{2,1},{3,0},{4,7},{5,6},{6,5},{7,4},{8,11},{9,10},{10,... | collective-permute-start | bytes 147464 | tf_op jit(solution)/shard_map/ppermute | solution.py:593
  16.5 13.4 %all-to-all-start = ((f32[32,1,128]{2,1,0:T(1,128)}), f32[32,1,128]{2,1,0:T(1,128)S(1)}, u32[]{:S(2)}, u32[]{:S(2)}) async-start(f32[32,1,128]{2,1,0:T(1,128)} %bitcast.16), calls=%async_computation | async-start | bytes 32768 | tf_op jit(solution)/shard_map/all_to_all | solution.py:621
  32.9 0.7 %copy-start.7 = (f32[8,128]{1,0:T(8,128)S(1)}, f32[8,128]{1,0:T(8,128)}, u32[]{:S(2)}) copy-start(f32[8,128]{1,0:T(8,128)} %get-tuple-element.21.token) | copy-start | bytes 12292
  34.7 13.2 %collective-permute-start.6 = (f32[12,8,512]{2,1,0:T(8,128)S(1)}, f32[12,8,512]{2,1,0:T(8,128)S(1)}, u32[]{:S(2)}, u32[]{:S(2)}) collective-permute-start(f32[12,8,512]{2,1,0:T(8,128)S(1)} %copy-done.11), channel_id=1, source_target_pairs={{1,2},{2,1},{5,6},{6,5},{9,10},{10,9},{13,14},{14,13},{17,18},{18,... | collective-permute-start | bytes 589832 | tf_op jit(solution)/shard_map/ppermute | solution.py:643
  37.3 2.7 %collective-permute-start.3 = (f32[2,8,512]{2,1,0:T(8,128)S(1)}, f32[2,8,512]{2,1,0:T(8,128)S(1)}, u32[]{:S(2)}, u32[]{:S(2)}) collective-permute-start(f32[2,8,512]{2,1,0:T(8,128)S(1)} %get-tuple-element.25.dense_hbm.dense), channel_id=1, source_target_pairs={{0,1},{1,0},{2,3},{3,2},{4,5},{5,4},{6,7},{7,6},{8,9},{9,8},{10,11... | collective-permute-start | bytes 98312 | tf_op jit(solution)/shard_map/ppermute | solution.py:593
  37.4 10.4 %collective-permute-start.4 = (f32[2,8,512]{2,1,0:T(8,128)S(1)}, f32[2,8,512]{2,1,0:T(8,128)S(1)}, u32[]{:S(2)}, u32[]{:S(2)}) collective-permute-start(f32[2,8,512]{2,1,0:T(8,128)S(1)} %get-tuple-element.25.dense_hbm.dense), channel_id=1, source_target_pairs={{0,2},{1,3},{2,0},{3,1},{4,6},{5,7},{6,4},{7,5},{8,10},{9,11},{10,... | collective-permute-start | bytes 98312 | tf_op jit(solution)/shard_map/ppermute | solution.py:593
  40.1 7.8 %collective-permute-start.5 = (f32[2,8,512]{2,1,0:T(8,128)S(1)}, f32[2,8,512]{2,1,0:T(8,128)S(1)}, u32[]{:S(2)}, u32[]{:S(2)}) collective-permute-start(f32[2,8,512]{2,1,0:T(8,128)S(1)} %get-tuple-element.25.dense_hbm.dense), channel_id=1, source_target_pairs={{0,3},{1,2},{2,1},{3,0},{4,7},{5,6},{6,5},{7,4},{8,11},{9,10},{10,... | collective-permute-start | bytes 98312 | tf_op jit(solution)/shard_map/ppermute | solution.py:593
  42.2 12.8 %all-to-all-start.1 = ((f32[32,1,128]{2,1,0:T(1,128)}), f32[32,1,128]{2,1,0:T(1,128)S(1)}, u32[]{:S(2)}, u32[]{:S(2)}) async-start(f32[32,1,128]{2,1,0:T(1,128)} %bitcast.6), calls=%async_computation.1 | async-start | bytes 32768 | tf_op jit(solution)/shard_map/all_to_all | solution.py:646
  47.9 7.0 %copy-start.1 = (f32[64,1024]{1,0:T(8,128)S(1)}, f32[64,1024]{1,0:T(8,128)}, u32[]{:S(2)}) copy-start(f32[64,1024]{1,0:T(8,128)} %temps.1) | copy-start | bytes 786436
  47.9 7.0 %copy-start.4 = (s32[1024]{0:T(1024)S(1)}, s32[1024]{0:T(1024)}, u32[]{:S(2)}) copy-start(s32[1024]{0:T(1024)} %param.12) | copy-start | bytes 12292
  48.0 7.0 %copy-start.5 = (s32[1024]{0:T(1024)S(1)}, s32[1024]{0:T(1024)}, u32[]{:S(2)}) copy-start(s32[1024]{0:T(1024)} %param.13) | copy-start | bytes 12292
  48.0 7.0 %copy-start.6 = (s32[1,1024]{1,0:T(1,128)S(1)}, s32[1,1024]{1,0:T(1,128)}, u32[]{:S(2)}) copy-start(s32[1,1024]{1,0:T(1,128)} %get-tuple-element.20.token.rank) | copy-start | bytes 12292
  48.0 7.0 %copy-start.10 = (f32[8]{0:T(128)S(1)}, f32[8]{0:T(128)}, u32[]{:S(2)}) copy-start(f32[8]{0:T(128)} %diffuse.1) | copy-start | bytes 100

commit v5 on v4

--- a/solution.py
+++ b/solution.py
@@ -117,6 +117,31 @@
     ]
     start_all(small)
     start_all(loads)
+    row = iota((8, 512), 0) // 2
+    stores = []
+    for c in range(4):
+        loads[c].wait()
+
+        def field(m, carry, c=c):
+            for block in (2 * c, 2 * c + 1):
+                high = jnp.zeros((8, 512), F32)
+                low = jnp.zeros((8, 512), F32)
+                for b in range(4):
+                    plane = flow[m, block * 4 + b]
+                    rolled_high = pltpu.roll(plane, (2 * b + 2) % 8, 0) if b != 3 else plane
+                    rolled_low = pltpu.roll(plane, 2 * b, 0) if b else plane
+                    high = jnp.where(row == b, rolled_high, high)
+                    low = jnp.where(row == b, rolled_low, low)
+                sides[0, m, block] = high
+                sides[1, m, block] = low
+            return carry
+
+        lax.fori_loop(0, 5, field, 0)
+        part = pl.ds(2 * c, 2)
+        for index, (side, there) in enumerate(((parity, pair_hbm), (1 - parity, cross_hbm))):
+            copy = pltpu.make_async_copy(sides.at[side, :, part], there.at[:, part], out_sem.at[index, c])
+            copy.start()
+            stores.append(copy)
     wait_all(small)
     cells = cell[...]
     tile = cells // 4096
@@ -147,31 +172,6 @@
             rows.append(jnp.where(slot, piece[level].astype(F32), 0.0).astype(BF16))
     sent = dot_nt(ones.astype(BF16), jnp.concatenate(rows, axis=0))
     outgoing[...] = sent[:, :128] + sent[:, 128:256] + sent[:, 256:]
-    row = iota((8, 512), 0) // 2
-    stores = []
-    for c in range(4):
-        loads[c].wait()
-
-        def field(m, carry, c=c):
-            for block in (2 * c, 2 * c + 1):
-                high = jnp.zeros((8, 512), F32)
-                low = jnp.zeros((8, 512), F32)
-                for b in range(4):
-                    plane = flow[m, block * 4 + b]
-                    rolled_high = pltpu.roll(plane, (2 * b + 2) % 8, 0) if b != 3 else plane
-                    rolled_low = pltpu.roll(plane, 2 * b, 0) if b else plane
-                    high = jnp.where(row == b, rolled_high, high)
-                    low = jnp.where(row == b, rolled_low, low)
-                sides[0, m, block] = high
-                sides[1, m, block] = low
-            return carry
-
-        lax.fori_loop(0, 5, field, 0)
-        part = pl.ds(2 * c, 2)
-        for index, (side, there) in enumerate(((parity, pair_hbm), (1 - parity, cross_hbm))):
-            copy = pltpu.make_async_copy(sides.at[side, :, part], there.at[:, part], out_sem.at[index, c])
-            copy.start()
-            stores.append(copy)
     layers = [(flow[m, 30 + n], flow[m, n]) for m in range(5) for n in range(2)]
     layers += [(spacing[30 + n], spacing[n]) for n in range(2)]
     for index, (top, bottom) in enumerate(layers):

time: 56.8 us -> 56.1 us (0.988)
  Pallas kernels: 22.6 us -> 21.9 us
    pallas_call x1, Pallas kernels: 4.31 us -> 3.68 us  [shards(): call(begin_kernel, 'begin', (struct(32, 128), struct(1, 1024, dtype=jnp.i...]
where the time goes in v5:
time: 56.1 us; the launch traced here: 55.9 us
  starting transfers between devices  27.4 us (49%)
  Pallas kernels  21.9 us (39%)
  waiting for transfers between devices  4.92 us (9%)
  between operations  0.89 us (2%)
  local copies, waits for them, and re-layouts  0.73 us (1%)
    ppermute x8, starting transfers between devices, swap(): lax.ppermute(value, axis, [(i, partner(i)) for i in range(lax.axis_size(a...  15.3 us
    pallas_call x1, Pallas kernels, shards(): call(side_kernel, 'side', (struct(5, 32, 8, 512), struct(8, 128)), in_spe...  7.87 us
    pallas_call x1, Pallas kernels, shards(): call(final_kernel, 'final', (struct(5, 32, 8, 512), struct(32, 8, 512), s...  6.7 us
    all_to_all x1, starting transfers between devices, shards(): lax.all_to_all(returned, 'surf', split_axis=0, concat_axis=0, tiled=True)  5.69 us
    all_to_all x1, starting transfers between devices, shards(): lax.all_to_all(outgoing, 'surf', split_axis=0, concat_axis=0, tiled=True)  3.79 us
    pallas_call x1, Pallas kernels, shards(): call(begin_kernel, 'begin', (struct(32, 128), struct(1, 1024, dtype=jnp.i...  3.68 us
    ppermute x8, waiting for transfers between devices, swap(): lax.ppermute(value, axis, [(i, partner(i)) for i in range(lax.axis_size(a...  2.93 us
    ppermute x1, starting transfers between devices, shards(): layers = lax.ppermute(cross_layers, 'wall', [(1, 2), (2, 1)])  2.64 us
  transfers between devices with their start and end apart: 11, of which 4 were waited for; matrix products, arithmetic and copies ran while one was open for 0% of the time, Pallas kernels for 30%

profile of v5, /device:TPU:1, one launch (start us, length us, event | category | flops | bytes accessed | tf_op | source)
XLA Modules:
  0.0 55.9 jit_solution(14105410161931109949)
XLA Ops:
  0.7 3.7 %begin.1 = (f32[32,128]{1,0:T(8,128)}, s32[1,1024]{1,0:T(1,128)}, f32[15,8,512]{2,1,0:T(8,128)}, f32[12,8,512]{2,1,0:T(8,128)}, f32[3,8,512]{2,1,0:T(8,128)}, /*...) custom-call(s32[1,1024]{1,0:T(1,128)} %bitcast.12, s32[1,1024]{1,0:T(1,128)} %bitcast.14, f32[64,1024]{1,0:T(8,128)} %temps.1, ...), custom_call_target="tpu_custom_call" | custom-call | flops 1000 | bytes 1000 | tf_op jit(solution)/shard_map/begin/pallas_call | solution.py:595
  4.4 0.0 copy-start.11
  4.4 7.2 %collective-permute-start.7 = (f32[5,8,8,512]{3,2,1,0:T(8,128)}, f32[5,8,8,512]{3,2,1,0:T(8,128)S(1)}, u32[]{:S(2)}, u32[]{:S(2)}) collective-permute-start(f32[5,8,8,512]{3,2,1,0:T(8,128)} %get-tuple-element.31), channel_id=1, source_target_pairs={{0,124},{4,8},{8,4},{12,16},{16,12},{20,24},{24,20},{28,32},{32,28... | collective-permute-start | bytes 1966088 | tf_op jit(solution)/shard_map/ppermute | solution.py:593
  11.6 1.0 %collective-permute-start = (f32[15,8,512]{2,1,0:T(8,128)}, f32[15,8,512]{2,1,0:T(8,128)S(1)}, u32[]{:S(2)}, u32[]{:S(2)}) collective-permute-start(f32[15,8,512]{2,1,0:T(8,128)} %get-tuple-element.24), channel_id=1, source_target_pairs={{0,1},{1,0},{2,3},{3,2},{4,5},{5,4},{6,7},{7,6},{8,9},{9,8},{10,11... | collective-permute-start | bytes 737288 | tf_op jit(solution)/shard_map/ppermute | solution.py:593
  12.5 3.3 %collective-permute-start.1 = (f32[3,8,512]{2,1,0:T(8,128)}, f32[3,8,512]{2,1,0:T(8,128)S(1)}, u32[]{:S(2)}, u32[]{:S(2)}) collective-permute-start(f32[3,8,512]{2,1,0:T(8,128)} %get-tuple-element.23.own), channel_id=1, source_target_pairs={{0,2},{1,3},{2,0},{3,1},{4,6},{5,7},{6,4},{7,5},{8,10},{9,11},{10,... | collective-permute-start | bytes 147464 | tf_op jit(solution)/shard_map/ppermute | solution.py:593
  15.9 3.8 %all-to-all-start = ((f32[32,1,128]{2,1,0:T(1,128)}), f32[32,1,128]{2,1,0:T(1,128)S(1)}, u32[]{:S(2)}, u32[]{:S(2)}) async-start(f32[32,1,128]{2,1,0:T(1,128)} %bitcast.16), calls=%async_computation | async-start | bytes 32768 | tf_op jit(solution)/shard_map/all_to_all | solution.py:621
  19.6 7.9 %side.1 = (f32[5,32,8,512]{3,2,1,0:T(8,128)}, f32[8,128]{1,0:T(8,128)}) custom-call(s32[1,1024]{1,0:T(1,128)} %get-tuple-element.20.token.rank, f32[5,32,8,512]{3,2,1,0:T(8,128)} %flow_hbm.5), custom_call_target="tpu_custom_call" | custom-call | flops 1000 | bytes 1000 | tf_op jit(solution)/shard_map/side/pallas_call | solution.py:627
  27.5 1.8 %all-to-all-done = f32[32,1,128]{2,1,0:T(1,128)S(1)} async-done(((f32[32,1,128]{2,1,0:T(1,128)}), f32[32,1,128]{2,1,0:T(1,128)S(1)}, u32[]{:S(2)}, u32[]{:S(2)}) %all-to-all-start) | async-done | bytes 16416 | tf_op jit(solution)/shard_map/all_to_all | solution.py:621
  29.3 1.9 %collective-permute-done.1.twin = f32[3,8,512]{2,1,0:T(8,128)S(1)} collective-permute-done((f32[3,8,512]{2,1,0:T(8,128)}, f32[3,8,512]{2,1,0:T(8,128)S(1)}, u32[]{:S(2)}, u32[]{:S(2)}) %collective-permute-start.1) | collective-permute-done | bytes 49184 | tf_op jit(solution)/shard_map/ppermute | solution.py:593
  31.1 1.1 %collective-permute-done.2.cross = f32[3,8,512]{2,1,0:T(8,128)S(1)} collective-permute-done((f32[3,8,512]{2,1,0:T(8,128)}, f32[3,8,512]{2,1,0:T(8,128)S(1)}, u32[]{:S(2)}, u32[]{:S(2)}) %collective-permute-start.2) | collective-permute-done | bytes 49184 | tf_op jit(solution)/shard_map/ppermute | solution.py:593
  32.2 0.7 %copy-done.7 = f32[8,128]{1,0:T(8,128)S(1)} copy-done((f32[8,128]{1,0:T(8,128)S(1)}, f32[8,128]{1,0:T(8,128)}, u32[]{:S(2)}) %copy-start.7) | copy-done | bytes 4120
  32.9 1.1 %surface.1 = (f32[2,8,512]{2,1,0:T(8,128)S(1)}, f32[2,8,512]{2,1,0:T(8,128)S(1)}, f32[1,1024]{1,0:T(1,128)S(1)}) custom-call(f32[8]{0:T(128)S(1)} %copy-done.8, f32[8]{0:T(128)S(1)} %copy-done.9, f32[8,128]{1,0:T(8,128)S(1)} %copy-done.7, f32[32,128]{1,0:T(8,128)S(1)} %bitcast.11, f32[3,8,512]{2,1,0:T(8,128)S(1)} %copy-done.2, ...), custom_call_target="tpu_custom_call" | custom-call | flops 1000 | bytes 1000 | tf_op jit(solution)/shard_map/surface/pallas_call | solution.py:635
  34.1 2.6 %collective-permute-start.6 = (f32[12,8,512]{2,1,0:T(8,128)S(1)}, f32[12,8,512]{2,1,0:T(8,128)S(1)}, u32[]{:S(2)}, u32[]{:S(2)}) collective-permute-start(f32[12,8,512]{2,1,0:T(8,128)S(1)} %copy-done.11), channel_id=1, source_target_pairs={{1,2},{2,1},{5,6},{6,5},{9,10},{10,9},{13,14},{14,13},{17,18},{18,... | collective-permute-start | bytes 589832 | tf_op jit(solution)/shard_map/ppermute | solution.py:643
  36.7 0.1 collective-permute-start.3
  36.8 2.6 %collective-permute-start.4 = (f32[2,8,512]{2,1,0:T(8,128)S(1)}, f32[2,8,512]{2,1,0:T(8,128)S(1)}, u32[]{:S(2)}, u32[]{:S(2)}) collective-permute-start(f32[2,8,512]{2,1,0:T(8,128)S(1)} %get-tuple-element.25.dense_hbm.dense), channel_id=1, source_target_pairs={{0,2},{1,3},{2,0},{3,1},{4,6},{5,7},{6,4},{7,5},{8,10},{9,11},{10,... | collective-permute-start | bytes 98312 | tf_op jit(solution)/shard_map/ppermute | solution.py:593
  39.4 1.1 %collective-permute-start.5 = (f32[2,8,512]{2,1,0:T(8,128)S(1)}, f32[2,8,512]{2,1,0:T(8,128)S(1)}, u32[]{:S(2)}, u32[]{:S(2)}) collective-permute-start(f32[2,8,512]{2,1,0:T(8,128)S(1)} %get-tuple-element.25.dense_hbm.dense), channel_id=1, source_target_pairs={{0,3},{1,2},{2,1},{3,0},{4,7},{5,6},{6,5},{7,4},{8,11},{9,10},{10,... | collective-permute-start | bytes 98312 | tf_op jit(solution)/shard_map/ppermute | solution.py:593
  40.5 1.0 %answer.1 = f32[32,128]{1,0:T(8,128)} custom-call(f32[1,1024]{1,0:T(1,128)S(1)} %get-tuple-element.36.where_in, f32[2,8,512]{2,1,0:T(8,128)S(1)} %get-tuple-element.25.dense_hbm.dense), custom_call_target="tpu_custom_call" | custom-call | flops 1000 | bytes 1000 | tf_op jit(solution)/shard_map/answer/pallas_call | solution.py:645
  41.5 5.7 %all-to-all-start.1 = ((f32[32,1,128]{2,1,0:T(1,128)}), f32[32,1,128]{2,1,0:T(1,128)S(1)}, u32[]{:S(2)}, u32[]{:S(2)}) async-start(f32[32,1,128]{2,1,0:T(1,128)} %bitcast.6), calls=%async_computation.1 | async-start | bytes 32768 | tf_op jit(solution)/shard_map/all_to_all | solution.py:646
  47.3 0.0 copy-start.1
  47.3 0.0 copy-start.4
  47.3 0.0 copy-start.5
  47.4 6.7 %final.1 = (f32[5,32,8,512]{3,2,1,0:T(8,128)}, f32[32,8,512]{2,1,0:T(8,128)}, f32[8,128]{1,0:T(8,128)S(1)}) custom-call(f32[2,8,512]{2,1,0:T(8,128)S(1)} %get-tuple-element.25.dense_hbm.dense, f32[2,8,512]{2,1,0:T(8,128)S(1)} %collective-permute-done.3.dense_1_hbm, f32[2,8,512]{2,1,0:T(8,128)S(1)} %collective-permute-done.4.dense_2_hbm, ...), custom_call_target="tpu_custom_call" | custom-call | flops 1000 | bytes 1000 | tf_op jit(solution)/shard_map/final/pallas_call | solution.py:647
  54.1 0.2 all-to-all-done.1
  54.3 1.5 %ablate.1 = f32[64,1024]{1,0:T(8,128)} custom-call(f32[8]{0:T(128)S(1)} %copy-done.10, f32[8,128]{1,0:T(8,128)S(1)} %get-tuple-element.35.token, s32[1,1024]{1,0:T(1,128)S(1)} %bitcast.13, s32[1,1024]{1,0:T(1,128)S(1)} %copy-done.6, s32[1,1024]{1,0:T(1,128)S(1)} %bitcast.15, f32[32,128]{1,0:T(8,128)S(1)} %bitcast.10, f32[64,1024]{1,0:T(8,128)S(1)} %copy-done.1), custom_call_target="tpu_custom_call" | custom-call | flops 1000 | bytes 1000 | tf_op jit(solution)/shard_map/ablate/pallas_call | solution.py:689
  (28 shorter events, 0.1 us)
Async XLA Ops:
  0.6 31.6 %copy-start.8 = (f32[8]{0:T(128)S(1)}, f32[8]{0:T(128)}, u32[]{:S(2)}) copy-start(f32[8]{0:T(128)} %conduct.1) | copy-start | bytes 100
  0.6 31.6 %copy-start.9 = (f32[8]{0:T(128)S(1)}, f32[8]{0:T(128)}, u32[]{:S(2)}) copy-start(f32[8]{0:T(128)} %rate.1) | copy-start | bytes 100
  0.7 46.6 %copy-start = (f32[32,8,512]{2,1,0:T(8,128)S(1)}, f32[32,8,512]{2,1,0:T(8,128)}, u32[]{:S(2)}) copy-start(f32[32,8,512]{2,1,0:T(8,128)} %spacing_hbm.3) | copy-start | bytes 1572868
  0.7 46.6 %copy-start.3 = (s32[8,512]{1,0:T(8,128)S(1)}, s32[8,512]{1,0:T(8,128)}, u32[]{:S(2)}) copy-start(s32[8,512]{1,0:T(8,128)} %kinds_hbm.1) | copy-start | bytes 49156
  4.4 27.9 %copy-start.2 = (f32[3,8,512]{2,1,0:T(8,128)S(1)}, f32[3,8,512]{2,1,0:T(8,128)}, u32[]{:S(2)}) copy-start(f32[3,8,512]{2,1,0:T(8,128)} %get-tuple-element.23.own) | copy-start | bytes 147460
  4.4 29.7 %copy-start.11 = (f32[12,8,512]{2,1,0:T(8,128)S(1)}, f32[12,8,512]{2,1,0:T(8,128)}, u32[]{:S(2)}) copy-start(f32[12,8,512]{2,1,0:T(8,128)} %get-tuple-element.29) | copy-start | bytes 589828
  4.4 42.9 %collective-permute-start.7 = (f32[5,8,8,512]{3,2,1,0:T(8,128)}, f32[5,8,8,512]{3,2,1,0:T(8,128)S(1)}, u32[]{:S(2)}, u32[]{:S(2)}) collective-permute-start(f32[5,8,8,512]{3,2,1,0:T(8,128)} %get-tuple-element.31), channel_id=1, source_target_pairs={{0,124},{4,8},{8,4},{12,16},{16,12},{20,24},{24,20},{28,32},{32,28... | collective-permute-start | bytes 1966088 | tf_op jit(solution)/shard_map/ppermute | solution.py:593
  11.6 35.7 %collective-permute-start.8 = (f32[5,8,8,512]{3,2,1,0:T(8,128)}, f32[5,8,8,512]{3,2,1,0:T(8,128)}, u32[]{:S(2)}, u32[]{:S(2)}) collective-permute-start(f32[5,8,8,512]{3,2,1,0:T(8,128)} %get-tuple-element.32), channel_id=1, source_target_pairs={{0,4},{4,0},{8,12},{12,8},{16,20},{20,16},{24,28},{28,24},{32,36},... | collective-permute-start | bytes 1966088 | tf_op jit(solution)/shard_map/ppermute | solution.py:593
  11.6 20.6 %collective-permute-start = (f32[15,8,512]{2,1,0:T(8,128)}, f32[15,8,512]{2,1,0:T(8,128)S(1)}, u32[]{:S(2)}, u32[]{:S(2)}) collective-permute-start(f32[15,8,512]{2,1,0:T(8,128)} %get-tuple-element.24), channel_id=1, source_target_pairs={{0,1},{1,0},{2,3},{3,2},{4,5},{5,4},{6,7},{7,6},{8,9},{9,8},{10,11... | collective-permute-start | bytes 737288 | tf_op jit(solution)/shard_map/ppermute | solution.py:593
  12.5 18.6 %collective-permute-start.1 = (f32[3,8,512]{2,1,0:T(8,128)}, f32[3,8,512]{2,1,0:T(8,128)S(1)}, u32[]{:S(2)}, u32[]{:S(2)}) collective-permute-start(f32[3,8,512]{2,1,0:T(8,128)} %get-tuple-element.23.own), channel_id=1, source_target_pairs={{0,2},{1,3},{2,0},{3,1},{4,6},{5,7},{6,4},{7,5},{8,10},{9,11},{10,... | collective-permute-start | bytes 147464 | tf_op jit(solution)/shard_map/ppermute | solution.py:593
  15.9 16.4 %collective-permute-start.2 = (f32[3,8,512]{2,1,0:T(8,128)}, f32[3,8,512]{2,1,0:T(8,128)S(1)}, u32[]{:S(2)}, u32[]{:S(2)}) collective-permute-start(f32[3,8,512]{2,1,0:T(8,128)} %get-tuple-element.23.own), channel_id=1, source_target_pairs={{0,3},{1,2},{2,1},{3,0},{4,7},{5,6},{6,5},{7,4},{8,11},{9,10},{10,... | collective-permute-start | bytes 147464 | tf_op jit(solution)/shard_map/ppermute | solution.py:593
  15.9 13.4 %all-to-all-start = ((f32[32,1,128]{2,1,0:T(1,128)}), f32[32,1,128]{2,1,0:T(1,128)S(1)}, u32[]{:S(2)}, u32[]{:S(2)}) async-start(f32[32,1,128]{2,1,0:T(1,128)} %bitcast.16), calls=%async_computation | async-start | bytes 32768 | tf_op jit(solution)/shard_map/all_to_all | solution.py:621
  32.2 0.7 %copy-start.7 = (f32[8,128]{1,0:T(8,128)S(1)}, f32[8,128]{1,0:T(8,128)}, u32[]{:S(2)}) copy-start(f32[8,128]{1,0:T(8,128)} %get-tuple-element.21.token) | copy-start | bytes 12292
  34.1 13.2 %collective-permute-start.6 = (f32[12,8,512]{2,1,0:T(8,128)S(1)}, f32[12,8,512]{2,1,0:T(8,128)S(1)}, u32[]{:S(2)}, u32[]{:S(2)}) collective-permute-start(f32[12,8,512]{2,1,0:T(8,128)S(1)} %copy-done.11), channel_id=1, source_target_pairs={{1,2},{2,1},{5,6},{6,5},{9,10},{10,9},{13,14},{14,13},{17,18},{18,... | collective-permute-start | bytes 589832 | tf_op jit(solution)/shard_map/ppermute | solution.py:643
  36.7 2.7 %collective-permute-start.3 = (f32[2,8,512]{2,1,0:T(8,128)S(1)}, f32[2,8,512]{2,1,0:T(8,128)S(1)}, u32[]{:S(2)}, u32[]{:S(2)}) collective-permute-start(f32[2,8,512]{2,1,0:T(8,128)S(1)} %get-tuple-element.25.dense_hbm.dense), channel_id=1, source_target_pairs={{0,1},{1,0},{2,3},{3,2},{4,5},{5,4},{6,7},{7,6},{8,9},{9,8},{10,11... | collective-permute-start | bytes 98312 | tf_op jit(solution)/shard_map/ppermute | solution.py:593
  36.8 10.4 %collective-permute-start.4 = (f32[2,8,512]{2,1,0:T(8,128)S(1)}, f32[2,8,512]{2,1,0:T(8,128)S(1)}, u32[]{:S(2)}, u32[]{:S(2)}) collective-permute-start(f32[2,8,512]{2,1,0:T(8,128)S(1)} %get-tuple-element.25.dense_hbm.dense), channel_id=1, source_target_pairs={{0,2},{1,3},{2,0},{3,1},{4,6},{5,7},{6,4},{7,5},{8,10},{9,11},{10,... | collective-permute-start | bytes 98312 | tf_op jit(solution)/shard_map/ppermute | solution.py:593
  39.4 7.8 %collective-permute-start.5 = (f32[2,8,512]{2,1,0:T(8,128)S(1)}, f32[2,8,512]{2,1,0:T(8,128)S(1)}, u32[]{:S(2)}, u32[]{:S(2)}) collective-permute-start(f32[2,8,512]{2,1,0:T(8,128)S(1)} %get-tuple-element.25.dense_hbm.dense), channel_id=1, source_target_pairs={{0,3},{1,2},{2,1},{3,0},{4,7},{5,6},{6,5},{7,4},{8,11},{9,10},{10,... | collective-permute-start | bytes 98312 | tf_op jit(solution)/shard_map/ppermute | solution.py:593
  41.5 12.8 %all-to-all-start.1 = ((f32[32,1,128]{2,1,0:T(1,128)}), f32[32,1,128]{2,1,0:T(1,128)S(1)}, u32[]{:S(2)}, u32[]{:S(2)}) async-start(f32[32,1,128]{2,1,0:T(1,128)} %bitcast.6), calls=%async_computation.1 | async-start | bytes 32768 | tf_op jit(solution)/shard_map/all_to_all | solution.py:646
  47.3 7.0 %copy-start.1 = (f32[64,1024]{1,0:T(8,128)S(1)}, f32[64,1024]{1,0:T(8,128)}, u32[]{:S(2)}) copy-start(f32[64,1024]{1,0:T(8,128)} %temps.1) | copy-start | bytes 786436
  47.3 7.0 %copy-start.4 = (s32[1024]{0:T(1024)S(1)}, s32[1024]{0:T(1024)}, u32[]{:S(2)}) copy-start(s32[1024]{0:T(1024)} %param.12) | copy-start | bytes 12292
  47.3 7.0 %copy-start.5 = (s32[1024]{0:T(1024)S(1)}, s32[1024]{0:T(1024)}, u32[]{:S(2)}) copy-start(s32[1024]{0:T(1024)} %param.13) | copy-start | bytes 12292
  47.3 7.0 %copy-start.6 = (s32[1,1024]{1,0:T(1,128)S(1)}, s32[1,1024]{1,0:T(1,128)}, u32[]{:S(2)}) copy-start(s32[1,1024]{1,0:T(1,128)} %get-tuple-element.20.token.rank) | copy-start | bytes 12292
  47.3 7.0 %copy-start.10 = (f32[8]{0:T(128)S(1)}, f32[8]{0:T(128)}, u32[]{:S(2)}) copy-start(f32[8]{0:T(128)} %diffuse.1) | copy-start | bytes 100

commit v6 on v5

--- a/solution.py
+++ b/solution.py
@@ -195,12 +195,12 @@
     wall = lax.axis_index("wall")
     received = arrived[...]
     pieces = jnp.concatenate(split3(received), axis=0)
-    lane = iota((128, 1024), 1) % 32
     line = iota((128, 1024), 0)
     source = iota((32, 1024), 0) == iota((32, 1024), 1) // 32
+    slots = onehot(iota((32, 1024), 0) == iota((32, 1024), 1) % 32)
     flat = []
     for f in range(4):
-        spread = join3(dot_nn(pieces, onehot(line == lane + 32 * f)), 32)
+        spread = join3(dot_nn(pieces[:, 32 * f : 32 * f + 32], slots), 32)
         flat.append(jnp.sum(jnp.where(source, spread, 0.0), axis=0, keepdims=True))
     where_out[...] = flat[0]
     cells = flat[0].astype(jnp.int32)
@@ -259,8 +259,8 @@
 
 
 def ablate_kernel(diffuse, token, cell, rank, zone, back, temps, out):
-    pieces = jnp.concatenate(split3(back[...]), axis=0)
-    slot = onehot(iota((128, 1024), 0) == rank[...])
+    pieces = jnp.concatenate(split3(back[...]), axis=0)[:, :32]
+    slot = onehot(iota((32, 1024), 0) == rank[...])
     spread = join3(dot_nn(pieces, slot), 32)
     tile_hit = iota((32, 1024), 0) == cell[...] // 4096
     surface = jnp.sum(jnp.where(tile_hit, spread, 0.0), axis=0, keepdims=True)

time: 56.1 us -> 56.1 us (level)
  no operation moved by 1% of the time
where the time goes in v6:
time: 56.1 us; the launch traced here: 55.9 us
  starting transfers between devices  27.4 us (49%)
  Pallas kernels  21.9 us (39%)
  waiting for transfers between devices  4.92 us (9%)
  between operations  0.89 us (2%)
  local copies, waits for them, and re-layouts  0.73 us (1%)
    ppermute x8, starting transfers between devices, swap(): lax.ppermute(value, axis, [(i, partner(i)) for i in range(lax.axis_size(a...  15.3 us
    pallas_call x1, Pallas kernels, shards(): call(side_kernel, 'side', (struct(5, 32, 8, 512), struct(8, 128)), in_spe...  7.87 us
    pallas_call x1, Pallas kernels, shards(): call(final_kernel, 'final', (struct(5, 32, 8, 512), struct(32, 8, 512), s...  6.7 us
    all_to_all x1, starting transfers between devices, shards(): lax.all_to_all(returned, 'surf', split_axis=0, concat_axis=0, tiled=True)  5.69 us
    all_to_all x1, starting transfers between devices, shards(): lax.all_to_all(outgoing, 'surf', split_axis=0, concat_axis=0, tiled=True)  3.79 us
    pallas_call x1, Pallas kernels, shards(): call(begin_kernel, 'begin', (struct(32, 128), struct(1, 1024, dtype=jnp.i...  3.68 us
    ppermute x8, waiting for transfers between devices, swap(): lax.ppermute(value, axis, [(i, partner(i)) for i in range(lax.axis_size(a...  2.93 us
    ppermute x1, starting transfers between devices, shards(): layers = lax.ppermute(cross_layers, 'wall', [(1, 2), (2, 1)])  2.64 us
  transfers between devices with their start and end apart: 11, of which 4 were waited for; matrix products, arithmetic and copies ran while one was open for 0% of the time, Pallas kernels for 30%

profile of v6, /device:TPU:1, one launch (start us, length us, event | category | flops | bytes accessed | tf_op | source)
XLA Modules:
  0.0 55.9 jit_solution(11763046276419210368)
XLA Ops:
  0.7 3.7 %begin.1 = (f32[32,128]{1,0:T(8,128)}, s32[1,1024]{1,0:T(1,128)}, f32[15,8,512]{2,1,0:T(8,128)}, f32[12,8,512]{2,1,0:T(8,128)}, f32[3,8,512]{2,1,0:T(8,128)}, /*...) custom-call(s32[1,1024]{1,0:T(1,128)} %bitcast.12, s32[1,1024]{1,0:T(1,128)} %bitcast.14, f32[64,1024]{1,0:T(8,128)} %temps.1, ...), custom_call_target="tpu_custom_call" | custom-call | flops 1000 | bytes 1000 | tf_op jit(solution)/shard_map/begin/pallas_call | solution.py:595
  4.4 0.0 copy-start.11
  4.4 7.2 %collective-permute-start.7 = (f32[5,8,8,512]{3,2,1,0:T(8,128)}, f32[5,8,8,512]{3,2,1,0:T(8,128)S(1)}, u32[]{:S(2)}, u32[]{:S(2)}) collective-permute-start(f32[5,8,8,512]{3,2,1,0:T(8,128)} %get-tuple-element.31), channel_id=1, source_target_pairs={{0,124},{4,8},{8,4},{12,16},{16,12},{20,24},{24,20},{28,32},{32,28... | collective-permute-start | bytes 1966088 | tf_op jit(solution)/shard_map/ppermute | solution.py:593
  11.6 1.0 %collective-permute-start = (f32[15,8,512]{2,1,0:T(8,128)}, f32[15,8,512]{2,1,0:T(8,128)S(1)}, u32[]{:S(2)}, u32[]{:S(2)}) collective-permute-start(f32[15,8,512]{2,1,0:T(8,128)} %get-tuple-element.24), channel_id=1, source_target_pairs={{0,1},{1,0},{2,3},{3,2},{4,5},{5,4},{6,7},{7,6},{8,9},{9,8},{10,11... | collective-permute-start | bytes 737288 | tf_op jit(solution)/shard_map/ppermute | solution.py:593
  12.5 3.3 %collective-permute-start.1 = (f32[3,8,512]{2,1,0:T(8,128)}, f32[3,8,512]{2,1,0:T(8,128)S(1)}, u32[]{:S(2)}, u32[]{:S(2)}) collective-permute-start(f32[3,8,512]{2,1,0:T(8,128)} %get-tuple-element.23.own), channel_id=1, source_target_pairs={{0,2},{1,3},{2,0},{3,1},{4,6},{5,7},{6,4},{7,5},{8,10},{9,11},{10,... | collective-permute-start | bytes 147464 | tf_op jit(solution)/shard_map/ppermute | solution.py:593
  15.9 3.8 %all-to-all-start = ((f32[32,1,128]{2,1,0:T(1,128)}), f32[32,1,128]{2,1,0:T(1,128)S(1)}, u32[]{:S(2)}, u32[]{:S(2)}) async-start(f32[32,1,128]{2,1,0:T(1,128)} %bitcast.16), calls=%async_computation | async-start | bytes 32768 | tf_op jit(solution)/shard_map/all_to_all | solution.py:621
  19.6 7.9 %side.1 = (f32[5,32,8,512]{3,2,1,0:T(8,128)}, f32[8,128]{1,0:T(8,128)}) custom-call(s32[1,1024]{1,0:T(1,128)} %get-tuple-element.20.token.rank, f32[5,32,8,512]{3,2,1,0:T(8,128)} %flow_hbm.5), custom_call_target="tpu_custom_call" | custom-call | flops 1000 | bytes 1000 | tf_op jit(solution)/shard_map/side/pallas_call | solution.py:627
  27.5 1.8 %all-to-all-done = f32[32,1,128]{2,1,0:T(1,128)S(1)} async-done(((f32[32,1,128]{2,1,0:T(1,128)}), f32[32,1,128]{2,1,0:T(1,128)S(1)}, u32[]{:S(2)}, u32[]{:S(2)}) %all-to-all-start) | async-done | bytes 16416 | tf_op jit(solution)/shard_map/all_to_all | solution.py:621
  29.3 1.9 %collective-permute-done.1.twin = f32[3,8,512]{2,1,0:T(8,128)S(1)} collective-permute-done((f32[3,8,512]{2,1,0:T(8,128)}, f32[3,8,512]{2,1,0:T(8,128)S(1)}, u32[]{:S(2)}, u32[]{:S(2)}) %collective-permute-start.1) | collective-permute-done | bytes 49184 | tf_op jit(solution)/shard_map/ppermute | solution.py:593
  31.1 1.1 %collective-permute-done.2.cross = f32[3,8,512]{2,1,0:T(8,128)S(1)} collective-permute-done((f32[3,8,512]{2,1,0:T(8,128)}, f32[3,8,512]{2,1,0:T(8,128)S(1)}, u32[]{:S(2)}, u32[]{:S(2)}) %collective-permute-start.2) | collective-permute-done | bytes 49184 | tf_op jit(solution)/shard_map/ppermute | solution.py:593
  32.2 0.7 %copy-done.7 = f32[8,128]{1,0:T(8,128)S(1)} copy-done((f32[8,128]{1,0:T(8,128)S(1)}, f32[8,128]{1,0:T(8,128)}, u32[]{:S(2)}) %copy-start.7) | copy-done | bytes 4120
  32.9 1.2 %surface.1 = (f32[2,8,512]{2,1,0:T(8,128)S(1)}, f32[2,8,512]{2,1,0:T(8,128)S(1)}, f32[1,1024]{1,0:T(1,128)S(1)}) custom-call(f32[8]{0:T(128)S(1)} %copy-done.8, f32[8]{0:T(128)S(1)} %copy-done.9, f32[8,128]{1,0:T(8,128)S(1)} %copy-done.7, f32[32,128]{1,0:T(8,128)S(1)} %bitcast.11, f32[3,8,512]{2,1,0:T(8,128)S(1)} %copy-done.2, ...), custom_call_target="tpu_custom_call" | custom-call | flops 1000 | bytes 1000 | tf_op jit(solution)/shard_map/surface/pallas_call | solution.py:635
  34.1 2.6 %collective-permute-start.6 = (f32[12,8,512]{2,1,0:T(8,128)S(1)}, f32[12,8,512]{2,1,0:T(8,128)S(1)}, u32[]{:S(2)}, u32[]{:S(2)}) collective-permute-start(f32[12,8,512]{2,1,0:T(8,128)S(1)} %copy-done.11), channel_id=1, source_target_pairs={{1,2},{2,1},{5,6},{6,5},{9,10},{10,9},{13,14},{14,13},{17,18},{18,... | collective-permute-start | bytes 589832 | tf_op jit(solution)/shard_map/ppermute | solution.py:643
  36.7 0.1 collective-permute-start.3
  36.8 2.6 %collective-permute-start.4 = (f32[2,8,512]{2,1,0:T(8,128)S(1)}, f32[2,8,512]{2,1,0:T(8,128)S(1)}, u32[]{:S(2)}, u32[]{:S(2)}) collective-permute-start(f32[2,8,512]{2,1,0:T(8,128)S(1)} %get-tuple-element.25.dense_hbm.dense), channel_id=1, source_target_pairs={{0,2},{1,3},{2,0},{3,1},{4,6},{5,7},{6,4},{7,5},{8,10},{9,11},{10,... | collective-permute-start | bytes 98312 | tf_op jit(solution)/shard_map/ppermute | solution.py:593
  39.5 1.1 %collective-permute-start.5 = (f32[2,8,512]{2,1,0:T(8,128)S(1)}, f32[2,8,512]{2,1,0:T(8,128)S(1)}, u32[]{:S(2)}, u32[]{:S(2)}) collective-permute-start(f32[2,8,512]{2,1,0:T(8,128)S(1)} %get-tuple-element.25.dense_hbm.dense), channel_id=1, source_target_pairs={{0,3},{1,2},{2,1},{3,0},{4,7},{5,6},{6,5},{7,4},{8,11},{9,10},{10,... | collective-permute-start | bytes 98312 | tf_op jit(solution)/shard_map/ppermute | solution.py:593
  40.5 1.0 %answer.1 = f32[32,128]{1,0:T(8,128)} custom-call(f32[1,1024]{1,0:T(1,128)S(1)} %get-tuple-element.36.where_in, f32[2,8,512]{2,1,0:T(8,128)S(1)} %get-tuple-element.25.dense_hbm.dense), custom_call_target="tpu_custom_call" | custom-call | flops 1000 | bytes 1000 | tf_op jit(solution)/shard_map/answer/pallas_call | solution.py:645
  41.5 5.7 %all-to-all-start.1 = ((f32[32,1,128]{2,1,0:T(1,128)}), f32[32,1,128]{2,1,0:T(1,128)S(1)}, u32[]{:S(2)}, u32[]{:S(2)}) async-start(f32[32,1,128]{2,1,0:T(1,128)} %bitcast.6), calls=%async_computation.1 | async-start | bytes 32768 | tf_op jit(solution)/shard_map/all_to_all | solution.py:646
  47.3 0.0 copy-start.1
  47.3 0.0 copy-start.4
  47.3 0.0 copy-start.5
  47.4 6.7 %final.1 = (f32[5,32,8,512]{3,2,1,0:T(8,128)}, f32[32,8,512]{2,1,0:T(8,128)}, f32[8,128]{1,0:T(8,128)S(1)}) custom-call(f32[2,8,512]{2,1,0:T(8,128)S(1)} %get-tuple-element.25.dense_hbm.dense, f32[2,8,512]{2,1,0:T(8,128)S(1)} %collective-permute-done.3.dense_1_hbm, f32[2,8,512]{2,1,0:T(8,128)S(1)} %collective-permute-done.4.dense_2_hbm, ...), custom_call_target="tpu_custom_call" | custom-call | flops 1000 | bytes 1000 | tf_op jit(solution)/shard_map/final/pallas_call | solution.py:647
  54.1 0.2 all-to-all-done.1
  54.3 1.5 %ablate.1 = f32[64,1024]{1,0:T(8,128)} custom-call(f32[8]{0:T(128)S(1)} %copy-done.10, f32[8,128]{1,0:T(8,128)S(1)} %get-tuple-element.35.token, s32[1,1024]{1,0:T(1,128)S(1)} %bitcast.13, s32[1,1024]{1,0:T(1,128)S(1)} %copy-done.6, s32[1,1024]{1,0:T(1,128)S(1)} %bitcast.15, f32[32,128]{1,0:T(8,128)S(1)} %bitcast.10, f32[64,1024]{1,0:T(8,128)S(1)} %copy-done.1), custom_call_target="tpu_custom_call" | custom-call | flops 1000 | bytes 1000 | tf_op jit(solution)/shard_map/ablate/pallas_call | solution.py:689
  (28 shorter events, 0.1 us)
Async XLA Ops:
  0.6 31.6 %copy-start.8 = (f32[8]{0:T(128)S(1)}, f32[8]{0:T(128)}, u32[]{:S(2)}) copy-start(f32[8]{0:T(128)} %conduct.1) | copy-start | bytes 100
  0.6 31.6 %copy-start.9 = (f32[8]{0:T(128)S(1)}, f32[8]{0:T(128)}, u32[]{:S(2)}) copy-start(f32[8]{0:T(128)} %rate.1) | copy-start | bytes 100
  0.7 46.6 %copy-start = (f32[32,8,512]{2,1,0:T(8,128)S(1)}, f32[32,8,512]{2,1,0:T(8,128)}, u32[]{:S(2)}) copy-start(f32[32,8,512]{2,1,0:T(8,128)} %spacing_hbm.3) | copy-start | bytes 1572868
  0.7 46.6 %copy-start.3 = (s32[8,512]{1,0:T(8,128)S(1)}, s32[8,512]{1,0:T(8,128)}, u32[]{:S(2)}) copy-start(s32[8,512]{1,0:T(8,128)} %kinds_hbm.1) | copy-start | bytes 49156
  4.4 27.9 %copy-start.2 = (f32[3,8,512]{2,1,0:T(8,128)S(1)}, f32[3,8,512]{2,1,0:T(8,128)}, u32[]{:S(2)}) copy-start(f32[3,8,512]{2,1,0:T(8,128)} %get-tuple-element.23.own) | copy-start | bytes 147460
  4.4 29.7 %copy-start.11 = (f32[12,8,512]{2,1,0:T(8,128)S(1)}, f32[12,8,512]{2,1,0:T(8,128)}, u32[]{:S(2)}) copy-start(f32[12,8,512]{2,1,0:T(8,128)} %get-tuple-element.29) | copy-start | bytes 589828
  4.4 42.9 %collective-permute-start.7 = (f32[5,8,8,512]{3,2,1,0:T(8,128)}, f32[5,8,8,512]{3,2,1,0:T(8,128)S(1)}, u32[]{:S(2)}, u32[]{:S(2)}) collective-permute-start(f32[5,8,8,512]{3,2,1,0:T(8,128)} %get-tuple-element.31), channel_id=1, source_target_pairs={{0,124},{4,8},{8,4},{12,16},{16,12},{20,24},{24,20},{28,32},{32,28... | collective-permute-start | bytes 1966088 | tf_op jit(solution)/shard_map/ppermute | solution.py:593
  11.6 35.7 %collective-permute-start.8 = (f32[5,8,8,512]{3,2,1,0:T(8,128)}, f32[5,8,8,512]{3,2,1,0:T(8,128)}, u32[]{:S(2)}, u32[]{:S(2)}) collective-permute-start(f32[5,8,8,512]{3,2,1,0:T(8,128)} %get-tuple-element.32), channel_id=1, source_target_pairs={{0,4},{4,0},{8,12},{12,8},{16,20},{20,16},{24,28},{28,24},{32,36},... | collective-permute-start | bytes 1966088 | tf_op jit(solution)/shard_map/ppermute | solution.py:593
  11.6 20.6 %collective-permute-start = (f32[15,8,512]{2,1,0:T(8,128)}, f32[15,8,512]{2,1,0:T(8,128)S(1)}, u32[]{:S(2)}, u32[]{:S(2)}) collective-permute-start(f32[15,8,512]{2,1,0:T(8,128)} %get-tuple-element.24), channel_id=1, source_target_pairs={{0,1},{1,0},{2,3},{3,2},{4,5},{5,4},{6,7},{7,6},{8,9},{9,8},{10,11... | collective-permute-start | bytes 737288 | tf_op jit(solution)/shard_map/ppermute | solution.py:593
  12.5 18.6 %collective-permute-start.1 = (f32[3,8,512]{2,1,0:T(8,128)}, f32[3,8,512]{2,1,0:T(8,128)S(1)}, u32[]{:S(2)}, u32[]{:S(2)}) collective-permute-start(f32[3,8,512]{2,1,0:T(8,128)} %get-tuple-element.23.own), channel_id=1, source_target_pairs={{0,2},{1,3},{2,0},{3,1},{4,6},{5,7},{6,4},{7,5},{8,10},{9,11},{10,... | collective-permute-start | bytes 147464 | tf_op jit(solution)/shard_map/ppermute | solution.py:593
  15.9 16.4 %collective-permute-start.2 = (f32[3,8,512]{2,1,0:T(8,128)}, f32[3,8,512]{2,1,0:T(8,128)S(1)}, u32[]{:S(2)}, u32[]{:S(2)}) collective-permute-start(f32[3,8,512]{2,1,0:T(8,128)} %get-tuple-element.23.own), channel_id=1, source_target_pairs={{0,3},{1,2},{2,1},{3,0},{4,7},{5,6},{6,5},{7,4},{8,11},{9,10},{10,... | collective-permute-start | bytes 147464 | tf_op jit(solution)/shard_map/ppermute | solution.py:593
  15.9 13.4 %all-to-all-start = ((f32[32,1,128]{2,1,0:T(1,128)}), f32[32,1,128]{2,1,0:T(1,128)S(1)}, u32[]{:S(2)}, u32[]{:S(2)}) async-start(f32[32,1,128]{2,1,0:T(1,128)} %bitcast.16), calls=%async_computation | async-start | bytes 32768 | tf_op jit(solution)/shard_map/all_to_all | solution.py:621
  32.2 0.7 %copy-start.7 = (f32[8,128]{1,0:T(8,128)S(1)}, f32[8,128]{1,0:T(8,128)}, u32[]{:S(2)}) copy-start(f32[8,128]{1,0:T(8,128)} %get-tuple-element.21.token) | copy-start | bytes 12292
  34.1 13.2 %collective-permute-start.6 = (f32[12,8,512]{2,1,0:T(8,128)S(1)}, f32[12,8,512]{2,1,0:T(8,128)S(1)}, u32[]{:S(2)}, u32[]{:S(2)}) collective-permute-start(f32[12,8,512]{2,1,0:T(8,128)S(1)} %copy-done.11), channel_id=1, source_target_pairs={{1,2},{2,1},{5,6},{6,5},{9,10},{10,9},{13,14},{14,13},{17,18},{18,... | collective-permute-start | bytes 589832 | tf_op jit(solution)/shard_map/ppermute | solution.py:643
  36.7 2.7 %collective-permute-start.3 = (f32[2,8,512]{2,1,0:T(8,128)S(1)}, f32[2,8,512]{2,1,0:T(8,128)S(1)}, u32[]{:S(2)}, u32[]{:S(2)}) collective-permute-start(f32[2,8,512]{2,1,0:T(8,128)S(1)} %get-tuple-element.25.dense_hbm.dense), channel_id=1, source_target_pairs={{0,1},{1,0},{2,3},{3,2},{4,5},{5,4},{6,7},{7,6},{8,9},{9,8},{10,11... | collective-permute-start | bytes 98312 | tf_op jit(solution)/shard_map/ppermute | solution.py:593
  36.8 10.4 %collective-permute-start.4 = (f32[2,8,512]{2,1,0:T(8,128)S(1)}, f32[2,8,512]{2,1,0:T(8,128)S(1)}, u32[]{:S(2)}, u32[]{:S(2)}) collective-permute-start(f32[2,8,512]{2,1,0:T(8,128)S(1)} %get-tuple-element.25.dense_hbm.dense), channel_id=1, source_target_pairs={{0,2},{1,3},{2,0},{3,1},{4,6},{5,7},{6,4},{7,5},{8,10},{9,11},{10,... | collective-permute-start | bytes 98312 | tf_op jit(solution)/shard_map/ppermute | solution.py:593
  39.5 7.8 %collective-permute-start.5 = (f32[2,8,512]{2,1,0:T(8,128)S(1)}, f32[2,8,512]{2,1,0:T(8,128)S(1)}, u32[]{:S(2)}, u32[]{:S(2)}) collective-permute-start(f32[2,8,512]{2,1,0:T(8,128)S(1)} %get-tuple-element.25.dense_hbm.dense), channel_id=1, source_target_pairs={{0,3},{1,2},{2,1},{3,0},{4,7},{5,6},{6,5},{7,4},{8,11},{9,10},{10,... | collective-permute-start | bytes 98312 | tf_op jit(solution)/shard_map/ppermute | solution.py:593
  41.5 12.8 %all-to-all-start.1 = ((f32[32,1,128]{2,1,0:T(1,128)}), f32[32,1,128]{2,1,0:T(1,128)S(1)}, u32[]{:S(2)}, u32[]{:S(2)}) async-start(f32[32,1,128]{2,1,0:T(1,128)} %bitcast.6), calls=%async_computation.1 | async-start | bytes 32768 | tf_op jit(solution)/shard_map/all_to_all | solution.py:646
  47.3 7.0 %copy-start.1 = (f32[64,1024]{1,0:T(8,128)S(1)}, f32[64,1024]{1,0:T(8,128)}, u32[]{:S(2)}) copy-start(f32[64,1024]{1,0:T(8,128)} %temps.1) | copy-start | bytes 786436
  47.3 7.0 %copy-start.4 = (s32[1024]{0:T(1024)S(1)}, s32[1024]{0:T(1024)}, u32[]{:S(2)}) copy-start(s32[1024]{0:T(1024)} %param.12) | copy-start | bytes 12292
  47.3 7.0 %copy-start.5 = (s32[1024]{0:T(1024)S(1)}, s32[1024]{0:T(1024)}, u32[]{:S(2)}) copy-start(s32[1024]{0:T(1024)} %param.13) | copy-start | bytes 12292
  47.3 7.0 %copy-start.6 = (s32[1,1024]{1,0:T(1,128)S(1)}, s32[1,1024]{1,0:T(1,128)}, u32[]{:S(2)}) copy-start(s32[1,1024]{1,0:T(1,128)} %get-tuple-element.20.token.rank) | copy-start | bytes 12292
  47.4 7.0 %copy-start.10 = (f32[8]{0:T(128)S(1)}, f32[8]{0:T(128)}, u32[]{:S(2)}) copy-start(f32[8]{0:T(128)} %diffuse.1) | copy-start | bytes 100
